TPU v7x, 32 devices: a whole 2x2x4 slice. The times are simulated.
32 devices in a mesh: rows: 4 (over z), pos: 8 (over y, x, core).
Axes of the slice: x: 2, y: 2, z: 4, core: 2. Of those that a mesh axis runs over, the one named last changes fastest.
Arguments:
- tokens: bfloat16 [16, 2048, 768], P('rows', 'pos'), may hold values from -6 to 6
- segment_ids: int32 [16, 2048], P('rows', 'pos'), may hold values from 0 to 2, as said below
- group_sizes: int32 [16, 2], P('rows'), may hold values from 4 to 16, as said below
- prefix_lens: int32 [16, 2], P('rows'), may hold values from 1 to 768, as said below
- solution_lens: int32 [16, 2, 16], P('rows'), may hold values from 0 to 657, as said below
- padding_counts: int32 [16], P('rows'), may hold values from 0 to 128, as said below
- attn_gain: bfloat16 [768], replicated, may hold values from 0.5 to 1.5
- attn_shift: bfloat16 [768], replicated, may hold values from -1 to 1
- w_qkv: bfloat16 [768, 2304], replicated, may hold values from -0.21875 to 0.21875
- query_bias: bfloat16 [768], replicated, may hold values from -2.5 to 2.5
- value_bias: bfloat16 [768], replicated, may hold values from -1.5 to 1.5
- w_out: bfloat16 [768, 768], replicated, may hold values from -0.875 to 0.875
- out_bias: bfloat16 [768], replicated, may hold values from -1.5 to 1.5
- ffn_gain: bfloat16 [768], replicated, may hold values from 0.5 to 1.5
- ffn_shift: bfloat16 [768], replicated, may hold values from -1 to 1
- w_up: bfloat16 [768, 3072], replicated, may hold values from -0.21875 to 0.21875
- up_bias: bfloat16 [3072], replicated, may hold values from -2.5 to 2.5
- w_down: bfloat16 [3072, 768], replicated, may hold values from -0.109375 to 0.109375
- down_bias: bfloat16 [768], replicated, may hold values from -1.5 to 1.5
- cotangent: bfloat16 [16, 2048, 768], P('rows', 'pos'), may hold values from -6 to 6
Outputs:
- layer_out: bfloat16 [16, 2048, 768], P('rows', 'pos')
- tokens_grad: bfloat16 [16, 2048, 768], P('rows', 'pos')
- grad_attn_gain: float32 [768], replicated
- grad_attn_shift: float32 [768], replicated
- grad_w_qkv: float32 [768, 2304], replicated
- grad_query_bias: float32 [768], replicated
- grad_value_bias: float32 [768], replicated
- grad_w_out: float32 [768, 768], replicated
- grad_out_bias: float32 [768], replicated
- grad_ffn_gain: float32 [768], replicated
- grad_ffn_shift: float32 [768], replicated
- grad_w_up: float32 [768, 3072], replicated
- grad_up_bias: float32 [3072], replicated
- grad_w_down: float32 [3072, 768], replicated
- grad_down_bias: float32 [768], replicated
Inputs may be any that keep to these rules, and one draw needn't show every extreme that they name: `group_sizes`: each group holds this many solutions. `solution_lens`: A group's solutions at index group_sizes or more have length 0, the others 1 or more. `prefix_lens`: each prefix has 1 or more positions. `segment_ids`: A row holds group 0 (its prefix, then its solutions in order), then group 1, then padding_counts padding positions marked 2; together exactly 2048 positions. `padding_counts`: the row's positions after both groups.
All inputs are finite; a program needn't handle non-finite values.
Results may differ from a plain program's by a relative error of at most 0.012.
Values may be sent and summed in bfloat16 or wider, within the bound.
No kernel may reach another device: no remote copies, remote signals or barrier semaphores. Data moves between devices by JAX's collectives and lax.ppermute only.
A program may use at most 448 MiB of HBM per device.

v0:
```python
import math

import jax
import jax.numpy as jnp
from jax import lax
from jax.sharding import PartitionSpec as P

HEAD_DIM = 64


EPS = 1e-05
NEG = -1e30
GELU_C = 0.7978845608028654


def layer_norm(values, gain, shift):
    center = values - jnp.mean(values, axis=-1, keepdims=True)
    spread = jnp.mean(center * center, axis=-1, keepdims=True)
    return center * lax.rsqrt(spread + EPS) * gain + shift


def gelu_tanh(values):
    return 0.5 * values * (1.0 + jnp.tanh(GELU_C * (values + 0.044715 * values * values * values)))


def classes(places, segments, sizes_row, prefix_row, lens_row, padding_row, length):
    slots = jnp.arange(lens_row.shape[-1], dtype=jnp.int32)
    kept_lens = jnp.where(slots[None, None, :] < sizes_row[:, :, None], lens_row, 0)
    solution_ends = jnp.cumsum(kept_lens, axis=-1)
    totals = prefix_row + solution_ends[:, :, -1]
    starts = jnp.cumsum(totals, axis=-1) - totals
    groups = jnp.arange(sizes_row.shape[-1], dtype=jnp.int32)
    member = segments[:, :, None] == groups[None, None, :]
    group_start = jnp.sum(jnp.where(member, starts[:, None, :], 0), axis=-1)
    prefix_here = jnp.sum(jnp.where(member, prefix_row[:, None, :], 0), axis=-1)
    inside = places[None, :] - group_start - prefix_here
    passed = jnp.where(
        member[:, :, :, None], inside[:, :, None, None] >= solution_ends[:, None, :, :], False
    )
    passed_count = jnp.sum(passed.astype(jnp.int32), axis=(2, 3))
    branch = jnp.where(inside < 0, -1, passed_count)
    padded = places[None, :] >= length - padding_row[:, None]
    class_id = jnp.where(padded, -1, segments)
    branch = jnp.where(padded, -2, branch)
    return (class_id, branch)


def visible(query_class, query_branch, query_places, key_class, key_branch, key_places):
    same = query_class[:, :, None] == key_class[:, None, :]
    causal = key_places[None, None, :] <= query_places[None, :, None]
    shared = (key_branch[:, None, :] == -1) | (key_branch[:, None, :] == query_branch[:, :, None])
    return same & causal & shared


def heads_first(values):
    return values.reshape(
        values.shape[0], values.shape[1], values.shape[2] // HEAD_DIM, HEAD_DIM
    ).transpose(2, 0, 1, 3)


def heads_last(values):
    return values.transpose(1, 2, 0, 3).reshape(
        values.shape[1], values.shape[2], values.shape[0] * values.shape[3]
    )


def head_scores(query_head, key_head, allowed, score_scale):
    product = (
        jnp.einsum("rqe,rke->rqk", query_head, key_head, preferred_element_type=jnp.float32)
        * score_scale
    )
    return jnp.where(allowed, product, NEG)


def outer_sum(left, right):
    return lax.dot_general(
        left.reshape(-1, left.shape[-1]),
        right.reshape(-1, right.shape[-1]),
        (((0,), (0,)), ((), ())),
        preferred_element_type=jnp.float32,
    )


def back_through(grad, weight):
    return jnp.einsum("rpo,io->rpi", grad, weight, preferred_element_type=jnp.float32)


def column_sum(values):
    return jnp.sum(values, axis=(0, 1), dtype=jnp.float32)


def per_device(
    tokens,
    segment_ids,
    group_sizes,
    prefix_lens,
    solution_lens,
    padding_counts,
    attn_gain,
    attn_shift,
    w_qkv,
    query_bias,
    value_bias,
    w_out,
    out_bias,
    ffn_gain,
    ffn_shift,
    w_up,
    up_bias,
    w_down,
    down_bias,
    cotangent,
):
    row_count, local_len, model_width = tokens.shape
    row_len = local_len * lax.axis_size("pos")
    score_scale = 1.0 / math.sqrt(HEAD_DIM)
    local_places = lax.axis_index("pos") * local_len + jnp.arange(local_len, dtype=jnp.int32)
    all_places = jnp.arange(row_len, dtype=jnp.int32)
    inputs = tokens.astype(jnp.float32)
    normed_one, norm_one_pull = jax.vjp(
        layer_norm, inputs, attn_gain.astype(jnp.float32), attn_shift.astype(jnp.float32)
    )
    act_one = normed_one.astype(jnp.bfloat16)
    projected = jnp.dot(act_one, w_qkv, preferred_element_type=jnp.float32)
    queries = (projected[..., :model_width] + query_bias.astype(jnp.float32)).astype(jnp.bfloat16)
    keys_local = projected[..., model_width : 2 * model_width].astype(jnp.bfloat16)
    values_local = (projected[..., 2 * model_width :] + value_bias.astype(jnp.float32)).astype(
        jnp.bfloat16
    )
    segment_wire = segment_ids.astype(jnp.bfloat16)
    keys_all, values_all, segment_all = (
        lax.all_gather(keys_local, "pos", axis=1, tiled=True),
        lax.all_gather(values_local, "pos", axis=1, tiled=True),
        lax.all_gather(segment_wire, "pos", axis=1, tiled=True),
    )
    query_class, query_branch = classes(
        local_places, segment_ids, group_sizes, prefix_lens, solution_lens, padding_counts, row_len
    )
    key_class, key_branch = classes(
        all_places,
        segment_all.astype(jnp.int32),
        group_sizes,
        prefix_lens,
        solution_lens,
        padding_counts,
        row_len,
    )
    allowed = visible(query_class, query_branch, local_places, key_class, key_branch, all_places)

    def forward_head(triple):
        query_head, key_head, value_head = triple
        scores = head_scores(query_head, key_head, allowed, score_scale)
        top_head = jnp.max(scores, axis=-1)
        weights = jnp.exp(scores - top_head[..., None])
        total_head = jnp.sum(weights, axis=-1)
        probs_low = (weights / total_head[..., None]).astype(jnp.bfloat16)
        mixed_head = jnp.einsum(
            "rqk,rke->rqe", probs_low, value_head, preferred_element_type=jnp.float32
        )
        return (mixed_head, top_head, total_head)

    queries_heads = heads_first(queries)
    mixed_heads, top, total = lax.map(
        forward_head, (queries_heads, heads_first(keys_all), heads_first(values_all))
    )
    mixed_low = heads_last(mixed_heads).astype(jnp.bfloat16)
    resid = inputs + (
        jnp.dot(mixed_low, w_out, preferred_element_type=jnp.float32) + out_bias.astype(jnp.float32)
    )
    normed_two, norm_two_pull = jax.vjp(
        layer_norm, resid, ffn_gain.astype(jnp.float32), ffn_shift.astype(jnp.float32)
    )
    act_two = normed_two.astype(jnp.bfloat16)
    upper = jnp.dot(act_two, w_up, preferred_element_type=jnp.float32) + up_bias.astype(jnp.float32)
    hidden_full, gelu_pull = jax.vjp(gelu_tanh, upper)
    hidden = hidden_full.astype(jnp.bfloat16)
    layer_out = (
        resid
        + (
            jnp.dot(hidden, w_down, preferred_element_type=jnp.float32)
            + down_bias.astype(jnp.float32)
        )
    ).astype(jnp.bfloat16)
    grad_out = cotangent.astype(jnp.float32)
    grad_w_down = outer_sum(hidden, cotangent)
    grad_down_bias = column_sum(grad_out)
    (grad_upper_full,) = gelu_pull(back_through(cotangent, w_down))
    grad_upper = grad_upper_full.astype(jnp.bfloat16)
    grad_w_up = outer_sum(act_two, grad_upper)
    grad_up_bias = column_sum(grad_upper)
    grad_resid_norm, grad_ffn_gain, grad_ffn_shift = norm_two_pull(back_through(grad_upper, w_up))
    grad_resid = grad_out + grad_resid_norm
    grad_attn = grad_resid.astype(jnp.bfloat16)
    grad_w_out = outer_sum(mixed_low, grad_attn)
    grad_out_bias = column_sum(grad_attn)
    grad_mixed = back_through(grad_attn, w_out).astype(jnp.bfloat16)
    keys_again, values_again = (
        lax.all_gather(keys_local, "pos", axis=1, tiled=True),
        lax.all_gather(values_local, "pos", axis=1, tiled=True),
    )
    grad_mixed_heads = heads_first(grad_mixed)

    def backward_head(items):
        query_head, key_head, value_head, grad_head, top_head, total_head = items
        scores = head_scores(query_head, key_head, allowed, score_scale)
        probs = jnp.exp(scores - top_head[..., None]) / total_head[..., None]
        grad_probs = jnp.einsum(
            "rqe,rke->rqk", grad_head, value_head, preferred_element_type=jnp.float32
        )
        delta_head = jnp.sum(probs * grad_probs, axis=-1)
        grad_scores = (probs * (grad_probs - delta_head[..., None])).astype(jnp.bfloat16)
        query_grad = (
            jnp.einsum("rqk,rke->rqe", grad_scores, key_head, preferred_element_type=jnp.float32)
            * score_scale
        ).astype(jnp.bfloat16)
        key_term = (
            jnp.einsum("rqk,rqe->rke", grad_scores, query_head, preferred_element_type=jnp.float32)
            * score_scale
        )
        value_term = jnp.einsum(
            "rqk,rqe->rke",
            probs.astype(jnp.bfloat16),
            grad_head,
            preferred_element_type=jnp.float32,
        )
        return (query_grad, key_term, value_term, delta_head)

    query_heads_grad, key_heads, value_heads, delta = lax.map(
        backward_head,
        (
            queries_heads,
            heads_first(keys_again),
            heads_first(values_again),
            grad_mixed_heads,
            top,
            total,
        ),
    )
    key_sum, value_sum = (
        lax.psum_scatter(heads_last(key_heads), "pos", scatter_dimension=1, tiled=True),
        lax.psum_scatter(heads_last(value_heads), "pos", scatter_dimension=1, tiled=True),
    )
    grad_queries = heads_last(query_heads_grad)
    grad_keys = key_sum.astype(jnp.bfloat16)
    grad_values = value_sum.astype(jnp.bfloat16)
    grad_project = jnp.concatenate([grad_queries, grad_keys, grad_values], axis=-1)
    grad_w_qkv = outer_sum(act_one, grad_project)
    grad_query_bias = column_sum(grad_queries)
    grad_value_bias = column_sum(grad_values)
    grad_input_norm, grad_attn_gain, grad_attn_shift = norm_one_pull(
        back_through(grad_project, w_qkv)
    )
    tokens_grad = (grad_resid + grad_input_norm).astype(jnp.bfloat16)
    summed = lax.psum(
        (
            grad_attn_gain,
            grad_attn_shift,
            grad_w_qkv,
            grad_query_bias,
            grad_value_bias,
            grad_w_out,
            grad_out_bias,
            grad_ffn_gain,
            grad_ffn_shift,
            grad_w_up,
            grad_up_bias,
            grad_w_down,
            grad_down_bias,
        ),
        ("rows", "pos"),
    )
    return (
        layer_out,
        tokens_grad,
        summed[0],
        summed[1],
        summed[2],
        summed[3],
        summed[4],
        summed[5],
        summed[6],
        summed[7],
        summed[8],
        summed[9],
        summed[10],
        summed[11],
        summed[12],
    )


def solution(mesh):
    in_specs = (
        P("rows", "pos", None),
        P("rows", "pos"),
        P("rows", None),
        P("rows", None),
        P("rows", None, None),
        P("rows"),
        P(),
        P(),
        P(),
        P(),
        P(),
        P(),
        P(),
        P(),
        P(),
        P(),
        P(),
        P(),
        P(),
        P("rows", "pos", None),
    )
    out_specs = (
        P("rows", "pos", None),
        P("rows", "pos", None),
        P(),
        P(),
        P(),
        P(),
        P(),
        P(),
        P(),
        P(),
        P(),
        P(),
        P(),
        P(),
        P(),
    )
    return jax.shard_map(
        per_device, mesh=mesh, in_specs=in_specs, out_specs=out_specs, check_vma=False
    )
```

profile of v0, /device:TPU:0, one launch (start us, length us, event | category | flops | bytes accessed | tf_op | source)
XLA Modules:
  0.0 1607.0 jit_solution(12968616290820048877)
XLA Ops:
  39.0 10.9 all_gather.12
  60.9 38.5 %all-gather.5.cloned.1.call-done = bf16[4,2048,768]{2,1,0:T(8,128)(2,1)} async-done(((bf16[4,256,768]{2,1,0:T(8,128)(2,1)}), bf16[4,2048,768]{2,1,0:T(8,128)(2,1)}) %all-gather.5.cloned.1.call-update) | async-done | bytes 12582928 | tf_op jit(solution)/shard_map/all_gather | solution.py:133
  99.3 16.5 %copy.82 = bf16[4,2048,768]{1,2,0:T(8,128)(2,1)} copy(bf16[4,2048,768]{2,1,0:T(8,128)(2,1)} %all-gather.5.cloned.1.call-done) | data formatting | bytes 25165824 | tf_op jit(solution)/shard_map/all_gather | solution.py:133
  115.8 10.7 copy.89
  126.5 47.4 %all-gather.3.cloned.1.call-done = bf16[4,2048,768]{2,1,0:T(8,128)(2,1)} async-done(((bf16[4,256,768]{2,1,0:T(8,128)(2,1)}), bf16[4,2048,768]{2,1,0:T(8,128)(2,1)}) %all-gather.3.cloned.1.call-update) | async-done | bytes 12582928 | tf_op jit(solution)/shard_map/all_gather | solution.py:132
  173.8 16.0 copy.81
  189.9 10.7 copy.88
  200.6 127.0 %while.30 = (s32[]{:T(128)}, bf16[12,4,256,64]{2,3,0,1:T(8,128)(2,1)}, f32[12,4,256]{2,1,0:T(4,128)}, f32[12,4,256]{2,1,0:T(4,128)}, bf16[12,4,256,64]{2,3,1,0:T...) while((s32[]{:T(128)}, ...), condition=%wide.region_13.14_spmd.clone, body=%wide.region_10.13_spmd.clone.sunk | while | flops 564131840 | bytes 28301456 | solution.py:163
  200.6 5.2 fusion.127
  242.9 5.2 fusion.127
  264.1 5.2 fusion.127
  332.2 8.5 fusion.65
  340.7 17.8 %convert_reduce_fusion = (f32[3072]{0:T(1024)}, bf16[4,256,3072]{2,1,0:T(8,128)(2,1)S(1)}) fusion(bf16[4,256,768]{2,1,0:T(8,128)(2,1)S(1)} %copy-done.12, bf16[3072,768]{1,0:T(8,128)(2,1)} %param.41, f32[4,256,3072]{2,1,0:T(8,128)} %fusion.65, f32[3072]{0:T(1024)S(1)} %copy-done.50), kind=kOutput, calls=%fused_computation.65 | convolution fusion | flops 4916769792 | bytes 25190400 | tf_op jit(solution)/shard_map/rpo,io->rpi/dot_general | solution.py:85
  358.5 6.1 multiply_reduce_fusion.1
  374.3 422.0 %while.31 = (s32[]{:T(128)}, bf16[12,4,256,64]{2,3,0,1:T(8,128)(2,1)}, f32[12,4,2048,64]{2,3,0,1:T(8,128)}, f32[12,4,2048,64]{2,3,0,1:T(8,128)}, bf16[12,4,256,6...) while((s32[]{:T(128)}, ...), condition=%wide.region_20.21_spmd.clone, body=%wide.region_18.20_spmd.clone.sunk | while | flops 1374288896 | bytes 124245304 | solution.py:228
  377.7 9.8 multiply_reduce_fusion.5
  387.5 8.5 multiply_convert_fusion.5
  400.6 5.8 fusion.141
  412.8 9.8 multiply_reduce_fusion.5
  422.6 8.5 multiply_convert_fusion.5
  435.7 5.8 fusion.141
  447.9 9.8 multiply_reduce_fusion.5
  457.7 8.5 multiply_convert_fusion.5
  470.8 5.8 fusion.141
  483.1 9.8 multiply_reduce_fusion.5
  492.8 8.5 multiply_convert_fusion.5
  506.0 5.8 fusion.141
  518.3 9.8 multiply_reduce_fusion.5
  528.1 8.5 multiply_convert_fusion.5
  541.2 5.8 fusion.141
  553.5 9.8 multiply_reduce_fusion.5
  563.3 8.5 multiply_convert_fusion.5
  576.4 5.9 fusion.141
  588.7 9.8 multiply_reduce_fusion.5
  598.5 8.5 multiply_convert_fusion.5
  611.6 5.8 fusion.141
  624.0 9.8 multiply_reduce_fusion.5
  633.8 8.5 multiply_convert_fusion.5
  646.9 5.8 fusion.141
  659.1 9.8 multiply_reduce_fusion.5
  668.9 8.5 multiply_convert_fusion.5
  682.0 5.8 fusion.141
  694.3 9.8 multiply_reduce_fusion.5
  704.0 8.5 multiply_convert_fusion.5
  717.1 5.8 fusion.141
  729.4 9.8 multiply_reduce_fusion.5
  739.2 8.5 multiply_convert_fusion.5
  752.3 5.9 fusion.141
  764.7 9.8 multiply_reduce_fusion.5
  774.5 8.5 multiply_convert_fusion.5
  787.5 5.8 fusion.141
  796.4 24.7 %copy.99 = f32[4,2048,768]{2,1,0:T(8,128)} copy(f32[4,2048,768]{1,2,0:T(8,128)} %bitcast.185) | data formatting | bytes 50331648 | tf_op jit(solution)/shard_map/reshape | solution.py:62
  821.2 27.0 %copy.101 = f32[4,2048,768]{2,1,0:T(8,128)} copy(f32[4,2048,768]{1,2,0:T(8,128)} %bitcast.184) | data formatting | bytes 50331648 | tf_op jit(solution)/shard_map/reshape | solution.py:62
  851.5 5.3 convolution_bitcast_fusion.3
  856.8 10.8 convolution_bitcast_fusion.1
  867.7 13.2 convolution_bitcast_fusion
  880.8 96.7 %reduce-scatter.3.cloned.1.call-done = f32[4,256,768]{2,1,0:T(8,128)} async-done(((f32[4,2048,768]{2,1,0:T(8,128)}), f32[4,256,768]{2,1,0:T(8,128)}) %reduce-scatter.3.cloned.1.call-update) | async-done | bytes 3145744 | tf_op jit(solution)/shard_map/reduce_scatter | solution.py:240
  980.8 156.6 %reduce-scatter.5.cloned.1.call-done = f32[4,256,768]{2,1,0:T(8,128)} async-done(((f32[4,2048,768]{2,1,0:T(8,128)}), f32[4,256,768]{2,1,0:T(8,128)}) %reduce-scatter.5.cloned.1.call-update) | async-done | bytes 3145744 | tf_op jit(solution)/shard_map/reduce_scatter | solution.py:241
  1141.6 7.2 convolution_bitcast_fusion.2
  1153.1 14.9 add_convert_fusion.1
  1178.6 42.5 %all-reduce = (f32[768]{0:T(1024)}, f32[768]{0:T(1024)}, f32[768]{0:T(1024)}, f32[768]{0:T(1024)}, f32[768]{0:T(1024)}, /*index=5*/f32[768]{0:T(1024)}, f32[768]{0:T(1024)}, f32[3072]{0:T(1024)}, f32[768]{0:T(1024)}) all-reduce(f32[768]{0:T(1024)} %get-tuple-element.258, ...), channel_id=1, replica_groups=mesh['rows'=4,'pos'=8] {'rows','pos'}, use_global_device_ids=true, to_apply=%region_26.27 | all-reduce | flops 9216 | bytes 73728 | tf_op jit(solution)/shard_map/psum | solution.py:254
  1221.1 357.8 %all-reduce.4.cloned.1.call-done = (f32[768,2304]{1,0:T(8,128)}, f32[768,768]{1,0:T(8,128)}, f32[768,3072]{1,0:T(8,128)}, f32[3072,768]{1,0:T(8,128)}) async-done(((f32[768,2304]{1,0:T(8,128)}, f32[768,768]{1,0:T(8,128)}, f32[768,3072]{1,0:T(8,128)}, f32[3072,768]{1,0:T(8,128)}), (f32[768,2304]{1,0:T(8,128)}, f32[768,768]{1,0:T(8,128)}, f32[768,3072]{1,0:T(8,128)}, ...) | async-done | bytes 28311568 | tf_op jit(solution)/shard_map/psum | solution.py:254
  1578.9 6.6 copy.172
  1586.9 9.3 copy.174
  (426 shorter events, 330.9 us)
Async XLA Ops:
  7.2 8.3 copy-start
  7.2 92.1 %all-gather.5.cloned.1.call-start = ((), (), s32[]{:S(2)}) async-start(), calls=%async_computation.3 | async-start | bytes 14155776 | tf_op jit(solution)/shard_map/all_gather | solution.py:133
  7.2 8.3 copy-start.7
  8.1 6.8 copy-start.39
  9.2 5.7 copy-start.58
  19.7 4.7 copy-start.10
  24.4 149.4 %all-gather.3.cloned.1.call-start = ((), (), s32[]{:S(2)}) async-start(), calls=%async_computation.2 | async-start | bytes 14155776 | tf_op jit(solution)/shard_map/all_gather | solution.py:132
  27.7 949.9 %reduce-scatter.3.cloned.1.call-start = ((), (), s32[]{:S(2)}) async-start(), calls=%async_computation.4 | async-start | bytes 28311552 | tf_op jit(solution)/shard_map/reduce_scatter | solution.py:240
  28.7 336.0 %copy-start.24 = (f32[768]{0:T(1024)}, f32[768]{0:T(1024)S(1)}, u32[]{:S(2)}) copy-start(f32[768]{0:T(1024)S(1)} %convert_element_type.132) | copy-start | bytes 9220
  29.4 302.8 %copy-start.26 = (f32[768]{0:T(1024)}, f32[768]{0:T(1024)S(1)}, u32[]{:S(2)}) copy-start(f32[768]{0:T(1024)S(1)} %convert_element_type.133) | copy-start | bytes 9220
  52.6 7.1 copy-start.54
  189.9 10.7 copy-start.55
  327.6 4.6 slice-start.4
  331.6 33.0 %copy-start.3 = (f32[4,256,768]{2,1,0:T(8,128)}, f32[4,256,768]{2,1,0:T(8,128)S(1)}, u32[]{:S(2)}) copy-start(f32[4,256,768]{2,1,0:T(8,128)S(1)} %get-tuple-element.364) | copy-start | bytes 9437188
  331.7 33.0 %copy-start.28 = (f32[4,256]{1,0:T(4,128)}, f32[4,256]{1,0:T(4,128)S(1)}, u32[]{:S(2)}) copy-start(f32[4,256]{1,0:T(4,128)S(1)} %broadcast_multiply_fusion) | copy-start | bytes 12292
  332.2 32.5 %copy-start.30 = (f32[4,256]{1,0:T(4,128)}, f32[4,256]{1,0:T(4,128)S(1)}, u32[]{:S(2)}) copy-start(f32[4,256]{1,0:T(4,128)S(1)} %fusion.92) | copy-start | bytes 12292
  332.2 8.5 copy-start.12
  332.2 8.5 copy-start.50
  358.5 6.1 copy-start.11
  377.7 9.8 copy-start.1
  400.6 5.8 copy-start.2
  412.8 9.8 copy-start.1
  435.7 5.8 copy-start.2
  447.9 9.8 copy-start.1
  470.8 5.8 copy-start.2
  483.1 9.8 copy-start.1
  506.0 5.8 copy-start.2
  518.3 9.8 copy-start.1
  541.2 5.8 copy-start.2
  553.5 9.8 copy-start.1
  576.4 5.9 copy-start.2
  588.7 9.8 copy-start.1
  611.6 5.9 copy-start.2
  624.0 9.8 copy-start.1
  646.9 5.8 copy-start.2
  659.1 9.8 copy-start.1
  682.0 5.8 copy-start.2
  694.3 9.8 copy-start.1
  717.1 5.8 copy-start.2
  729.4 9.8 copy-start.1
  752.3 5.9 copy-start.2
  764.7 9.8 copy-start.1
  787.5 5.8 copy-start.2
  821.1 316.3 %reduce-scatter.5.cloned.1.call-start = ((), (), s32[]{:S(2)}) async-start(), calls=%async_computation.5 | async-start | bytes 28311552 | tf_op jit(solution)/shard_map/reduce_scatter | solution.py:241
  848.2 730.7 %all-reduce.4.cloned.1.call-start = ((), (), s32[]{:S(2)}) async-start(), calls=%async_computation.6 | async-start | bytes 56623104 | tf_op jit(solution)/shard_map/psum | solution.py:254
  851.4 5.3 copy-start.4
  851.4 5.3 copy-start.25
  851.4 5.3 copy-start.27
  851.4 5.3 copy-start.29
  851.4 5.3 copy-start.31
  856.8 10.8 copy-start.13
  856.8 10.8 copy-start.51
  977.6 163.9 %copy-start.40 = (f32[768]{0:T(1024)S(1)}, f32[768]{0:T(1024)}, u32[]{:S(2)}) copy-start(f32[768]{0:T(1024)} %copy-done.39) | copy-start | bytes 9220
  977.6 163.9 %copy-start.42 = (f32[4,256]{1,0:T(4,128)S(1)}, f32[4,256]{1,0:T(4,128)}, u32[]{:S(2)}) copy-start(f32[4,256]{1,0:T(4,128)} %copy-done.41) | copy-start | bytes 12292
  977.6 163.9 %copy-start.59 = (f32[768]{0:T(1024)S(1)}, f32[768]{0:T(1024)}, u32[]{:S(2)}) copy-start(f32[768]{0:T(1024)} %copy-done.58) | copy-start | bytes 9220
  980.8 160.7 %copy-start.38 = (f32[4,256]{1,0:T(4,128)S(1)}, f32[4,256]{1,0:T(4,128)}, u32[]{:S(2)}) copy-start(f32[4,256]{1,0:T(4,128)} %copy-done.37) | copy-start | bytes 12292
  1153.1 14.9 copy-start.9
  1153.1 14.9 copy-start.17
  1153.1 14.9 copy-start.20
  1153.1 14.9 copy-start.22
  1578.9 6.6 copy-start.15
  1585.5 10.7 slice-start
  1586.9 9.3 slice-start.1
  1586.9 9.3 slice-start.2
  (67 other events, 179.5 us)
Sparse Core Ops, SparseCore 0:
  24.5 74.7 all-gather.4
  101.8 71.9 all-gather.2
  821.2 156.2 reduce-scatter.2
  981.0 156.3 reduce-scatter.4
  1148.9 429.9 all-reduce.3
where the time goes:
time: 1620 us; the launch traced here: 1610 us
  waiting for transfers between devices  697 us (43%)
  matrix products  514 us (32%)
  local copies, waits for them, and re-layouts  167 us (10%)
  other arithmetic  160 us (10%)
  blocking collectives  53.4 us (3%)
    psum x1, waiting for transfers between devices, per_device(): lax.psum((grad_attn_gain, grad_attn_shift, grad_w_qkv, grad_query_bias, g...  358 us
    dot_general x24, matrix products, head_scores(): jnp.einsum('rqe,rke->rqk', query_head, key_head, preferred_element_type=j...  179 us
    reduce_scatter x1, waiting for transfers between devices, per_device(): lax.psum_scatter(heads_last(value_heads), 'pos', scatter_dimension=1, til...  157 us
    convert_element_type x12, other arithmetic, backward_head(): (probs * (grad_probs - delta_head[..., None])).astype(jnp.bfloat16)  102 us
    reduce_scatter x1, waiting for transfers between devices, per_device(): lax.psum_scatter(heads_last(key_heads), 'pos', scatter_dimension=1, tiled...  96.7 us
    dot_general x12, matrix products, backward_head(): jnp.einsum('rqk,rqe->rke', probs.astype(jnp.bfloat16), grad_head, preferr...  69.7 us
    reshape x3, local copies, waits for them, and re-layouts, heads_last(): values.transpose(1, 2, 0, 3)  54.9 us
    dot_general x12, matrix products, backward_head(): jnp.einsum('rqk,rke->rqe', grad_scores, key_head, preferred_element_type=...  54.6 us
  transfers between devices with their start and end apart: 5, of which 5 were waited for; matrix products, arithmetic and copies ran while one was open for 9% of the time, Pallas kernels for 0%

commit v1 on v0

v1 whole, which is shorter than its diff:
```python
import functools

import jax
import jax.numpy as jnp
from jax import lax
from jax.experimental import pallas as pl
from jax.experimental.pallas import tpu as pltpu
from jax.sharding import PartitionSpec as P

HEAD_DIM = 64
EPS = 1e-05
NEG = -1e30
GELU_C = 0.7978845608028654
F32 = jnp.float32
BF16 = jnp.bfloat16
NT = (((1,), (1,)), ((), ()))
TN = (((0,), (0,)), ((), ()))


def layer_norm(values, gain, shift):
    center = values - jnp.mean(values, axis=-1, keepdims=True)
    spread = jnp.mean(center * center, axis=-1, keepdims=True)
    return center * lax.rsqrt(spread + EPS) * gain + shift


def gelu_tanh(values):
    return 0.5 * values * (1.0 + jnp.tanh(GELU_C * (values + 0.044715 * values * values * values)))


def matmul(left, right, dims=(((1,), (0,)), ((), ()))):
    return lax.dot_general(left, right, dims, preferred_element_type=F32)


def head_pairs(heads):
    return [(h // 2, min(128, heads * HEAD_DIM - (h // 2) * 128)) for h in range(heads)]


def mask_bias(info_ref, key_start, size):
    prefix_start, prefix_end = info_ref[0, 0:1, :], info_ref[0, 1:2, :]
    own_start, query_place = info_ref[0, 2:3, :], info_ref[0, 3:4, :]
    key_place = key_start + lax.broadcasted_iota(jnp.int32, (size, size), 0)
    allowed = ((key_place >= prefix_start) & (key_place < prefix_end)) | (
        (key_place >= own_start) & (key_place <= query_place)
    )
    return jnp.where(allowed, 0.0, NEG).astype(F32)


def fill_padded(source_ref, target_ref, heads):
    for h, (pair, width) in enumerate(head_pairs(heads)):
        rows = source_ref[0, pair * 128 : pair * 128 + width, :]
        if width == 128:
            keep = (lax.broadcasted_iota(jnp.int32, rows.shape, 0) // HEAD_DIM) == (h % 2)
            rows = jnp.where(keep, rows, jnp.zeros_like(rows))
        target_ref[h, 0:width, :] = rows


def forward_kernel(
    heads, blocks, phys_ref, flag_ref, query_t_ref, key_ref, value_t_ref, info_ref,
    mixed_ref, out_t_ref, lse_ref, bias_sc, top_sc, total_sc, acc_sc, query_sc,
):
    size = query_t_ref.shape[2]
    i = pl.program_id(0)
    fill_padded(query_t_ref, query_sc, heads)
    top_sc[...] = jnp.full_like(top_sc, NEG)
    total_sc[...] = jnp.zeros_like(total_sc)
    acc_sc[...] = jnp.zeros_like(acc_sc)

    @pl.loop(0, i + 1)
    def _(j):
        @pl.when(flag_ref[i * blocks + j] > 0)
        def _():
            at = phys_ref[j]
            bias_sc[...] = mask_bias(info_ref, j * size, size)
            for h, (pair, width) in enumerate(head_pairs(heads)):
                rows = slice(h * HEAD_DIM, (h + 1) * HEAD_DIM)
                scores = (
                    matmul(key_ref[at, :, pair * 128 : pair * 128 + width], query_sc[h, 0:width, :])
                    + bias_sc[...]
                )
                old = top_sc[h]
                top = jnp.maximum(old, jnp.max(scores, axis=0, keepdims=True))
                shrink = jnp.exp(old - top)
                weights = jnp.exp(scores - top)
                total_sc[h] = shrink * total_sc[h] + jnp.sum(weights, axis=0, keepdims=True)
                top_sc[h] = top
                acc_sc[rows, :] = shrink * acc_sc[rows, :] + matmul(
                    value_t_ref[at, rows, :], weights.astype(BF16)
                )

    for h in range(heads):
        rows = slice(h * HEAD_DIM, (h + 1) * HEAD_DIM)
        out_t_ref[0, rows, :] = acc_sc[rows, :] / total_sc[h]
        lse_ref[0, h : h + 1, :] = top_sc[h] + jnp.log(total_sc[h])
    mixed_ref[0] = out_t_ref[0].T.astype(BF16)


def attention_forward(phys, flags, query_t, key, value_t, info, heads):
    blocks, width, size = query_t.shape
    lse_rows = -(-heads // 8) * 8
    whole = pl.Buffered(1)
    spec = pltpu.PrefetchScalarGridSpec(
        num_scalar_prefetch=2,
        grid=(blocks,),
        in_specs=[
            pl.BlockSpec((1, width, size), lambda i, p, f: (p[i], 0, 0)),
            pl.BlockSpec((blocks, size, width), lambda i, p, f: (0, 0, 0), pipeline_mode=whole),
            pl.BlockSpec((blocks, width, size), lambda i, p, f: (0, 0, 0), pipeline_mode=whole),
            pl.BlockSpec((1, 8, size), lambda i, p, f: (i, 0, 0)),
        ],
        out_specs=[
            pl.BlockSpec((1, size, width), lambda i, p, f: (p[i], 0, 0)),
            pl.BlockSpec((1, width, size), lambda i, p, f: (p[i], 0, 0)),
            pl.BlockSpec((1, lse_rows, size), lambda i, p, f: (p[i], 0, 0)),
        ],
        scratch_shapes=[
            pltpu.VMEM((size, size), F32),
            pltpu.VMEM((heads, 1, size), F32),
            pltpu.VMEM((heads, 1, size), F32),
            pltpu.VMEM((width, size), F32),
            pltpu.VMEM((heads, 128, size), BF16),
        ],
    )
    pairs = heads * blocks * (blocks + 1) // 2 * size * size
    return pl.pallas_call(
        functools.partial(forward_kernel, heads, blocks),
        grid_spec=spec,
        out_shape=(
            jax.ShapeDtypeStruct((blocks, size, width), BF16),
            jax.ShapeDtypeStruct((blocks, width, size), F32),
            jax.ShapeDtypeStruct((blocks, lse_rows, size), F32),
        ),
        compiler_params=pltpu.CompilerParams(
            dimension_semantics=("arbitrary",), vmem_limit_bytes=60 * 1024 * 1024
        ),
        cost_estimate=pl.CostEstimate(
            flops=pairs * 4 * 128, transcendentals=pairs, bytes_accessed=blocks * size * width * 16
        ),
        name="attention_forward",
    )(phys, flags, query_t, key, value_t, info)


def backward_kernel(
    heads, blocks, phys_ref, flag_ref, query_t_ref, grad_t_ref, out_t_ref, lse_ref, info_ref,
    key_ref, key_t_ref, value_ref, query_grad_ref, key_grad_ref, value_grad_ref,
    bias_sc, query_grad_sc, key_grad_sc, value_grad_sc, query_sc, grad_sc, delta_sc,
):
    size = query_t_ref.shape[2]
    i = pl.program_id(0)

    @pl.when(i == 0)
    def _():
        key_grad_sc[...] = jnp.zeros_like(key_grad_sc)
        value_grad_sc[...] = jnp.zeros_like(value_grad_sc)

    fill_padded(query_t_ref, query_sc, heads)
    fill_padded(grad_t_ref, grad_sc, heads)
    query_grad_sc[...] = jnp.zeros_like(query_grad_sc)
    for h in range(heads):
        rows = slice(h * HEAD_DIM, (h + 1) * HEAD_DIM)
        delta_sc[h] = jnp.sum(
            grad_t_ref[0, rows, :].astype(F32) * out_t_ref[0, rows, :], axis=0, keepdims=True
        )

    @pl.loop(0, i + 1)
    def _(j):
        @pl.when(flag_ref[i * blocks + j] > 0)
        def _():
            at = phys_ref[j]
            bias_sc[...] = mask_bias(info_ref, j * size, size)
            for h, (pair, width) in enumerate(head_pairs(heads)):
                rows = slice(h * HEAD_DIM, (h + 1) * HEAD_DIM)
                lanes = slice(pair * 128, pair * 128 + width)
                scores = matmul(key_ref[at, :, lanes], query_sc[h, 0:width, :]) + bias_sc[...]
                probs = jnp.exp(scores - lse_ref[0, h : h + 1, :])
                grad_probs = matmul(value_ref[at, :, lanes], grad_sc[h, 0:width, :])
                grad_scores = (probs * (grad_probs - delta_sc[h])).astype(BF16)
                query_grad_sc[rows, :] += matmul(key_t_ref[at, rows, :], grad_scores)
                value_grad_sc[at, rows, :] += matmul(
                    grad_t_ref[0, rows, :], probs.astype(BF16), NT
                )
                key_grad_sc[at, rows, :] += matmul(query_t_ref[0, rows, :], grad_scores, NT)

    query_grad_ref[0] = (query_grad_sc[...] * 0.125).T.astype(BF16)

    @pl.when(i == blocks - 1)
    def _():
        for block in range(blocks):
            key_grad_ref[block] = key_grad_sc[block].T.astype(BF16)
            value_grad_ref[block] = value_grad_sc[block].T.astype(BF16)


def attention_backward(phys, flags, query_t, grad_t, out_t, lse, info, key, key_t, value, heads):
    blocks, width, size = query_t.shape
    moving_t = pl.BlockSpec((1, width, size), lambda i, p, f: (p[i], 0, 0))
    moving = pl.BlockSpec((1, size, width), lambda i, p, f: (p[i], 0, 0))
    whole = pl.BlockSpec(
        (blocks, size, width), lambda i, p, f: (0, 0, 0), pipeline_mode=pl.Buffered(1)
    )
    whole_t = pl.BlockSpec(
        (blocks, width, size), lambda i, p, f: (0, 0, 0), pipeline_mode=pl.Buffered(1)
    )
    spec = pltpu.PrefetchScalarGridSpec(
        num_scalar_prefetch=2,
        grid=(blocks,),
        in_specs=[
            moving_t,
            moving_t,
            moving_t,
            pl.BlockSpec((1, lse.shape[1], size), lambda i, p, f: (p[i], 0, 0)),
            pl.BlockSpec((1, 8, size), lambda i, p, f: (i, 0, 0)),
            whole,
            whole_t,
            whole,
        ],
        out_specs=[moving, whole, whole],
        scratch_shapes=[
            pltpu.VMEM((size, size), F32),
            pltpu.VMEM((width, size), F32),
            pltpu.VMEM((blocks, width, size), F32),
            pltpu.VMEM((blocks, width, size), F32),
            pltpu.VMEM((heads, 128, size), BF16),
            pltpu.VMEM((heads, 128, size), BF16),
            pltpu.VMEM((heads, 1, size), F32),
        ],
    )
    out = jax.ShapeDtypeStruct((blocks, size, width), BF16)
    pairs = heads * blocks * (blocks + 1) // 2 * size * size
    return pl.pallas_call(
        functools.partial(backward_kernel, heads, blocks),
        grid_spec=spec,
        out_shape=(out, out, out),
        compiler_params=pltpu.CompilerParams(
            dimension_semantics=("arbitrary",), vmem_limit_bytes=60 * 1024 * 1024
        ),
        cost_estimate=pl.CostEstimate(
            flops=pairs * 10 * 128, transcendentals=pairs, bytes_accessed=blocks * size * width * 20
        ),
        name="attention_backward",
    )(phys, flags, query_t, grad_t, out_t, lse, info, key, key_t, value)


def row_layout(sizes, prefixes, lens, padding, length, size):
    slots = jnp.arange(lens.shape[-1], dtype=jnp.int32)
    kept = jnp.where(slots[None, :] < sizes[:, None], lens, 0)
    ends = jnp.cumsum(kept, axis=-1)
    totals = prefixes + ends[:, -1]
    starts = jnp.cumsum(totals) - totals
    places = jnp.arange(length, dtype=jnp.int32)
    padded = places >= length - padding
    prefix_start = jnp.broadcast_to(length - padding, (length,))
    prefix_end = prefix_start
    own_start = prefix_start
    for g in range(sizes.shape[0]):
        member = (places >= starts[g]) & (places < starts[g] + totals[g]) & ~padded
        body = starts[g] + prefixes[g]
        inside = places - body
        base = jnp.max(jnp.where(inside[:, None] >= ends[g][None, :], ends[g][None, :], 0), axis=-1)
        solution = inside >= 0
        prefix_start = jnp.where(member, starts[g], prefix_start)
        prefix_end = jnp.where(member, jnp.where(solution, body, starts[g]), prefix_end)
        own_start = jnp.where(member, jnp.where(solution, body + base, starts[g]), own_start)
    blocks = length // size
    low = jnp.arange(blocks, dtype=jnp.int32)[None, :] * size
    high = low + size
    need = (
        jnp.maximum(prefix_start[:, None], low) < jnp.minimum(prefix_end[:, None], high)
    ) | (jnp.maximum(own_start[:, None], low) < jnp.minimum(places[:, None] + 1, high))
    flags = jnp.any(need.reshape(blocks, size, blocks), axis=1).astype(jnp.int32).reshape(-1)
    zero = jnp.zeros_like(places)
    info = jnp.stack([prefix_start, prefix_end, own_start, places, zero, zero, zero, zero])
    info = info.astype(jnp.int32).reshape(8, blocks, size).transpose(1, 0, 2)
    return info, flags


def swap(values, axis, mask):
    count = lax.axis_size(axis)
    return lax.ppermute(values, axis, [(i, i ^ mask) for i in range(count)])


def bits(count):
    return [1 << b for b in range(count.bit_length() - 1)]


def take(values, index):
    return lax.dynamic_index_in_dim(values, index, 0, keepdims=False)


def halve(values, steps):
    for axis, mask, bit in steps:
        two = values.reshape(2, values.shape[0] // 2, *values.shape[1:])
        arrived = swap(take(two, 1 - bit), axis, mask)
        values = (take(two, bit).astype(F32) + arrived.astype(F32)).astype(values.dtype)
    return values


def double(values, steps):
    for axis, mask, bit in reversed(steps):
        arrived = swap(values, axis, mask)
        first = jnp.where(bit == 0, values, arrived)
        second = jnp.where(bit == 0, arrived, values)
        values = jnp.concatenate([first, second], axis=0)
    return values


def per_device(
    row_axis,
    tokens,
    segment_ids,
    group_sizes,
    prefix_lens,
    solution_lens,
    padding_counts,
    attn_gain,
    attn_shift,
    w_qkv,
    query_bias,
    value_bias,
    w_out,
    out_bias,
    ffn_gain,
    ffn_shift,
    w_up,
    up_bias,
    w_down,
    down_bias,
    cotangent,
):
    rows, size, model = tokens.shape
    devices = lax.axis_size("pos")
    parts = devices // rows
    blocks = devices
    heads = model // HEAD_DIM // parts
    width = heads * HEAD_DIM
    place = lax.axis_index("pos")
    owner, part = place // parts, place % parts

    def bring(values):
        return jnp.stack(
            [
                swap(take(values, owner ^ m), "pos", m * parts) if m else take(values, owner)
                for m in range(rows)
            ]
        )

    def give_back(values):
        out = jnp.zeros_like(values)
        for m in range(rows):
            slab = swap(values[m], "pos", m * parts) if m else values[m]
            out = lax.dynamic_update_index_in_dim(out, slab, owner ^ m, 0)
        return out

    info, flags = row_layout(
        take(group_sizes, owner),
        take(prefix_lens, owner),
        take(solution_lens, owner),
        take(padding_counts, owner),
        blocks * size,
        size,
    )
    order = jnp.arange(blocks, dtype=jnp.int32)
    phys = (((order % parts) ^ part) * rows + ((order // parts) ^ owner)).astype(jnp.int32)

    def my_columns(start):
        return lax.dynamic_slice_in_dim(w_qkv, start * model + part * width, width, 1)

    w_mine = jnp.concatenate([my_columns(0), my_columns(1), my_columns(2)], axis=1)
    bias_q = lax.dynamic_slice_in_dim(query_bias, part * width, width, 0).astype(F32)
    bias_v = lax.dynamic_slice_in_dim(value_bias, part * width, width, 0).astype(F32)
    w_out_parts = [take(w_out.reshape(parts, width, model), part ^ s) for s in range(parts)]

    mine = bring(tokens)
    row = jnp.concatenate([mine] + [swap(mine, "pos", s) for s in range(1, parts)], axis=0)
    act_one = layer_norm(
        row.reshape(-1, model).astype(F32), attn_gain.astype(F32), attn_shift.astype(F32)
    ).astype(BF16)
    projected = matmul(act_one, w_mine)
    query = ((projected[:, :width] + bias_q).astype(BF16) * 0.125).astype(BF16)
    key = projected[:, width : 2 * width].astype(BF16)
    value = (projected[:, 2 * width :] + bias_v).astype(BF16)

    def blocked(values):
        return values.reshape(blocks, size, width)

    def turned(values):
        return blocked(values).transpose(0, 2, 1)

    query_t, key_t = turned(query), turned(key)
    mixed_all, out_t, lse = attention_forward(
        phys, flags, query_t, blocked(key), turned(value), info, heads
    )
    own_cotangent = bring(cotangent).reshape(-1, model)
    mixed_parts = []
    for s in range(parts):
        piece = mixed_all[s * rows : (s + 1) * rows]
        mixed_parts.append((swap(piece, "pos", s) if s else piece).reshape(-1, width))

    inputs = mine.reshape(-1, model).astype(F32)
    attn = sum(matmul(m, w) for m, w in zip(mixed_parts, w_out_parts))
    resid = inputs + (attn + out_bias.astype(F32))
    normed_two, norm_two_pull = jax.vjp(
        layer_norm, resid, ffn_gain.astype(F32), ffn_shift.astype(F32)
    )
    act_two = normed_two.astype(BF16)
    upper = matmul(act_two, w_up) + up_bias.astype(F32)
    hidden_full, gelu_pull = jax.vjp(gelu_tanh, upper)
    hidden = hidden_full.astype(BF16)
    layer_out = (resid + (matmul(hidden, w_down) + down_bias.astype(F32))).astype(BF16)
    grad_out = own_cotangent.astype(F32)
    grad_w_down = matmul(hidden, own_cotangent, TN).astype(BF16)
    grad_down_bias = jnp.sum(grad_out, axis=0)
    (grad_upper_full,) = gelu_pull(matmul(own_cotangent, w_down, NT))
    grad_upper = grad_upper_full.astype(BF16)
    grad_w_up = matmul(act_two, grad_upper, TN).astype(BF16)
    grad_up_bias = jnp.sum(grad_upper.astype(F32), axis=0)
    grad_resid_norm, grad_ffn_gain, grad_ffn_shift = norm_two_pull(matmul(grad_upper, w_up, NT))
    grad_resid = grad_out + grad_resid_norm
    grad_attn = grad_resid.astype(BF16)
    stacked = jnp.stack(mixed_parts)
    mixed = jnp.concatenate([take(stacked, g ^ part) for g in range(parts)], axis=1)
    grad_w_out = matmul(mixed, grad_attn, TN).astype(BF16)
    grad_out_bias = jnp.sum(grad_attn.astype(F32), axis=0)
    grad_mixed = [matmul(grad_attn, w, NT).astype(BF16) for w in w_out_parts]
    grad_all = jnp.concatenate(
        [swap(g, "pos", s) if s else g for s, g in enumerate(grad_mixed)], axis=0
    )
    grad_q, grad_k, grad_v = attention_backward(
        phys, flags, query_t, turned(grad_all), out_t, lse, info,
        blocked(key), key_t, blocked(value), heads,
    )
    grad_project = jnp.concatenate([grad_q, grad_k, grad_v], axis=2).reshape(-1, 3 * width)
    grad_w_mine = matmul(act_one, grad_project, TN).astype(BF16)
    grad_query_mine = jnp.sum(grad_q.astype(F32), axis=(0, 1))
    grad_value_mine = jnp.sum(grad_v.astype(F32), axis=(0, 1))
    grad_act = matmul(grad_project, w_mine, NT)
    local = rows * size
    grad_act_own = grad_act[:local]
    for s in range(1, parts):
        sent = grad_act[s * local : (s + 1) * local].astype(BF16)
        grad_act_own = grad_act_own + swap(sent, "pos", s).astype(F32)
    _, norm_one_pull = jax.vjp(layer_norm, inputs, attn_gain.astype(F32), attn_shift.astype(F32))
    grad_input_norm, grad_attn_gain, grad_attn_shift = norm_one_pull(grad_act_own)
    tokens_grad = (grad_resid + grad_input_norm).astype(BF16)

    row_place = lax.axis_index(row_axis)
    row_steps = [(row_axis, m, (row_place // m) % 2) for m in bits(lax.axis_size(row_axis))]
    own_steps = [("pos", m * parts, (owner // m) % 2) for m in bits(rows)]
    part_steps = [("pos", m, (part // m) % 2) for m in bits(parts)]
    one_way = part_steps + own_steps + row_steps
    other_way = part_steps + own_steps[::-1] + row_steps

    def total(values, steps):
        return double(halve(values, steps), steps).astype(F32)

    sum_w_down = total(grad_w_down, one_way)
    sum_w_up = total(grad_w_up, other_way)
    sum_w_out = total(grad_w_out, one_way)
    steps = other_way[len(part_steps) :]
    summed_mine = double(halve(grad_w_mine, steps), steps)
    pieces = [summed_mine] + [swap(summed_mine, "pos", s) for s in range(1, parts)]
    pieces = jnp.stack(pieces).reshape(parts, model, 3, width)
    pieces = [take(pieces, g ^ part) for g in range(parts)]
    sum_w_qkv = jnp.stack(pieces, axis=2).reshape(model, 3 * model).astype(F32)

    def placed(values):
        return lax.dynamic_update_slice_in_dim(jnp.zeros((model,), F32), values, part * width, 0)

    small = jnp.concatenate(
        [
            grad_attn_gain,
            grad_attn_shift,
            placed(grad_query_mine),
            placed(grad_value_mine),
            grad_out_bias,
            grad_ffn_gain,
            grad_ffn_shift,
            grad_down_bias,
            grad_up_bias,
        ]
    )
    for axis, mask, _ in one_way:
        small = small + swap(small, axis, mask)
    vectors = small[: 8 * model].reshape(8, model)
    return (
        give_back(layer_out.reshape(rows, size, model)),
        give_back(tokens_grad.reshape(rows, size, model)),
        vectors[0],
        vectors[1],
        sum_w_qkv,
        vectors[2],
        vectors[3],
        sum_w_out,
        vectors[4],
        vectors[5],
        vectors[6],
        sum_w_up,
        small[8 * model :],
        sum_w_down,
        vectors[7],
    )


def solution(mesh):
    in_specs = (
        P("rows", "pos", None),
        P("rows", "pos"),
        P("rows", None),
        P("rows", None),
        P("rows", None, None),
        P("rows"),
        *([P()] * 13),
        P("rows", "pos", None),
    )
    out_specs = (P("rows", "pos", None), P("rows", "pos", None), *([P()] * 13))
    return jax.shard_map(
        functools.partial(per_device, "rows"),
        mesh=mesh,
        in_specs=in_specs,
        out_specs=out_specs,
        check_vma=False,
    )
```

time: 1620 us -> 645 us (0.40)
  waiting for transfers between devices: 697 us -> 167 us
  matrix products: 514 us -> 84.6 us
  Pallas kernels: 0 us -> 101 us
  starting transfers between devices: 0.21 us -> 74.8 us
  other arithmetic: 160 us -> 97.7 us
  local copies, waits for them, and re-layouts: 167 us -> 108 us
  blocking collectives: 53.4 us -> 0 us
    dot_general x96 -> x14, matrix products: 514 us -> 84.6 us  [matmul(): return lax.dot_general(left, right, dims, preferred_element_type=F32)]
    psum x1 -> x0, waiting for transfers between devices: 358 us -> none  [per_device(): lax.psum((grad_attn_gain, grad_attn_shift, grad_w_qkv, grad_query_bias, g...]
    reduce_scatter x2 -> x0, waiting for transfers between devices: 253 us -> none  [the longest x1 157 us: per_device(): lax.psum_scatter(heads_last(value_heads), 'pos', scatter_dimension=1, til...]
    ppermute x0 -> x60, waiting for transfers between devices: none -> 167 us  [swap(): return lax.ppermute(values, axis, [(i, i ^ mask) for i in range(count)])]
    pallas_call x0 -> x2, Pallas kernels: none -> 101 us  [the longest x1 53.9 us: attention_backward(): pl.pallas_call(functools.partial(backward_kernel, heads, blocks), grid_sp...]
    all_gather x2 -> x0, waiting for transfers between devices: 85.8 us -> none  [the longest x1 47.4 us: per_device(): lax.all_gather(keys_local, 'pos', axis=1, tiled=True)]
    convert_element_type x24 -> x35, other arithmetic: 116 us -> 39.7 us  [the longest x3 11.1 us: total(): return double(halve(values, steps), steps).astype(F32)]
    ppermute x0 -> x60, starting transfers between devices: none -> 74.8 us  [swap(): return lax.ppermute(values, axis, [(i, i ^ mask) for i in range(count)])]
  transfers between devices with their start and end apart: 5 -> 60, of which waited for: 5 -> 30; matrix products, arithmetic and copies ran while one was open for 9% -> 32% of each run, Pallas kernels for 0% -> 16%
where the time goes in v1:
time: 645 us; the launch traced here: 641 us
  waiting for transfers between devices  167 us (26%)
  local copies, waits for them, and re-layouts  108 us (17%)
  Pallas kernels  101 us (16%)
  other arithmetic  97.7 us (15%)
  matrix products  84.6 us (13%)
  starting transfers between devices  74.8 us (12%)
  between operations  8.56 us (1%)
    ppermute x60, waiting for transfers between devices, swap(): return lax.ppermute(values, axis, [(i, i ^ mask) for i in range(count)])  167 us
    dot_general x14, matrix products, matmul(): return lax.dot_general(left, right, dims, preferred_element_type=F32)  84.6 us
    ppermute x60, starting transfers between devices, swap(): return lax.ppermute(values, axis, [(i, i ^ mask) for i in range(count)])  74.8 us
    pallas_call x1, Pallas kernels, attention_backward(): pl.pallas_call(functools.partial(backward_kernel, heads, blocks), grid_sp...  53.9 us
    pallas_call x1, Pallas kernels, attention_forward(): pl.pallas_call(functools.partial(forward_kernel, heads, blocks), grid_spe...  46.6 us
    unnamed x167, local copies, waits for them, and re-layouts  24.1 us
  transfers between devices with their start and end apart: 60, of which 30 were waited for; matrix products, arithmetic and copies ran while one was open for 32% of the time, Pallas kernels for 16%

profile of v1, /device:TPU:0, one launch (start us, length us, event | category | flops | bytes accessed | tf_op | source)
XLA Modules:
  0.0 641.4 jit_solution(4653604184167232635)
XLA Ops:
  0.7 2.7 constant_dynamic-slice_fusion
  3.4 3.0 collective-permute-start.8
  27.4 6.0 collective-permute-done
  35.5 6.8 %collective-permute-done.2 = bf16[256,768]{1,0:T(8,128)(2,1)S(1)} collective-permute-done((bf16[256,768]{1,0:T(8,128)(2,1)}, bf16[256,768]{1,0:T(8,128)(2,1)S(1)}, u32[]{:S(2)}, u32[]{:S(2)}) %collective-permute-start.2) | collective-permute-done | bytes 393248 | tf_op jit(solution)/shard_map/ppermute | solution.py:277
  55.0 2.7 fusion.68
  69.2 4.3 fusion.42
  82.2 46.6 %attention_forward.1 = (bf16[8,256,384]{2,1,0:T(8,128)(2,1)}, f32[8,384,256]{2,1,0:T(8,128)}, f32[8,8,256]{2,1,0:T(8,128)}) custom-call(s32[8]{0:T(128)} %fusion.88.phys_ref, s32[64]{0:T(128)} %reshape.652.flag_ref, bf16[8,384,256]{2,1,0:T(8,128)(2,1)} %bitcast.296, bf16[8,256,384]{2,1,0:T(8,128)(2,1)} %bitcast.268, bf16[8,384,256]{2,1,0:T(8,128)(2,1)} %copy.107.value_t_ref, ...), custom_call_target="tpu_custom_call" | custom-call | flops 7247757312 | bytes 12582912 | tf_op jit(solution)/shard_map/attention_forward/pallas_call | solution.py:124
  131.8 3.3 convert_reduce_fusion.2
  142.3 3.0 copy.116
  147.2 2.7 fusion.111
  150.3 5.6 fusion.97
  155.9 4.6 copy-done.15
  160.5 8.0 %convolution_convert_fusion = bf16[3072,768]{1,0:T(8,128)(2,1)S(1)} fusion(bf16[1024,768]{1,0:T(8,128)(2,1)S(1)} %bitcast.263, f32[1024,3072]{1,0:T(8,128)S(1)} %fusion.97, f32[3072]{0:T(1024)S(1)} %copy-done.62), kind=kOutput, calls=%fused_computation.20 | convolution fusion | flops 4865654784 | bytes 18886656 | tf_op jit(solution)/shard_map/dot_general | solution.py:31
  168.5 20.7 %convert_reduce_fusion = (f32[3072]{0:T(1024)}, bf16[1024,3072]{1,0:T(8,128)(2,1)}) fusion(bf16[1024,768]{1,0:T(8,128)(2,1)S(1)} %bitcast.264, bf16[3072,768]{1,0:T(8,128)(2,1)} %param.36, f32[1024,3072]{1,0:T(8,128)} %copy-done.15, f32[3072]{0:T(1024)S(1)} %copy-done.62), kind=kOutput, calls=%fused_computation.10 | convolution fusion | flops 4916769792 | bytes 25190400 | tf_op jit(solution)/shard_map/dot_general | solution.py:31
  189.3 9.6 %fusion.112 = (f32[768]{0:T(1024)}, f32[1024,768]{1,0:T(8,128)}) fusion(bf16[1024,3072]{1,0:T(8,128)(2,1)} %get-tuple-element.171, bf16[768,3072]{1,0:T(8,128)(2,1)S(1)} %bitcast.273), kind=kOutput, calls=%fused_computation.342 | convolution fusion | flops 4832623616 | bytes 14158848 | tf_op jit(solution)/shard_map/dot_general | solution.py:31
  198.9 5.6 convolution_convert_fusion.1
  204.6 12.3 %add_convert_fusion.3 = bf16[1024,768]{0,1:T(8,128)(2,1)S(1)} fusion(f32[1024,768]{0,1:T(8,128)S(1)} %get-tuple-element.167, bf16[3072,768]{1,0:T(8,128)(2,1)} %param.36, f32[768]{0:T(1024)S(1)} %copy-done.64, f32[1024,3072]{1,0:T(8,128)} %copy-done.15, f32[3072]{0:T(1024)S(1)} %copy-done.62), kind=kOutput, calls=%fused_computation.58 | convolution fusion | flops 4865654784 | bytes 22035456 | tf_op jit(solution)/shard_map/dot_general | solution.py:31
  218.1 3.1 collective-permute-start.7
  225.0 3.7 copy.114
  228.8 3.9 multiply_reduce_fusion.1
  258.7 2.6 copy.115
  261.3 53.9 %attention_backward.1 = (bf16[8,256,384]{2,1,0:T(8,128)(2,1)}, bf16[8,256,384]{2,1,0:T(8,128)(2,1)}, bf16[8,256,384]{2,1,0:T(8,128)(2,1)}) custom-call(s32[8]{0:T(128)} %fusion.88.phys_ref, s32[64]{0:T(128)} %reshape.652.flag_ref, bf16[8,384,256]{2,1,0:T(8,128)(2,1)} %bitcast.297, bf16[8,384,256]{2,1,0:T(8,128)(2,1)} %bitcast.299, ...), custom_call_target="tpu_custom_call" | custom-call | flops 18119393280 | bytes 15728640 | tf_op jit(solution)/shard_map/attention_backward/pallas_call | solution.py:228
  317.7 4.9 collective-permute-done.32
  323.2 4.0 collective-permute-done.33
  327.2 6.0 collective-permute-start.34
  333.3 5.0 fusion.12
  338.4 4.3 fusion.41
  349.8 17.3 %collective-permute-done.37 = bf16[96,768]{1,0:T(8,128)(2,1)S(1)} collective-permute-done((bf16[96,768]{1,0:T(8,128)(2,1)S(1)}, bf16[96,768]{1,0:T(8,128)(2,1)S(1)}, u32[]{:S(2)}, u32[]{:S(2)}) %collective-permute-start.37) | collective-permute-done | bytes 147488 | tf_op jit(solution)/shard_map/ppermute | solution.py:277
  373.0 4.7 collective-permute-done.38
  378.9 3.9 collective-permute-done.22
  385.3 3.6 collective-permute-done.23
  389.1 3.1 collective-permute-start.24
  392.2 3.0 fusion.10
  399.7 3.3 multiply_reduce_fusion.2
  409.5 5.1 collective-permute-done.25
  414.8 4.5 collective-permute-done.17
  422.5 12.3 %collective-permute-done.41 = bf16[192,3072]{1,0:T(8,128)(2,1)S(1)} collective-permute-done((bf16[192,3072]{1,0:T(8,128)(2,1)S(1)}, bf16[192,3072]{1,0:T(8,128)(2,1)S(1)}, u32[]{:S(2)}, u32[]{:S(2)}) %collective-permute-start.41) | collective-permute-done | bytes 1179680 | tf_op jit(solution)/shard_map/ppermute | solution.py:277
  439.0 10.6 %collective-permute-done.42 = bf16[96,3072]{1,0:T(8,128)(2,1)S(1)} collective-permute-done((bf16[96,3072]{1,0:T(8,128)(2,1)S(1)}, bf16[96,3072]{1,0:T(8,128)(2,1)S(1)}, u32[]{:S(2)}, u32[]{:S(2)}) %collective-permute-start.42) | collective-permute-done | bytes 589856 | tf_op jit(solution)/shard_map/ppermute | solution.py:277
  453.0 8.4 %collective-permute-done.43 = bf16[48,3072]{1,0:T(8,128)(2,1)S(1)} collective-permute-done((bf16[48,3072]{1,0:T(8,128)(2,1)S(1)}, bf16[48,3072]{1,0:T(8,128)(2,1)S(1)}, u32[]{:S(2)}, u32[]{:S(2)}) %collective-permute-start.43) | collective-permute-done | bytes 294944 | tf_op jit(solution)/shard_map/ppermute | solution.py:277
  465.1 2.9 collective-permute-start.54
  468.0 7.6 %collective-permute-done.44 = bf16[24,3072]{1,0:T(8,128)(2,1)S(1)} collective-permute-done((bf16[24,3072]{1,0:T(8,128)(2,1)S(1)}, bf16[24,3072]{1,0:T(8,128)(2,1)S(1)}, u32[]{:S(2)}, u32[]{:S(2)}) %collective-permute-start.44) | collective-permute-done | bytes 147488 | tf_op jit(solution)/shard_map/ppermute | solution.py:277
  475.6 3.0 collective-permute-done.54
  478.8 6.3 collective-permute-done.45
  489.4 5.7 collective-permute-done.46
  498.9 3.2 collective-permute-start.57
  502.1 3.3 collective-permute-done.47
  505.7 3.3 collective-permute-start.48
  509.0 10.5 %collective-permute-done.28 = bf16[384,1152]{1,0:T(8,128)(2,1)S(1)} collective-permute-done((bf16[384,1152]{1,0:T(8,128)(2,1)S(1)}, bf16[384,1152]{1,0:T(8,128)(2,1)S(1)}, u32[]{:S(2)}, u32[]{:S(2)}) %collective-permute-start.28) | collective-permute-done | bytes 884768 | tf_op jit(solution)/shard_map/ppermute | solution.py:277
  521.2 11.0 %collective-permute-done.57 = bf16[384,768]{1,0:T(8,128)(2,1)S(1)} collective-permute-done((bf16[384,768]{1,0:T(8,128)(2,1)S(1)}, bf16[384,768]{1,0:T(8,128)(2,1)S(1)}, u32[]{:S(2)}, u32[]{:S(2)}) %collective-permute-start.57) | collective-permute-done | bytes 589856 | tf_op jit(solution)/shard_map/ppermute | solution.py:277
  535.1 16.2 %collective-permute-done.48 = bf16[192,3072]{1,0:T(8,128)(2,1)S(1)} collective-permute-done((bf16[192,3072]{1,0:T(8,128)(2,1)S(1)}, bf16[192,3072]{1,0:T(8,128)(2,1)S(1)}, u32[]{:S(2)}, u32[]{:S(2)}) %collective-permute-start.48) | collective-permute-done | bytes 1179680 | tf_op jit(solution)/shard_map/ppermute | solution.py:277
  554.9 3.4 add_convert_fusion.2
  559.7 3.0 collective-permute-start.15
  564.4 3.2 collective-permute-done.20
  584.3 3.9 copy.125
  588.1 3.9 copy.126
  592.0 5.1 fusion.23
  597.1 3.8 copy.127
  600.9 3.8 copy.128
  604.7 5.4 maximum_convert_fusion.2
  610.2 8.0 %copy.129 = f32[768,3,2,384]{0,3,2,1:T(8,128)} copy(f32[768,3,2,384]{3,0,2,1:T(8,128)} %maximum_convert_fusion.2) | data formatting | bytes 14155776 | tf_op jit(solution)/shard_map/convert_element_type | solution.py:462
  618.2 8.1 %copy.130 = f32[768,2304]{1,0:T(8,128)} copy(f32[768,2304]{0,1:T(8,128)} %bitcast.250) | data formatting | bytes 14155776
  626.3 2.8 broadcast_select_fusion.3
  629.1 5.0 maximum_convert_fusion
  636.6 4.5 maximum_convert_fusion.1
  (439 shorter events, 177.4 us)
Async XLA Ops:
  0.6 144.6 %copy-start = (bf16[768,768]{1,0:T(8,128)(2,1)S(1)}, bf16[768,768]{1,0:T(8,128)(2,1)}, u32[]{:S(2)}) copy-start(bf16[768,768]{1,0:T(8,128)(2,1)} %param.30) | copy-start | bytes 3538948
  3.4 128.3 %collective-permute-start.8 = (bf16[256,768]{1,0:T(8,128)(2,1)}, bf16[256,768]{1,0:T(8,128)(2,1)}, u32[]{:S(2)}, u32[]{:S(2)}) collective-permute-start(bf16[256,768]{1,0:T(8,128)(2,1)} %get-tuple-element.100), channel_id=1, source_target_pairs={{0,2},{1,3},{2,0},{3,1},{4,6},{5,7},{6,4},{7,5},{8,10},{9,11},{10,... | collective-permute-start | bytes 1179656 | tf_op jit(solution)/shard_map/ppermute | solution.py:277
  6.4 40.2 %copy-start.67 = (bf16[768]{0:T(1024)(128)(2,1)S(1)}, bf16[768]{0:T(1024)(128)(2,1)}, u32[]{:S(2)}) copy-start(bf16[768]{0:T(1024)(128)(2,1)} %param.32) | copy-start | bytes 4612
  6.4 125.4 %collective-permute-start.10 = (bf16[256,768]{1,0:T(8,128)(2,1)}, bf16[256,768]{1,0:T(8,128)(2,1)}, u32[]{:S(2)}, u32[]{:S(2)}) collective-permute-start(bf16[256,768]{1,0:T(8,128)(2,1)} %get-tuple-element.101), channel_id=1, source_target_pairs={{0,6},{1,7},{2,4},{3,5},{4,2},{5,3},{6,0},{7,1},{8,14},{9,15},{10,... | collective-permute-start | bytes 1179656 | tf_op jit(solution)/shard_map/ppermute | solution.py:277
  9.0 24.4 %collective-permute-start = (bf16[256,768]{1,0:T(8,128)(2,1)}, bf16[256,768]{1,0:T(8,128)(2,1)S(1)}, u32[]{:S(2)}, u32[]{:S(2)}) collective-permute-start(bf16[256,768]{1,0:T(8,128)(2,1)} %get-tuple-element.109), channel_id=1, source_target_pairs={{0,2},{1,3},{2,0},{3,1},{4,6},{5,7},{6,4},{7,5},{8,10},{9,11},{10,... | collective-permute-start | bytes 1179656 | tf_op jit(solution)/shard_map/ppermute | solution.py:277
  10.5 31.8 %collective-permute-start.2 = (bf16[256,768]{1,0:T(8,128)(2,1)}, bf16[256,768]{1,0:T(8,128)(2,1)S(1)}, u32[]{:S(2)}, u32[]{:S(2)}) collective-permute-start(bf16[256,768]{1,0:T(8,128)(2,1)} %get-tuple-element.110), channel_id=1, source_target_pairs={{0,6},{1,7},{2,4},{3,5},{4,2},{5,3},{6,0},{7,1},{8,14},{9,15},{10,... | collective-permute-start | bytes 1179656 | tf_op jit(solution)/shard_map/ppermute | solution.py:277
  10.5 31.8 %collective-permute-start.1 = (bf16[256,768]{1,0:T(8,128)(2,1)}, bf16[256,768]{1,0:T(8,128)(2,1)S(1)}, u32[]{:S(2)}, u32[]{:S(2)}) collective-permute-start(bf16[256,768]{1,0:T(8,128)(2,1)} %get-tuple-element.111), channel_id=1, source_target_pairs={{0,4},{1,5},{2,6},{3,7},{4,0},{5,1},{6,2},{7,3},{8,12},{9,13},{10,... | collective-permute-start | bytes 1179656 | tf_op jit(solution)/shard_map/ppermute | solution.py:277
  33.4 98.3 %collective-permute-start.9 = (bf16[256,768]{1,0:T(8,128)(2,1)}, bf16[256,768]{1,0:T(8,128)(2,1)}, u32[]{:S(2)}, u32[]{:S(2)}) collective-permute-start(bf16[256,768]{1,0:T(8,128)(2,1)} %get-tuple-element.102), channel_id=1, source_target_pairs={{0,4},{1,5},{2,6},{3,7},{4,0},{5,1},{6,2},{7,3},{8,12},{9,13},{10,... | collective-permute-start | bytes 1179656 | tf_op jit(solution)/shard_map/ppermute | solution.py:277
  44.5 19.4 %collective-permute-start.3 = (bf16[4,256,768]{2,1,0:T(8,128)(2,1)S(1)}, bf16[4,256,768]{2,1,0:T(8,128)(2,1)}, u32[]{:S(2)}, u32[]{:S(2)}) collective-permute-start(bf16[4,256,768]{2,1,0:T(8,128)(2,1)S(1)} %get-tuple-element.69), channel_id=1, source_target_pairs={{0,1},{1,0},{2,3},{3,2},{4,5},{5,4},{6,7},{7,6},{8,9},{9,8},{10,11... | collective-permute-start | bytes 4718600 | tf_op jit(solution)/shard_map/ppermute | solution.py:277
  131.3 15.1 %collective-permute-start.4 = (bf16[4,256,384]{2,1,0:T(8,128)(2,1)}, bf16[4,256,384]{2,1,0:T(8,128)(2,1)}, u32[]{:S(2)}, u32[]{:S(2)}) collective-permute-start(bf16[4,256,384]{2,1,0:T(8,128)(2,1)} %get-tuple-element.107), channel_id=1, source_target_pairs={{0,1},{1,0},{2,3},{3,2},{4,5},{5,4},{6,7},{7,6},{8,9},{9,8},{10,11... | collective-permute-start | bytes 2359304 | tf_op jit(solution)/shard_map/ppermute | solution.py:277
  149.9 54.7 %copy-start.2 = (f32[1024,768]{0,1:T(8,128)}, f32[1024,768]{0,1:T(8,128)S(1)}, u32[]{:S(2)}) copy-start(f32[1024,768]{0,1:T(8,128)S(1)} %get-tuple-element.167) | copy-start | bytes 9437188
  168.5 53.3 %copy-start.28 = (bf16[3072,768]{1,0:T(8,128)(2,1)}, bf16[3072,768]{1,0:T(8,128)(2,1)S(1)}, u32[]{:S(2)}) copy-start(bf16[3072,768]{1,0:T(8,128)(2,1)S(1)} %convolution_convert_fusion) | copy-start | bytes 14155780
  218.1 28.6 %collective-permute-start.7 = (bf16[256,768]{0,1:T(8,128)(2,1)}, bf16[256,768]{0,1:T(8,128)(2,1)}, u32[]{:S(2)}, u32[]{:S(2)}) collective-permute-start(bf16[256,768]{0,1:T(8,128)(2,1)} %get-tuple-element.103), channel_id=1, source_target_pairs={{0,6},{1,7},{2,4},{3,5},{4,2},{5,3},{6,0},{7,1},{8,14},{9,15},{10,... | collective-permute-start | bytes 1179656 | tf_op jit(solution)/shard_map/ppermute | solution.py:277
  221.2 26.7 %collective-permute-start.6 = (bf16[256,768]{0,1:T(8,128)(2,1)}, bf16[256,768]{0,1:T(8,128)(2,1)}, u32[]{:S(2)}, u32[]{:S(2)}) collective-permute-start(bf16[256,768]{0,1:T(8,128)(2,1)} %get-tuple-element.104), channel_id=1, source_target_pairs={{0,4},{1,5},{2,6},{3,7},{4,0},{5,1},{6,2},{7,3},{8,12},{9,13},{10,... | collective-permute-start | bytes 1179656 | tf_op jit(solution)/shard_map/ppermute | solution.py:277
  221.3 28.5 %collective-permute-start.5 = (bf16[256,768]{0,1:T(8,128)(2,1)}, bf16[256,768]{0,1:T(8,128)(2,1)}, u32[]{:S(2)}, u32[]{:S(2)}) collective-permute-start(bf16[256,768]{0,1:T(8,128)(2,1)} %get-tuple-element.105), channel_id=1, source_target_pairs={{0,2},{1,3},{2,0},{3,1},{4,6},{5,7},{6,4},{7,5},{8,10},{9,11},{10,... | collective-permute-start | bytes 1179656 | tf_op jit(solution)/shard_map/ppermute | solution.py:277
  242.0 11.3 %collective-permute-start.30 = (bf16[384,768]{1,0:T(8,128)(2,1)}, bf16[384,768]{1,0:T(8,128)(2,1)}, u32[]{:S(2)}, u32[]{:S(2)}) collective-permute-start(bf16[384,768]{1,0:T(8,128)(2,1)} %dynamic-slice_bitcast_fusion.7), channel_id=1, source_target_pairs={{0,1},{1,0},{2,3},{3,2},{4,5},{5,4},{6,7},{7,6},{8,9},{9,8},{10,11... | collective-permute-start | bytes 1769480 | tf_op jit(solution)/shard_map/ppermute | solution.py:277
  244.2 12.1 %collective-permute-start.11 = (bf16[1024,384]{1,0:T(8,128)(2,1)}, bf16[1024,384]{1,0:T(8,128)(2,1)}, u32[]{:S(2)}, u32[]{:S(2)}) collective-permute-start(bf16[1024,384]{1,0:T(8,128)(2,1)} %convolution_convert_fusion.2), channel_id=1, source_target_pairs={{0,1},{1,0},{2,3},{3,2},{4,5},{5,4},{6,7},{7,6},{8,9},{9,8},{10,11... | collective-permute-start | bytes 2359304 | tf_op jit(solution)/shard_map/ppermute | solution.py:277
  246.8 145.5 %collective-permute-start.50 = (bf16[1536,768]{1,0:T(8,128)(2,1)}, bf16[1536,768]{1,0:T(8,128)(2,1)}, u32[]{:S(2)}, u32[]{:S(2)}) collective-permute-start(bf16[1536,768]{1,0:T(8,128)(2,1)} %dynamic-slice_bitcast_fusion), channel_id=1, source_target_pairs={{0,1},{1,0},{2,3},{3,2},{4,5},{5,4},{6,7},{7,6},{8,9},{9,8},{10,11... | collective-permute-start | bytes 7077896 | tf_op jit(solution)/shard_map/ppermute | solution.py:277
  248.0 155.2 %collective-permute-start.40 = (bf16[384,3072]{1,0:T(8,128)(2,1)}, bf16[384,3072]{1,0:T(8,128)(2,1)}, u32[]{:S(2)}, u32[]{:S(2)}) collective-permute-start(bf16[384,3072]{1,0:T(8,128)(2,1)} %dynamic-slice_bitcast_fusion.1), channel_id=1, source_target_pairs={{0,1},{1,0},{2,3},{3,2},{4,5},{5,4},{6,7},{7,6},{8,9},{9,8},{10,11... | collective-permute-start | bytes 7077896 | tf_op jit(solution)/shard_map/ppermute | solution.py:277
  254.7 62.3 %collective-permute-start.31 = (bf16[192,768]{1,0:T(8,128)(2,1)S(1)}, bf16[192,768]{1,0:T(8,128)(2,1)S(1)}, u32[]{:S(2)}, u32[]{:S(2)}) collective-permute-start(bf16[192,768]{1,0:T(8,128)(2,1)S(1)} %dynamic-slice_bitcast_fusion.17), channel_id=1, source_target_pairs={{0,2},{1,3},{2,0},{3,1},{4,6},{5,7},{6,4},{7,5},{8,10},{9,11},{10,... | collective-permute-start | bytes 884744 | tf_op jit(solution)/shard_map/ppermute | solution.py:277
  317.1 5.6 collective-permute-start.32
  322.7 4.4 collective-permute-start.33
  327.2 11.1 %collective-permute-start.34 = (bf16[24,768]{1,0:T(8,128)(2,1)S(1)}, bf16[24,768]{1,0:T(8,128)(2,1)S(1)}, u32[]{:S(2)}, u32[]{:S(2)}) collective-permute-start(bf16[24,768]{1,0:T(8,128)(2,1)S(1)} %dynamic-slice_bitcast_fusion.24), channel_id=1, source_target_pairs={{0,16},{8,24},{16,0},{24,8},{1,17},{9,25},{17,1},{25,9},{2,18},{10... | collective-permute-start | bytes 110600 | tf_op jit(solution)/shard_map/ppermute | solution.py:277
  338.3 4.9 collective-permute-start.35
  343.2 4.4 collective-permute-start.36
  345.4 24.3 %collective-permute-start.21 = (bf16[384,1152]{1,0:T(8,128)(2,1)S(1)}, bf16[384,1152]{1,0:T(8,128)(2,1)S(1)}, u32[]{:S(2)}, u32[]{:S(2)}) collective-permute-start(bf16[384,1152]{1,0:T(8,128)(2,1)S(1)} %dynamic-slice_bitcast_fusion.4), channel_id=1, source_target_pairs={{0,4},{1,5},{2,6},{3,7},{4,0},{5,1},{6,2},{7,3},{8,12},{9,13},{10,... | collective-permute-start | bytes 2654216 | tf_op jit(solution)/shard_map/ppermute | solution.py:277
  347.7 19.4 %collective-permute-start.37 = (bf16[96,768]{1,0:T(8,128)(2,1)S(1)}, bf16[96,768]{1,0:T(8,128)(2,1)S(1)}, u32[]{:S(2)}, u32[]{:S(2)}) collective-permute-start(bf16[96,768]{1,0:T(8,128)(2,1)S(1)} %pad_maximum_fusion.20), channel_id=1, source_target_pairs={{0,4},{1,5},{2,6},{3,7},{4,0},{5,1},{6,2},{7,3},{8,12},{9,13},{10,... | collective-permute-start | bytes 442376 | tf_op jit(solution)/shard_map/ppermute | solution.py:277
  367.2 10.4 %collective-permute-start.38 = (bf16[192,768]{1,0:T(8,128)(2,1)S(1)}, bf16[192,768]{1,0:T(8,128)(2,1)}, u32[]{:S(2)}, u32[]{:S(2)}) collective-permute-start(bf16[192,768]{1,0:T(8,128)(2,1)S(1)} %pad_maximum_fusion.16), channel_id=1, source_target_pairs={{0,2},{1,3},{2,0},{3,1},{4,6},{5,7},{6,4},{7,5},{8,10},{9,11},{10,... | collective-permute-start | bytes 884744 | tf_op jit(solution)/shard_map/ppermute | solution.py:277
  370.7 12.0 %collective-permute-start.22 = (bf16[192,1152]{1,0:T(8,128)(2,1)}, bf16[192,1152]{1,0:T(8,128)(2,1)S(1)}, u32[]{:S(2)}, u32[]{:S(2)}) collective-permute-start(bf16[192,1152]{1,0:T(8,128)(2,1)} %dynamic-slice_bitcast_fusion.8), channel_id=1, source_target_pairs={{0,2},{1,3},{2,0},{3,1},{4,6},{5,7},{6,4},{7,5},{8,10},{9,11},{10,... | collective-permute-start | bytes 1327112 | tf_op jit(solution)/shard_map/ppermute | solution.py:277
  372.5 24.8 %collective-permute-start.12 = (bf16[1024,768]{0,1:T(8,128)(2,1)}, bf16[1024,768]{0,1:T(8,128)(2,1)}, u32[]{:S(2)}, u32[]{:S(2)}) collective-permute-start(bf16[1024,768]{0,1:T(8,128)(2,1)} %slice.228), channel_id=1, source_target_pairs={{0,1},{1,0},{2,3},{3,2},{4,5},{5,4},{6,7},{7,6},{8,9},{9,8},{10,11... | collective-permute-start | bytes 4718600 | tf_op jit(solution)/shard_map/ppermute | solution.py:277
  378.8 4.8 collective-permute-start.39
  382.9 6.1 collective-permute-start.23
  389.1 16.7 %collective-permute-start.24 = (bf16[48,1152]{1,0:T(8,128)(2,1)S(1)}, bf16[48,1152]{1,0:T(8,128)(2,1)S(1)}, u32[]{:S(2)}, u32[]{:S(2)}) collective-permute-start(bf16[48,1152]{1,0:T(8,128)(2,1)S(1)} %dynamic-slice_bitcast_fusion.22), channel_id=1, source_target_pairs={{0,16},{8,24},{16,0},{24,8},{1,17},{9,25},{17,1},{25,9},{2,18},{10... | collective-permute-start | bytes 331784 | tf_op jit(solution)/shard_map/ppermute | solution.py:277
  395.3 41.8 %collective-permute-start.51 = (bf16[768,768]{1,0:T(8,128)(2,1)S(1)}, bf16[768,768]{1,0:T(8,128)(2,1)S(1)}, u32[]{:S(2)}, u32[]{:S(2)}) collective-permute-start(bf16[768,768]{1,0:T(8,128)(2,1)S(1)} %dynamic-slice_bitcast_fusion.2), channel_id=1, source_target_pairs={{0,2},{1,3},{2,0},{3,1},{4,6},{5,7},{6,4},{7,5},{8,10},{9,11},{10,... | collective-permute-start | bytes 3538952 | tf_op jit(solution)/shard_map/ppermute | solution.py:277
  403.1 4.6 collective-permute-start.16
  405.8 8.8 %collective-permute-start.25 = (bf16[48,1152]{1,0:T(8,128)(2,1)S(1)}, bf16[48,1152]{1,0:T(8,128)(2,1)S(1)}, u32[]{:S(2)}, u32[]{:S(2)}) collective-permute-start(bf16[48,1152]{1,0:T(8,128)(2,1)S(1)} %fusion.59), channel_id=1, source_target_pairs={{0,16},{8,24},{16,0},{24,8},{1,17},{9,25},{17,1},{25,9},{2,18},{10... | collective-permute-start | bytes 331784 | tf_op jit(solution)/shard_map/ppermute | solution.py:277
  406.2 28.7 %collective-permute-start.41 = (bf16[192,3072]{1,0:T(8,128)(2,1)S(1)}, bf16[192,3072]{1,0:T(8,128)(2,1)S(1)}, u32[]{:S(2)}, u32[]{:S(2)}) collective-permute-start(bf16[192,3072]{1,0:T(8,128)(2,1)S(1)} %dynamic-slice_bitcast_fusion.3), channel_id=1, source_target_pairs={{0,4},{1,5},{2,6},{3,7},{4,0},{5,1},{6,2},{7,3},{8,12},{9,13},{10,... | collective-permute-start | bytes 3538952 | tf_op jit(solution)/shard_map/ppermute | solution.py:277
  407.7 11.6 %collective-permute-start.17 = (f32[9216]{0:T(1024)S(1)}, f32[9216]{0:T(1024)S(1)}, u32[]{:S(2)}, u32[]{:S(2)}) collective-permute-start(f32[9216]{0:T(1024)S(1)} %add.550), channel_id=1, source_target_pairs={{0,2},{1,3},{2,0},{3,1},{4,6},{5,7},{6,4},{7,5},{8,10},{9,11},{10,... | collective-permute-start | bytes 110600 | tf_op jit(solution)/shard_map/ppermute | solution.py:277
  414.7 7.0 %collective-permute-start.26 = (bf16[96,1152]{1,0:T(8,128)(2,1)S(1)}, bf16[96,1152]{1,0:T(8,128)(2,1)S(1)}, u32[]{:S(2)}, u32[]{:S(2)}) collective-permute-start(bf16[96,1152]{1,0:T(8,128)(2,1)S(1)} %pad_maximum_fusion.19), channel_id=1, source_target_pairs={{0,8},{8,0},{16,24},{24,16},{1,9},{9,1},{17,25},{25,17},{2,10},{10... | collective-permute-start | bytes 663560 | tf_op jit(solution)/shard_map/ppermute | solution.py:277
  419.3 139.0 %collective-permute-start.18 = (f32[9216]{0:T(1024)S(1)}, f32[9216]{0:T(1024)S(1)}, u32[]{:S(2)}, u32[]{:S(2)}) collective-permute-start(f32[9216]{0:T(1024)S(1)} %add.551), channel_id=1, source_target_pairs={{0,4},{1,5},{2,6},{3,7},{4,0},{5,1},{6,2},{7,3},{8,12},{9,13},{10,... | collective-permute-start | bytes 110600 | tf_op jit(solution)/shard_map/ppermute | solution.py:277
  421.8 15.1 %collective-permute-start.27 = (bf16[192,1152]{1,0:T(8,128)(2,1)S(1)}, bf16[192,1152]{1,0:T(8,128)(2,1)S(1)}, u32[]{:S(2)}, u32[]{:S(2)}) collective-permute-start(bf16[192,1152]{1,0:T(8,128)(2,1)S(1)} %pad_maximum_fusion.15), channel_id=1, source_target_pairs={{0,2},{1,3},{2,0},{3,1},{4,6},{5,7},{6,4},{7,5},{8,10},{9,11},{10,... | collective-permute-start | bytes 1327112 | tf_op jit(solution)/shard_map/ppermute | solution.py:277
  435.3 14.4 %collective-permute-start.42 = (bf16[96,3072]{1,0:T(8,128)(2,1)S(1)}, bf16[96,3072]{1,0:T(8,128)(2,1)S(1)}, u32[]{:S(2)}, u32[]{:S(2)}) collective-permute-start(bf16[96,3072]{1,0:T(8,128)(2,1)S(1)} %dynamic-slice_bitcast_fusion.6), channel_id=1, source_target_pairs={{0,2},{1,3},{2,0},{3,1},{4,6},{5,7},{6,4},{7,5},{8,10},{9,11},{10,... | collective-permute-start | bytes 1769480 | tf_op jit(solution)/shard_map/ppermute | solution.py:277
  437.5 14.0 %collective-permute-start.52 = (bf16[384,768]{1,0:T(8,128)(2,1)S(1)}, bf16[384,768]{1,0:T(8,128)(2,1)S(1)}, u32[]{:S(2)}, u32[]{:S(2)}) collective-permute-start(bf16[384,768]{1,0:T(8,128)(2,1)S(1)} %dynamic-slice_bitcast_fusion.5), channel_id=1, source_target_pairs={{0,4},{1,5},{2,6},{3,7},{4,0},{5,1},{6,2},{7,3},{8,12},{9,13},{10,... | collective-permute-start | bytes 1769480 | tf_op jit(solution)/shard_map/ppermute | solution.py:277
  449.9 11.5 %collective-permute-start.43 = (bf16[48,3072]{1,0:T(8,128)(2,1)S(1)}, bf16[48,3072]{1,0:T(8,128)(2,1)S(1)}, u32[]{:S(2)}, u32[]{:S(2)}) collective-permute-start(bf16[48,3072]{1,0:T(8,128)(2,1)S(1)} %dynamic-slice_bitcast_fusion.16), channel_id=1, source_target_pairs={{0,8},{8,0},{16,24},{24,16},{1,9},{9,1},{17,25},{25,17},{2,10},{10... | collective-permute-start | bytes 884744 | tf_op jit(solution)/shard_map/ppermute | solution.py:277
  451.7 13.3 %collective-permute-start.53 = (bf16[192,768]{1,0:T(8,128)(2,1)S(1)}, bf16[192,768]{1,0:T(8,128)(2,1)S(1)}, u32[]{:S(2)}, u32[]{:S(2)}) collective-permute-start(bf16[192,768]{1,0:T(8,128)(2,1)S(1)} %dynamic-slice_bitcast_fusion.15), channel_id=1, source_target_pairs={{0,8},{8,0},{16,24},{24,16},{1,9},{9,1},{17,25},{25,17},{2,10},{10... | collective-permute-start | bytes 884744 | tf_op jit(solution)/shard_map/ppermute | solution.py:277
  461.5 14.0 %collective-permute-start.44 = (bf16[24,3072]{1,0:T(8,128)(2,1)S(1)}, bf16[24,3072]{1,0:T(8,128)(2,1)S(1)}, u32[]{:S(2)}, u32[]{:S(2)}) collective-permute-start(bf16[24,3072]{1,0:T(8,128)(2,1)S(1)} %dynamic-slice_bitcast_fusion.20), channel_id=1, source_target_pairs={{0,16},{8,24},{16,0},{24,8},{1,17},{9,25},{17,1},{25,9},{2,18},{10... | collective-permute-start | bytes 442376 | tf_op jit(solution)/shard_map/ppermute | solution.py:277
  465.1 13.6 %collective-permute-start.54 = (bf16[96,768]{1,0:T(8,128)(2,1)S(1)}, bf16[96,768]{1,0:T(8,128)(2,1)S(1)}, u32[]{:S(2)}, u32[]{:S(2)}) collective-permute-start(bf16[96,768]{1,0:T(8,128)(2,1)S(1)} %dynamic-slice_bitcast_fusion.19), channel_id=1, source_target_pairs={{0,16},{8,24},{16,0},{24,8},{1,17},{9,25},{17,1},{25,9},{2,18},{10... | collective-permute-start | bytes 442376 | tf_op jit(solution)/shard_map/ppermute | solution.py:277
  475.6 9.5 %collective-permute-start.45 = (bf16[24,3072]{1,0:T(8,128)(2,1)S(1)}, bf16[24,3072]{1,0:T(8,128)(2,1)S(1)}, u32[]{:S(2)}, u32[]{:S(2)}) collective-permute-start(bf16[24,3072]{1,0:T(8,128)(2,1)S(1)} %fusion.57), channel_id=1, source_target_pairs={{0,16},{8,24},{16,0},{24,8},{1,17},{9,25},{17,1},{25,9},{2,18},{10... | collective-permute-start | bytes 442376 | tf_op jit(solution)/shard_map/ppermute | solution.py:277
  478.7 8.9 %collective-permute-start.55 = (bf16[96,768]{1,0:T(8,128)(2,1)S(1)}, bf16[96,768]{1,0:T(8,128)(2,1)S(1)}, u32[]{:S(2)}, u32[]{:S(2)}) collective-permute-start(bf16[96,768]{1,0:T(8,128)(2,1)S(1)} %fusion.56), channel_id=1, source_target_pairs={{0,16},{8,24},{16,0},{24,8},{1,17},{9,25},{17,1},{25,9},{2,18},{10... | collective-permute-start | bytes 442376 | tf_op jit(solution)/shard_map/ppermute | solution.py:277
  485.1 9.9 %collective-permute-start.46 = (bf16[48,3072]{1,0:T(8,128)(2,1)S(1)}, bf16[48,3072]{1,0:T(8,128)(2,1)S(1)}, u32[]{:S(2)}, u32[]{:S(2)}) collective-permute-start(bf16[48,3072]{1,0:T(8,128)(2,1)S(1)} %pad_maximum_fusion.17), channel_id=1, source_target_pairs={{0,8},{8,0},{16,24},{24,16},{1,9},{9,1},{17,25},{25,17},{2,10},{10... | collective-permute-start | bytes 884744 | tf_op jit(solution)/shard_map/ppermute | solution.py:277
  487.7 11.1 %collective-permute-start.56 = (bf16[192,768]{1,0:T(8,128)(2,1)S(1)}, bf16[192,768]{1,0:T(8,128)(2,1)S(1)}, u32[]{:S(2)}, u32[]{:S(2)}) collective-permute-start(bf16[192,768]{1,0:T(8,128)(2,1)S(1)} %pad_maximum_fusion.18), channel_id=1, source_target_pairs={{0,8},{8,0},{16,24},{24,16},{1,9},{9,1},{17,25},{25,17},{2,10},{10... | collective-permute-start | bytes 884744 | tf_op jit(solution)/shard_map/ppermute | solution.py:277
  495.2 10.2 %collective-permute-start.47 = (bf16[96,3072]{1,0:T(8,128)(2,1)S(1)}, bf16[96,3072]{1,0:T(8,128)(2,1)S(1)}, u32[]{:S(2)}, u32[]{:S(2)}) collective-permute-start(bf16[96,3072]{1,0:T(8,128)(2,1)S(1)} %pad_maximum_fusion.13), channel_id=1, source_target_pairs={{0,2},{1,3},{2,0},{3,1},{4,6},{5,7},{6,4},{7,5},{8,10},{9,11},{10,... | collective-permute-start | bytes 1769480 | tf_op jit(solution)/shard_map/ppermute | solution.py:277
  496.9 22.6 %collective-permute-start.28 = (bf16[384,1152]{1,0:T(8,128)(2,1)S(1)}, bf16[384,1152]{1,0:T(8,128)(2,1)S(1)}, u32[]{:S(2)}, u32[]{:S(2)}) collective-permute-start(bf16[384,1152]{1,0:T(8,128)(2,1)S(1)} %pad_maximum_fusion.9), channel_id=1, source_target_pairs={{0,4},{1,5},{2,6},{3,7},{4,0},{5,1},{6,2},{7,3},{8,12},{9,13},{10,... | collective-permute-start | bytes 2654216 | tf_op jit(solution)/shard_map/ppermute | solution.py:277
  498.9 33.2 %collective-permute-start.57 = (bf16[384,768]{1,0:T(8,128)(2,1)S(1)}, bf16[384,768]{1,0:T(8,128)(2,1)S(1)}, u32[]{:S(2)}, u32[]{:S(2)}) collective-permute-start(bf16[384,768]{1,0:T(8,128)(2,1)S(1)} %pad_maximum_fusion.14), channel_id=1, source_target_pairs={{0,4},{1,5},{2,6},{3,7},{4,0},{5,1},{6,2},{7,3},{8,12},{9,13},{10,... | collective-permute-start | bytes 1769480 | tf_op jit(solution)/shard_map/ppermute | solution.py:277
  505.7 45.5 %collective-permute-start.48 = (bf16[192,3072]{1,0:T(8,128)(2,1)S(1)}, bf16[192,3072]{1,0:T(8,128)(2,1)S(1)}, u32[]{:S(2)}, u32[]{:S(2)}) collective-permute-start(bf16[192,3072]{1,0:T(8,128)(2,1)S(1)} %pad_maximum_fusion.7), channel_id=1, source_target_pairs={{0,4},{1,5},{2,6},{3,7},{4,0},{5,1},{6,2},{7,3},{8,12},{9,13},{10,... | collective-permute-start | bytes 3538952 | tf_op jit(solution)/shard_map/ppermute | solution.py:277
  521.2 67.0 %collective-permute-start.29 = (bf16[768,1152]{1,0:T(8,128)(2,1)}, bf16[768,1152]{1,0:T(8,128)(2,1)}, u32[]{:S(2)}, u32[]{:S(2)}) collective-permute-start(bf16[768,1152]{1,0:T(8,128)(2,1)} %pad_maximum_fusion.3), channel_id=1, source_target_pairs={{0,1},{1,0},{2,3},{3,2},{4,5},{5,4},{6,7},{7,6},{8,9},{9,8},{10,11... | collective-permute-start | bytes 5308424 | tf_op jit(solution)/shard_map/ppermute | solution.py:277
  533.6 35.4 %collective-permute-start.58 = (bf16[768,768]{1,0:T(8,128)(2,1)}, bf16[768,768]{1,0:T(8,128)(2,1)}, u32[]{:S(2)}, u32[]{:S(2)}) collective-permute-start(bf16[768,768]{1,0:T(8,128)(2,1)} %pad_maximum_fusion.8), channel_id=1, source_target_pairs={{0,2},{1,3},{2,0},{3,1},{4,6},{5,7},{6,4},{7,5},{8,10},{9,11},{10,... | collective-permute-start | bytes 3538952 | tf_op jit(solution)/shard_map/ppermute | solution.py:277
  553.3 73.0 %collective-permute-start.49 = (bf16[384,3072]{1,0:T(8,128)(2,1)}, bf16[384,3072]{1,0:T(8,128)(2,1)}, u32[]{:S(2)}, u32[]{:S(2)}) collective-permute-start(bf16[384,3072]{1,0:T(8,128)(2,1)} %pad_maximum_fusion), channel_id=1, source_target_pairs={{0,1},{1,0},{2,3},{3,2},{4,5},{5,4},{6,7},{7,6},{8,9},{9,8},{10,11... | collective-permute-start | bytes 7077896 | tf_op jit(solution)/shard_map/ppermute | solution.py:277
  558.4 4.3 collective-permute-start.19
  559.7 15.4 %collective-permute-start.15 = (bf16[256,768]{0,1:T(8,128)(2,1)}, bf16[256,768]{0,1:T(8,128)(2,1)S(1)}, u32[]{:S(2)}, u32[]{:S(2)}) collective-permute-start(bf16[256,768]{0,1:T(8,128)(2,1)} %get-tuple-element.95), channel_id=1, source_target_pairs={{0,6},{1,7},{2,4},{3,5},{4,2},{5,3},{6,0},{7,1},{8,14},{9,15},{10,... | collective-permute-start | bytes 1179656 | tf_op jit(solution)/shard_map/ppermute | solution.py:277
  562.7 4.9 collective-permute-start.20
  567.6 12.0 %collective-permute-start.14 = (bf16[256,768]{0,1:T(8,128)(2,1)}, bf16[256,768]{0,1:T(8,128)(2,1)}, u32[]{:S(2)}, u32[]{:S(2)}) collective-permute-start(bf16[256,768]{0,1:T(8,128)(2,1)} %get-tuple-element.96), channel_id=1, source_target_pairs={{0,4},{1,5},{2,6},{3,7},{4,0},{5,1},{6,2},{7,3},{8,12},{9,13},{10,... | collective-permute-start | bytes 1179656 | tf_op jit(solution)/shard_map/ppermute | solution.py:277
  569.0 11.8 %collective-permute-start.13 = (bf16[256,768]{0,1:T(8,128)(2,1)}, bf16[256,768]{0,1:T(8,128)(2,1)}, u32[]{:S(2)}, u32[]{:S(2)}) collective-permute-start(bf16[256,768]{0,1:T(8,128)(2,1)} %get-tuple-element.97), channel_id=1, source_target_pairs={{0,2},{1,3},{2,0},{3,1},{4,6},{5,7},{6,4},{7,5},{8,10},{9,11},{10,... | collective-permute-start | bytes 1179656 | tf_op jit(solution)/shard_map/ppermute | solution.py:277
  575.1 59.0 %collective-permute-start.59 = (bf16[1536,768]{1,0:T(8,128)(2,1)}, bf16[1536,768]{1,0:T(8,128)(2,1)}, u32[]{:S(2)}, u32[]{:S(2)}) collective-permute-start(bf16[1536,768]{1,0:T(8,128)(2,1)} %pad_maximum_fusion.1), channel_id=1, source_target_pairs={{0,1},{1,0},{2,3},{3,2},{4,5},{5,4},{6,7},{7,6},{8,9},{9,8},{10,11... | collective-permute-start | bytes 7077896 | tf_op jit(solution)/shard_map/ppermute | solution.py:277
  (70 other events, 537.9 us)

commit v2 on v1

--- a/solution.py
+++ b/solution.py
@@ -13,6 +13,7 @@
 GELU_C = 0.7978845608028654
 F32 = jnp.float32
 BF16 = jnp.bfloat16
+VMEM_LIMIT = 60 * 1024 * 1024
 NT = (((1,), (1,)), ((), ()))
 TN = (((0,), (0,)), ((), ()))
 
@@ -130,7 +131,7 @@
             jax.ShapeDtypeStruct((blocks, lse_rows, size), F32),
         ),
         compiler_params=pltpu.CompilerParams(
-            dimension_semantics=("arbitrary",), vmem_limit_bytes=60 * 1024 * 1024
+            dimension_semantics=("arbitrary",), vmem_limit_bytes=VMEM_LIMIT
         ),
         cost_estimate=pl.CostEstimate(
             flops=pairs * 4 * 128, transcendentals=pairs, bytes_accessed=blocks * size * width * 16
@@ -140,11 +141,12 @@
 
 
 def backward_kernel(
-    heads, blocks, phys_ref, flag_ref, query_t_ref, grad_t_ref, out_t_ref, lse_ref, info_ref,
-    key_ref, key_t_ref, value_ref, query_grad_ref, key_grad_ref, value_grad_ref,
+    heads, first, blocks, phys_ref, flag_ref, query_t_ref, grad_t_ref, out_t_ref, lse_ref, info_ref,
+    key_ref, key_t_ref, value_ref, grads_ref,
     bias_sc, query_grad_sc, key_grad_sc, value_grad_sc, query_sc, grad_sc, delta_sc,
 ):
     size = query_t_ref.shape[2]
+    span = heads * HEAD_DIM
     i = pl.program_id(0)
 
     @pl.when(i == 0)
@@ -171,7 +173,7 @@
                 rows = slice(h * HEAD_DIM, (h + 1) * HEAD_DIM)
                 lanes = slice(pair * 128, pair * 128 + width)
                 scores = matmul(key_ref[at, :, lanes], query_sc[h, 0:width, :]) + bias_sc[...]
-                probs = jnp.exp(scores - lse_ref[0, h : h + 1, :])
+                probs = jnp.exp(scores - lse_ref[0, first + h : first + h + 1, :])
                 grad_probs = matmul(value_ref[at, :, lanes], grad_sc[h, 0:width, :])
                 grad_scores = (probs * (grad_probs - delta_sc[h])).astype(BF16)
                 query_grad_sc[rows, :] += matmul(key_t_ref[at, rows, :], grad_scores)
@@ -180,24 +182,27 @@
                 )
                 key_grad_sc[at, rows, :] += matmul(query_t_ref[0, rows, :], grad_scores, NT)
 
-    query_grad_ref[0] = (query_grad_sc[...] * 0.125).T.astype(BF16)
+    grads_ref[phys_ref[i], :, 0:span] = (query_grad_sc[...] * 0.125).T.astype(BF16)
 
     @pl.when(i == blocks - 1)
     def _():
         for block in range(blocks):
-            key_grad_ref[block] = key_grad_sc[block].T.astype(BF16)
-            value_grad_ref[block] = value_grad_sc[block].T.astype(BF16)
-
-
-def attention_backward(phys, flags, query_t, grad_t, out_t, lse, info, key, key_t, value, heads):
-    blocks, width, size = query_t.shape
-    moving_t = pl.BlockSpec((1, width, size), lambda i, p, f: (p[i], 0, 0))
-    moving = pl.BlockSpec((1, size, width), lambda i, p, f: (p[i], 0, 0))
+            grads_ref[block, :, span : 2 * span] = key_grad_sc[block].T.astype(BF16)
+            grads_ref[block, :, 2 * span :] = value_grad_sc[block].T.astype(BF16)
+
+
+def attention_backward(
+    phys, flags, query_t, grad_t, out_t, lse, info, key, key_t, value, heads, first
+):
+    blocks, _, size = query_t.shape
+    span = heads * HEAD_DIM
+    c = first // heads
+    moving_t = pl.BlockSpec((1, span, size), lambda i, p, f: (p[i], c, 0))
     whole = pl.BlockSpec(
-        (blocks, size, width), lambda i, p, f: (0, 0, 0), pipeline_mode=pl.Buffered(1)
+        (blocks, size, span), lambda i, p, f: (0, 0, c), pipeline_mode=pl.Buffered(1)
     )
     whole_t = pl.BlockSpec(
-        (blocks, width, size), lambda i, p, f: (0, 0, 0), pipeline_mode=pl.Buffered(1)
+        (blocks, span, size), lambda i, p, f: (0, c, 0), pipeline_mode=pl.Buffered(1)
     )
     spec = pltpu.PrefetchScalarGridSpec(
         num_scalar_prefetch=2,
@@ -212,31 +217,227 @@
             whole_t,
             whole,
         ],
-        out_specs=[moving, whole, whole],
+        out_specs=pl.BlockSpec(
+            (blocks, size, 3 * span), lambda i, p, f: (0, 0, 0), pipeline_mode=pl.Buffered(1)
+        ),
         scratch_shapes=[
             pltpu.VMEM((size, size), F32),
-            pltpu.VMEM((width, size), F32),
-            pltpu.VMEM((blocks, width, size), F32),
-            pltpu.VMEM((blocks, width, size), F32),
+            pltpu.VMEM((span, size), F32),
+            pltpu.VMEM((blocks, span, size), F32),
+            pltpu.VMEM((blocks, span, size), F32),
             pltpu.VMEM((heads, 128, size), BF16),
             pltpu.VMEM((heads, 128, size), BF16),
             pltpu.VMEM((heads, 1, size), F32),
         ],
     )
-    out = jax.ShapeDtypeStruct((blocks, size, width), BF16)
     pairs = heads * blocks * (blocks + 1) // 2 * size * size
     return pl.pallas_call(
-        functools.partial(backward_kernel, heads, blocks),
+        functools.partial(backward_kernel, heads, first, blocks),
         grid_spec=spec,
-        out_shape=(out, out, out),
+        out_shape=jax.ShapeDtypeStruct((blocks, size, 3 * span), BF16),
         compiler_params=pltpu.CompilerParams(
-            dimension_semantics=("arbitrary",), vmem_limit_bytes=60 * 1024 * 1024
+            dimension_semantics=("arbitrary",), vmem_limit_bytes=VMEM_LIMIT
         ),
         cost_estimate=pl.CostEstimate(
-            flops=pairs * 10 * 128, transcendentals=pairs, bytes_accessed=blocks * size * width * 20
+            flops=pairs * 10 * 128, transcendentals=pairs, bytes_accessed=blocks * size * span * 20
         ),
         name="attention_backward",
     )(phys, flags, query_t, grad_t, out_t, lse, info, key, key_t, value)
+
+
+def project_kernel(
+    width, x_ref, gain_ref, shift_ref, w_ref, bias_q_ref, bias_v_ref,
+    act_ref, query_t_ref, key_ref, key_t_ref, value_ref, value_t_ref,
+):
+    act = layer_norm(x_ref[0].astype(F32), gain_ref[...], shift_ref[...]).astype(BF16)
+    act_ref[0] = act
+    query = (matmul(act, w_ref[:, :width]) + bias_q_ref[...]).astype(BF16).astype(F32) * 0.125
+    query_t_ref[0] = query.T.astype(BF16)
+    key = matmul(act, w_ref[:, width : 2 * width])
+    key_ref[0] = key.astype(BF16)
+    key_t_ref[0] = key.T.astype(BF16)
+    value = matmul(act, w_ref[:, 2 * width :]) + bias_v_ref[...]
+    value_ref[0] = value.astype(BF16)
+    value_t_ref[0] = value.T.astype(BF16)
+
+
+def project(x, gain, shift, weight, bias_q, bias_v):
+    blocks, size, model = x.shape
+    width = bias_q.shape[1]
+    still = lambda i: (0, 0)
+    step = lambda i: (i, 0, 0)
+    straight, turned = (
+        jax.ShapeDtypeStruct((blocks, size, width), BF16),
+        jax.ShapeDtypeStruct((blocks, width, size), BF16),
+    )
+    wide, tall = pl.BlockSpec((1, size, width), step), pl.BlockSpec((1, width, size), step)
+    return pl.pallas_call(
+        functools.partial(project_kernel, width),
+        grid=(blocks,),
+        in_specs=[
+            pl.BlockSpec((1, size, model), step),
+            pl.BlockSpec((1, model), still),
+            pl.BlockSpec((1, model), still),
+            pl.BlockSpec(weight.shape, still, pipeline_mode=pl.Buffered(1)),
+            pl.BlockSpec((1, width), still),
+            pl.BlockSpec((1, width), still),
+        ],
+        out_specs=[pl.BlockSpec((1, size, model), step), tall, wide, tall, wide, tall],
+        out_shape=(
+            jax.ShapeDtypeStruct((blocks, size, model), BF16),
+            turned, straight, turned, straight, turned,
+        ),
+        compiler_params=pltpu.CompilerParams(
+            dimension_semantics=("arbitrary",), vmem_limit_bytes=VMEM_LIMIT
+        ),
+        cost_estimate=pl.CostEstimate(
+            flops=2 * blocks * size * model * 3 * width,
+            transcendentals=blocks * size,
+            bytes_accessed=blocks * size * (4 * model + 10 * width),
+        ),
+        name="project",
+    )(x, gain, shift, weight, bias_q, bias_v)
+
+
+def feed_kernel(
+    parts, pieces, *refs
+):
+    mixed_refs, refs = refs[:parts], refs[parts:]
+    x_ref, cot_ref, refs = refs[0], refs[1], refs[2:]
+    w_out_refs, refs = refs[:parts], refs[parts:]
+    (w_up_ref, w_down_ref, out_bias_ref, gain_ref, shift_ref, up_bias_ref, down_bias_ref), refs = (
+        refs[:7], refs[7:],
+    )
+    act_ref, hidden_ref, grad_upper_ref, layer_ref, grad_resid_ref, grad_attn_ref = refs[:6]
+    refs = refs[6:]
+    grad_mixed_refs, refs = refs[:parts], refs[parts:]
+    sums_ref, up_sum_ref, cot_sc, layer_sc, back_sc = refs
+    first = pl.program_id(0) == 0
+
+    @pl.when(first)
+    def _():
+        sums_ref[...] = jnp.zeros_like(sums_ref)
+        up_sum_ref[...] = jnp.zeros_like(up_sum_ref)
+
+    attn = out_bias_ref[...]
+    for mixed_ref, w_ref in zip(mixed_refs, w_out_refs):
+        attn = attn + matmul(mixed_ref[0], w_ref[...])
+    resid = x_ref[0].astype(F32) + attn
+    center = resid - jnp.mean(resid, axis=-1, keepdims=True)
+    root = lax.rsqrt(jnp.mean(center * center, axis=-1, keepdims=True) + EPS)
+    normed = center * root
+    gain = gain_ref[...]
+    act_ref[0] = (normed * gain + shift_ref[...]).astype(BF16)
+    layer_sc[...] = resid + down_bias_ref[...]
+    back_sc[...] = jnp.zeros_like(back_sc)
+    span = w_up_ref.shape[1] // pieces
+
+    for c in range(pieces):
+        lanes = slice(c * span, (c + 1) * span)
+        upper = matmul(act_ref[0], w_up_ref[:, lanes]) + up_bias_ref[:, lanes]
+        square = upper * upper
+        bend = jnp.tanh(GELU_C * upper * (1.0 + 0.044715 * square))
+        half = 0.5 * (1.0 + bend)
+        hidden = (upper * half).astype(BF16)
+        hidden_ref[0, :, lanes] = hidden
+        slope = half + 0.5 * GELU_C * upper * (1.0 - bend * bend) * (1.0 + 0.134145 * square)
+        grad_upper = (matmul(cot_ref[0], w_down_ref[lanes, :], NT) * slope).astype(BF16)
+        grad_upper_ref[0, :, lanes] = grad_upper
+        up_sum_ref[0:1, lanes] += jnp.sum(grad_upper.astype(F32), axis=0, keepdims=True)
+        layer_sc[...] += matmul(hidden, w_down_ref[lanes, :])
+        back_sc[...] += matmul(grad_upper, w_up_ref[:, lanes], NT)
+
+    layer_ref[0] = layer_sc[...].astype(BF16)
+    back = back_sc[...]
+    scaled = back * gain
+    grad_out = cot_ref[0].astype(F32)
+    grad_resid = grad_out + root * (
+        scaled
+        - jnp.mean(scaled, axis=-1, keepdims=True)
+        - normed * jnp.mean(scaled * normed, axis=-1, keepdims=True)
+    )
+    grad_resid_ref[0] = grad_resid
+    grad_attn = grad_resid.astype(BF16)
+    grad_attn_ref[0] = grad_attn
+    for w_ref, grad_mixed_ref in zip(w_out_refs, grad_mixed_refs):
+        grad_mixed_ref[0] = matmul(grad_attn, w_ref[...], NT).astype(BF16)
+    sums_ref[0:1, :] += jnp.sum(grad_attn.astype(F32), axis=0, keepdims=True)
+    sums_ref[1:2, :] += jnp.sum(back * normed, axis=0, keepdims=True)
+    sums_ref[2:3, :] += jnp.sum(back, axis=0, keepdims=True)
+    sums_ref[3:4, :] += jnp.sum(grad_out, axis=0, keepdims=True)
+
+
+def feed(mixed, x, cotangent, w_out, part, w_up, w_down, vectors, up_bias):
+    parts = len(mixed)
+    rows, size, model = x.shape
+    width = mixed[0].shape[2]
+    wide = w_up.shape[1]
+    still = lambda i, p: (0, 0)
+    step = lambda i, p: (i, 0, 0)
+    once = pl.Buffered(1)
+    slab = pl.BlockSpec((1, size, model), step)
+    head_slab = pl.BlockSpec((1, size, width), step)
+    wide_slab = pl.BlockSpec((1, size, wide), step)
+    vector = pl.BlockSpec((1, model), still)
+    w_out_specs = [
+        pl.BlockSpec((width, model), lambda i, p, s=s: (p[0] ^ s, 0), pipeline_mode=once)
+        for s in range(parts)
+    ]
+
+    def body(p_ref, *refs):
+        feed_kernel(parts, wide // model, *refs)
+
+    shape = jax.ShapeDtypeStruct
+    out = pl.pallas_call(
+        body,
+        grid_spec=pltpu.PrefetchScalarGridSpec(
+            num_scalar_prefetch=1,
+            grid=(rows,),
+            in_specs=[head_slab] * parts
+            + [slab, slab]
+            + w_out_specs
+            + [
+                pl.BlockSpec(w_up.shape, still, pipeline_mode=once),
+                pl.BlockSpec(w_down.shape, still, pipeline_mode=once),
+                vector,
+                vector,
+                vector,
+                pl.BlockSpec((1, wide), still),
+                vector,
+            ],
+            out_specs=[slab, wide_slab, wide_slab, slab, slab, slab]
+            + [head_slab] * parts
+            + [pl.BlockSpec((8, model), still), pl.BlockSpec((8, wide), still)],
+            scratch_shapes=[
+                pltpu.VMEM((8, 128), F32),
+                pltpu.VMEM((size, model), F32),
+                pltpu.VMEM((size, model), F32),
+            ],
+        ),
+        out_shape=[
+            shape((rows, size, model), BF16),
+            shape((rows, size, wide), BF16),
+            shape((rows, size, wide), BF16),
+            shape((rows, size, model), BF16),
+            shape((rows, size, model), F32),
+            shape((rows, size, model), BF16),
+        ]
+        + [shape((rows, size, width), BF16)] * parts
+        + [shape((8, model), F32), shape((8, wide), F32)],
+        compiler_params=pltpu.CompilerParams(
+            dimension_semantics=("arbitrary",), vmem_limit_bytes=VMEM_LIMIT
+        ),
+        cost_estimate=pl.CostEstimate(
+            flops=2 * rows * size * model * (4 * wide + 2 * model),
+            transcendentals=rows * size * wide,
+            bytes_accessed=rows * size * (4 * wide + 16 * model),
+        ),
+        name="feed",
+    )(
+        part.reshape(1), *mixed, x, cotangent, *([w_out] * parts), w_up, w_down,
+        vectors["out_bias"], vectors["gain"], vectors["shift"], up_bias, vectors["down_bias"],
+    )
+    return out[:6], out[6 : 6 + parts], out[6 + parts], out[7 + parts]
 
 
 def row_layout(sizes, prefixes, lens, padding, length, size):
@@ -360,86 +561,59 @@
     order = jnp.arange(blocks, dtype=jnp.int32)
     phys = (((order % parts) ^ part) * rows + ((order // parts) ^ owner)).astype(jnp.int32)
 
-    def my_columns(start):
-        return lax.dynamic_slice_in_dim(w_qkv, start * model + part * width, width, 1)
-
-    w_mine = jnp.concatenate([my_columns(0), my_columns(1), my_columns(2)], axis=1)
-    bias_q = lax.dynamic_slice_in_dim(query_bias, part * width, width, 0).astype(F32)
-    bias_v = lax.dynamic_slice_in_dim(value_bias, part * width, width, 0).astype(F32)
-    w_out_parts = [take(w_out.reshape(parts, width, model), part ^ s) for s in range(parts)]
+    def my_columns(start, first=0, count=None):
+        begin = start * model + part * width + first
+        return lax.dynamic_slice_in_dim(w_qkv, begin, count or width, 1)
+
+    def as_row(vector):
+        return vector.astype(F32).reshape(1, -1)
+
+    group = 2 if heads % 2 == 0 else heads
+    starts = list(range(0, heads, group))
+    span = group * HEAD_DIM
+    w_mine = jnp.concatenate([my_columns(n) for n in range(3)], axis=1)
+    w_groups = [
+        jnp.concatenate([my_columns(n, h * HEAD_DIM, span) for n in range(3)], axis=1)
+        for h in starts
+    ]
+    bias_q = lax.dynamic_slice_in_dim(query_bias, part * width, width, 0)
+    bias_v = lax.dynamic_slice_in_dim(value_bias, part * width, width, 0)
 
     mine = bring(tokens)
     row = jnp.concatenate([mine] + [swap(mine, "pos", s) for s in range(1, parts)], axis=0)
-    act_one = layer_norm(
-        row.reshape(-1, model).astype(F32), attn_gain.astype(F32), attn_shift.astype(F32)
-    ).astype(BF16)
-    projected = matmul(act_one, w_mine)
-    query = ((projected[:, :width] + bias_q).astype(BF16) * 0.125).astype(BF16)
-    key = projected[:, width : 2 * width].astype(BF16)
-    value = (projected[:, 2 * width :] + bias_v).astype(BF16)
-
-    def blocked(values):
-        return values.reshape(blocks, size, width)
-
-    def turned(values):
-        return blocked(values).transpose(0, 2, 1)
-
-    query_t, key_t = turned(query), turned(key)
+    cotangent, row = lax.optimization_barrier((cotangent, row))
+    own_cotangent = bring(cotangent)
+    act_one, query_t, key, key_t, value, value_t = project(
+        row, as_row(attn_gain), as_row(attn_shift), w_mine, as_row(bias_q), as_row(bias_v)
+    )
     mixed_all, out_t, lse = attention_forward(
-        phys, flags, query_t, blocked(key), turned(value), info, heads
-    )
-    own_cotangent = bring(cotangent).reshape(-1, model)
+        phys, flags, query_t, key, value_t, info, heads
+    )
     mixed_parts = []
     for s in range(parts):
         piece = mixed_all[s * rows : (s + 1) * rows]
-        mixed_parts.append((swap(piece, "pos", s) if s else piece).reshape(-1, width))
-
-    inputs = mine.reshape(-1, model).astype(F32)
-    attn = sum(matmul(m, w) for m, w in zip(mixed_parts, w_out_parts))
-    resid = inputs + (attn + out_bias.astype(F32))
-    normed_two, norm_two_pull = jax.vjp(
-        layer_norm, resid, ffn_gain.astype(F32), ffn_shift.astype(F32)
-    )
-    act_two = normed_two.astype(BF16)
-    upper = matmul(act_two, w_up) + up_bias.astype(F32)
-    hidden_full, gelu_pull = jax.vjp(gelu_tanh, upper)
-    hidden = hidden_full.astype(BF16)
-    layer_out = (resid + (matmul(hidden, w_down) + down_bias.astype(F32))).astype(BF16)
-    grad_out = own_cotangent.astype(F32)
-    grad_w_down = matmul(hidden, own_cotangent, TN).astype(BF16)
-    grad_down_bias = jnp.sum(grad_out, axis=0)
-    (grad_upper_full,) = gelu_pull(matmul(own_cotangent, w_down, NT))
-    grad_upper = grad_upper_full.astype(BF16)
-    grad_w_up = matmul(act_two, grad_upper, TN).astype(BF16)
-    grad_up_bias = jnp.sum(grad_upper.astype(F32), axis=0)
-    grad_resid_norm, grad_ffn_gain, grad_ffn_shift = norm_two_pull(matmul(grad_upper, w_up, NT))
-    grad_resid = grad_out + grad_resid_norm
-    grad_attn = grad_resid.astype(BF16)
-    stacked = jnp.stack(mixed_parts)
-    mixed = jnp.concatenate([take(stacked, g ^ part) for g in range(parts)], axis=1)
-    grad_w_out = matmul(mixed, grad_attn, TN).astype(BF16)
-    grad_out_bias = jnp.sum(grad_attn.astype(F32), axis=0)
-    grad_mixed = [matmul(grad_attn, w, NT).astype(BF16) for w in w_out_parts]
+        mixed_parts.append(swap(piece, "pos", s) if s else piece)
+
+    (act_two, hidden, grad_upper, layer_out, grad_resid, grad_attn), grad_mixed, sums, up_sum = feed(
+        mixed_parts, mine, own_cotangent, w_out, part, w_up, w_down,
+        {
+            "out_bias": as_row(out_bias),
+            "gain": as_row(ffn_gain),
+            "shift": as_row(ffn_shift),
+            "down_bias": as_row(down_bias),
+        },
+        as_row(up_bias),
+    )
     grad_all = jnp.concatenate(
         [swap(g, "pos", s) if s else g for s, g in enumerate(grad_mixed)], axis=0
     )
-    grad_q, grad_k, grad_v = attention_backward(
-        phys, flags, query_t, turned(grad_all), out_t, lse, info,
-        blocked(key), key_t, blocked(value), heads,
-    )
-    grad_project = jnp.concatenate([grad_q, grad_k, grad_v], axis=2).reshape(-1, 3 * width)
-    grad_w_mine = matmul(act_one, grad_project, TN).astype(BF16)
-    grad_query_mine = jnp.sum(grad_q.astype(F32), axis=(0, 1))
-    grad_value_mine = jnp.sum(grad_v.astype(F32), axis=(0, 1))
-    grad_act = matmul(grad_project, w_mine, NT)
+    grad_t = grad_all.transpose(0, 2, 1)
+    layer_home = give_back(layer_out)
+
     local = rows * size
-    grad_act_own = grad_act[:local]
-    for s in range(1, parts):
-        sent = grad_act[s * local : (s + 1) * local].astype(BF16)
-        grad_act_own = grad_act_own + swap(sent, "pos", s).astype(F32)
-    _, norm_one_pull = jax.vjp(layer_norm, inputs, attn_gain.astype(F32), attn_shift.astype(F32))
-    grad_input_norm, grad_attn_gain, grad_attn_shift = norm_one_pull(grad_act_own)
-    tokens_grad = (grad_resid + grad_input_norm).astype(BF16)
+
+    def flat(values):
+        return values.reshape(-1, values.shape[-1])
 
     row_place = lax.axis_index(row_axis)
     row_steps = [(row_axis, m, (row_place // m) % 2) for m in bits(lax.axis_size(row_axis))]
@@ -448,18 +622,53 @@
     one_way = part_steps + own_steps + row_steps
     other_way = part_steps + own_steps[::-1] + row_steps
 
-    def total(values, steps):
-        return double(halve(values, steps), steps).astype(F32)
-
-    sum_w_down = total(grad_w_down, one_way)
-    sum_w_up = total(grad_w_up, other_way)
-    sum_w_out = total(grad_w_out, one_way)
+    grad_w_down = matmul(flat(hidden), flat(own_cotangent), TN).astype(BF16)
+    share_down = halve(grad_w_down, one_way)
+    stacked = jnp.stack(mixed_parts)
+    mixed = jnp.concatenate([flat(take(stacked, g ^ part)) for g in range(parts)], axis=1)
+    grad_w_up = jnp.concatenate(
+        [
+            matmul(flat(act_two), flat(grad_upper), TN).astype(BF16),
+            matmul(mixed, flat(grad_attn), TN).astype(BF16),
+        ],
+        axis=1,
+    )
+    share_up = halve(grad_w_up, other_way)
+
+    grads = [
+        attention_backward(
+            phys, flags, query_t, grad_t, out_t, lse, info, key, key_t, value, group, h
+        )
+        for h in starts
+    ]
+    sum_w_down = double(share_down, one_way).astype(F32)
+    sum_up = double(share_up, other_way)
+    sum_w_up, sum_w_out = sum_up[:, : w_up.shape[1]].astype(F32), sum_up[:, w_up.shape[1] :].astype(F32)
+
+    grad_act = sum(matmul(flat(g), w, NT) for g, w in zip(grads, w_groups))
+    grad_act_own = grad_act[:local]
+    for s in range(1, parts):
+        sent = grad_act[s * local : (s + 1) * local].astype(BF16)
+        grad_act_own = grad_act_own + swap(sent, "pos", s).astype(F32)
+    inputs = flat(mine).astype(F32)
+    _, norm_one_pull = jax.vjp(layer_norm, inputs, attn_gain.astype(F32), attn_shift.astype(F32))
+    grad_input_norm, grad_attn_gain, grad_attn_shift = norm_one_pull(grad_act_own)
+    tokens_grad = (flat(grad_resid) + grad_input_norm).astype(BF16).reshape(rows, size, model)
+
     steps = other_way[len(part_steps) :]
-    summed_mine = double(halve(grad_w_mine, steps), steps)
+    summed = []
+    for batch in (grads[:-1], grads[-1:]):
+        if batch:
+            share = jnp.concatenate([matmul(flat(act_one), flat(g), TN).astype(BF16) for g in batch], axis=1)
+            summed.append(double(halve(share, steps), steps))
+    summed_mine = jnp.concatenate(summed, axis=1)
     pieces = [summed_mine] + [swap(summed_mine, "pos", s) for s in range(1, parts)]
-    pieces = jnp.stack(pieces).reshape(parts, model, 3, width)
-    pieces = [take(pieces, g ^ part) for g in range(parts)]
-    sum_w_qkv = jnp.stack(pieces, axis=2).reshape(model, 3 * model).astype(F32)
+    pieces = jnp.stack(pieces).reshape(parts, model, len(starts), 3, span)
+    pieces = jnp.stack([take(pieces, g ^ part) for g in range(parts)], axis=3)
+    sum_w_qkv = pieces.transpose(0, 2, 3, 1, 4).reshape(model, 3 * model).astype(F32)
+
+    grad_query_mine = jnp.concatenate([jnp.sum(flat(g)[:, :span].astype(F32), axis=0) for g in grads])
+    grad_value_mine = jnp.concatenate([jnp.sum(flat(g)[:, 2 * span :].astype(F32), axis=0) for g in grads])
 
     def placed(values):
         return lax.dynamic_update_slice_in_dim(jnp.zeros((model,), F32), values, part * width, 0)
@@ -470,19 +679,16 @@
             grad_attn_shift,
             placed(grad_query_mine),
             placed(grad_value_mine),
-            grad_out_bias,
-            grad_ffn_gain,
-            grad_ffn_shift,
-            grad_down_bias,
-            grad_up_bias,
+            sums[:4].reshape(-1),
+            up_sum[0],
         ]
     )
     for axis, mask, _ in one_way:
         small = small + swap(small, axis, mask)
     vectors = small[: 8 * model].reshape(8, model)
     return (
-        give_back(layer_out.reshape(rows, size, model)),
-        give_back(tokens_grad.reshape(rows, size, model)),
+        layer_home,
+        give_back(tokens_grad),
         vectors[0],
         vectors[1],
         sum_w_qkv,

time: 645 us -> 589 us (0.913)
  Pallas kernels: 101 us -> 171 us
  matrix products: 84.6 us -> 34.1 us
  other arithmetic: 97.7 us -> 66.2 us
  local copies, waits for them, and re-layouts: 108 us -> 83.2 us
  starting transfers between devices: 74.8 us -> 52.2 us
    pallas_call x1 -> x5, Pallas kernels: 53.9 us -> 123 us  [the longest x3 73.7 us: attention_backward(): pl.pallas_call(functools.partial(backward_kernel, heads, first, blocks),...]
    dot_general x14 -> x9, matrix products: 84.6 us -> 34.1 us  [matmul(): return lax.dot_general(left, right, dims, preferred_element_type=F32)]
    ppermute x60 -> x58, starting transfers between devices: 74.8 us -> 52.2 us  [swap(): return lax.ppermute(values, axis, [(i, i ^ mask) for i in range(count)])]
    convert_element_type x15 -> x6, other arithmetic: 29.7 us -> 16.8 us  [the longest x1 5.43 us: per_device(): pieces.transpose(0, 2, 3, 1, 4).reshape(model, 3 * model).astype(F32)]
    reduce_sum x3 -> x1, other arithmetic: 9.49 us -> 2.02 us  [layer_norm(): return center * lax.rsqrt(spread + EPS) * gain + shift]
    broadcast_in_dim x6 -> x0, local copies, waits for them, and re-layouts: 7.06 us -> none  [give_back(): out = lax.dynamic_update_index_in_dim(out, slab, owner ^ m, 0)]
    unnamed x167 -> x147, local copies, waits for them, and re-layouts: 24.1 us -> 19 us
    ppermute x60 -> x58, waiting for transfers between devices: 167 us -> 168 us  [swap(): return lax.ppermute(values, axis, [(i, i ^ mask) for i in range(count)])]
  transfers between devices with their start and end apart: 60 -> 58, of which waited for: 30 -> 32; matrix products, arithmetic and copies ran while one was open for 32% -> 26% of each run, Pallas kernels for 16% -> 13%
where the time goes in v2:
time: 589 us; the launch traced here: 582 us
  Pallas kernels  171 us (29%)
  waiting for transfers between devices  168 us (29%)
  local copies, waits for them, and re-layouts  83.2 us (14%)
  other arithmetic  66.2 us (11%)
  starting transfers between devices  52.2 us (9%)
  matrix products  34.1 us (6%)
  between operations  8.34 us (1%)
    ppermute x58, waiting for transfers between devices, swap(): return lax.ppermute(values, axis, [(i, i ^ mask) for i in range(count)])  168 us
    pallas_call x3, Pallas kernels, attention_backward(): pl.pallas_call(functools.partial(backward_kernel, heads, first, blocks),...  73.7 us
    ppermute x58, starting transfers between devices, swap(): return lax.ppermute(values, axis, [(i, i ^ mask) for i in range(count)])  52.2 us
    pallas_call x1, Pallas kernels, attention_forward(): pl.pallas_call(functools.partial(forward_kernel, heads, blocks), grid_spe...  48.1 us
    pallas_call x1, Pallas kernels, feed(): pl.pallas_call(body, grid_spec=pltpu.PrefetchScalarGridSpec(num_scalar_pr...  36.5 us
    dot_general x9, matrix products, matmul(): return lax.dot_general(left, right, dims, preferred_element_type=F32)  34.1 us
    unnamed x147, local copies, waits for them, and re-layouts  19 us
    pallas_call x1, Pallas kernels, project(): pl.pallas_call(functools.partial(project_kernel, width), grid=(blocks,),...  12.3 us
  transfers between devices with their start and end apart: 58, of which 32 were waited for; matrix products, arithmetic and copies ran while one was open for 26% of the time, Pallas kernels for 13%

profile of v2, /device:TPU:0, one launch (start us, length us, event | category | flops | bytes accessed | tf_op | source)
XLA Modules:
  0.0 582.4 jit_solution(2186989369961136593)
XLA Ops:
  0.8 2.3 dynamic-slice_bitcast_fusion.10
  3.1 3.0 collective-permute-start
  42.9 12.3 %project.1 = (bf16[8,256,768]{2,1,0:T(8,128)(2,1)}, bf16[8,384,256]{2,1,0:T(8,128)(2,1)}, bf16[8,256,384]{2,1,0:T(8,128)(2,1)}, bf16[8,384,256]{2,1,0:T(8,128)(2...) custom-call(bf16[8,256,768]{2,1,0:T(8,128)(2,1)} %constant_dynamic-update-slice_fusion.x_ref, ...), custom_call_target="tpu_custom_call" | custom-call | flops 3623878656 | bytes 14155776 | tf_op jit(solution)/shard_map/project/pallas_call | solution.py:274
  55.1 48.1 %attention_forward.1 = (bf16[8,256,384]{2,1,0:T(8,128)(2,1)}, f32[8,384,256]{2,1,0:T(8,128)}, f32[8,8,256]{2,1,0:T(8,128)}) custom-call(s32[8]{0:T(128)} %fusion.73.phys_ref, s32[64]{0:T(128)} %reshape.619.flag_ref, bf16[8,384,256]{2,1,0:T(8,128)(2,1)} %get-tuple-element.37.query_t_ref, bf16[8,256,384]{2,1,0:T(8,128)(2,1)} %get-tuple-element.38.key_ref, ...), custom_call_target="tpu_custom_call" | custom-call | flops 7247757312 | bytes 12582912 | tf_op jit(solution)/shard_map/attention_forward/pallas_call | solution.py:125
  103.2 2.6 slice_bitcast_fusion.6
  106.6 3.4 collective-permute-start.7
  111.8 6.7 %collective-permute-done.5 = bf16[256,768]{1,0:T(8,128)(2,1)S(1)} collective-permute-done((bf16[256,768]{1,0:T(8,128)(2,1)S(1)}, bf16[256,768]{1,0:T(8,128)(2,1)S(1)}, u32[]{:S(2)}, u32[]{:S(2)}) %collective-permute-start.5) | collective-permute-done | bytes 393248 | tf_op jit(solution)/shard_map/ppermute | solution.py:478
  118.5 7.6 %collective-permute-done.6 = bf16[256,768]{1,0:T(8,128)(2,1)S(1)} collective-permute-done((bf16[256,768]{1,0:T(8,128)(2,1)S(1)}, bf16[256,768]{1,0:T(8,128)(2,1)S(1)}, u32[]{:S(2)}, u32[]{:S(2)}) %collective-permute-start.6) | collective-permute-done | bytes 393248 | tf_op jit(solution)/shard_map/ppermute | solution.py:478
  128.4 36.5 %feed.1 = (bf16[4,256,768]{2,1,0:T(8,128)(2,1)}, bf16[4,256,3072]{2,1,0:T(8,128)(2,1)}, bf16[4,256,3072]{2,1,0:T(8,128)(2,1)}, bf16[4,256,768]{2,1,0:T(8,128)(2,...) custom-call(s32[1]{0:T(128)} %bitcast.p_ref, ...), custom_call_target="tpu_custom_call" | custom-call | flops 21743271936 | bytes 25165824 | tf_op jit(solution)/shard_map/feed/pallas_call | solution.py:391
  165.0 9.0 %bitcast_convert_fusion = bf16[3072,768]{1,0:T(8,128)(2,1)S(1)} fusion(bf16[4,256,3072]{2,1,0:T(8,128)(2,1)} %get-tuple-element.56, bf16[1,256,768]{2,1,0:T(8,128)(2,1)S(1)} %bitcast.300, bf16[1,256,768]{2,1,0:T(8,128)(2,1)S(1)} %bitcast.298, bf16[1,256,768]{2,1,0:T(8,128)(2,1)S(1)} %bitcast.296, bf16[1,256,768]{2,1,0:T(8,128)(2,1)S(1)} %get-tuple-element.155), kind=kOutput, calls=%fused_computation | convolution fusion | flops 4836556800 | bytes 12582912 | tf_op jit(solution)/shard_map/dot_general | solution.py:32
  181.8 8.2 %bitcast_convert_fusion.1 = bf16[768,3072]{1,0:T(8,128)(2,1)S(1)} fusion(bf16[4,256,768]{2,1,0:T(8,128)(2,1)S(1)} %copy-done.63, bf16[4,256,3072]{2,1,0:T(8,128)(2,1)} %get-tuple-element.54), kind=kOutput, calls=%fused_computation.1 | convolution fusion | flops 4834197504 | bytes 12582912 | tf_op jit(solution)/shard_map/dot_general | solution.py:32
  191.4 2.5 fusion.12
  197.4 2.0 copy-done.4
  205.7 8.8 %collective-permute-done.10 = bf16[256,768]{1,0:T(8,128)(2,1)S(1)} collective-permute-done((bf16[256,768]{1,0:T(8,128)(2,1)S(1)}, bf16[256,768]{1,0:T(8,128)(2,1)S(1)}, u32[]{:S(2)}, u32[]{:S(2)}) %collective-permute-start.10) | collective-permute-done | bytes 393248 | tf_op jit(solution)/shard_map/ppermute | solution.py:478
  214.5 3.0 maximum_bitcast_fusion.grad_t_ref
  217.6 24.5 %attention_backward.4 = bf16[8,256,384]{2,1,0:T(8,128)(2,1)} custom-call(s32[8]{0:T(128)} %fusion.73.phys_ref, s32[64]{0:T(128)} %reshape.619.flag_ref, bf16[8,384,256]{2,1,0:T(8,128)(2,1)} %get-tuple-element.37.query_t_ref, bf16[8,384,256]{2,1,0:T(8,128)(2,1)} %maximum_bitcast_fusion.grad_t_ref, f32[8,384,256]{2,1,0:T(8,128)} %get-tuple-element.46.out_t_ref, ...), custom_call_target="tpu_custom_call" | custom-call | flops 6039797760 | bytes 5242880 | tf_op jit(solution)/shard_map/attention_backward/pallas_call | solution.py:234
  242.1 24.5 %attention_backward.3 = bf16[8,256,384]{2,1,0:T(8,128)(2,1)} custom-call(s32[8]{0:T(128)} %fusion.73.phys_ref, s32[64]{0:T(128)} %reshape.619.flag_ref, bf16[8,384,256]{2,1,0:T(8,128)(2,1)} %get-tuple-element.37.query_t_ref, bf16[8,384,256]{2,1,0:T(8,128)(2,1)} %maximum_bitcast_fusion.grad_t_ref, f32[8,384,256]{2,1,0:T(8,128)} %get-tuple-element.46.out_t_ref, ...), custom_call_target="tpu_custom_call" | custom-call | flops 6039797760 | bytes 5242880 | tf_op jit(solution)/shard_map/attention_backward/pallas_call | solution.py:234
  266.6 24.7 %attention_backward.5 = bf16[8,256,384]{2,1,0:T(8,128)(2,1)} custom-call(s32[8]{0:T(128)} %fusion.73.phys_ref, s32[64]{0:T(128)} %reshape.619.flag_ref, bf16[8,384,256]{2,1,0:T(8,128)(2,1)} %get-tuple-element.37.query_t_ref, bf16[8,384,256]{2,1,0:T(8,128)(2,1)} %maximum_bitcast_fusion.grad_t_ref, f32[8,384,256]{2,1,0:T(8,128)} %get-tuple-element.46.out_t_ref, ...), custom_call_target="tpu_custom_call" | custom-call | flops 6039797760 | bytes 5242880 | tf_op jit(solution)/shard_map/attention_backward/pallas_call | solution.py:234
  291.3 3.5 fusion.17
  297.5 2.7 copy.100
  301.4 3.8 fusion.18
  311.0 2.0 add_add_fusion
  313.9 8.7 %collective-permute-done.29 = bf16[384,384]{1,0:T(8,128)(2,1)S(1)} collective-permute-done((bf16[384,384]{1,0:T(8,128)(2,1)S(1)}, bf16[384,384]{1,0:T(8,128)(2,1)S(1)}, u32[]{:S(2)}, u32[]{:S(2)}) %collective-permute-start.29) | collective-permute-done | bytes 294944 | tf_op jit(solution)/shard_map/ppermute | solution.py:478
  323.1 4.8 collective-permute-done.30
  328.2 4.2 collective-permute-done.31
  332.5 3.3 collective-permute-start.32
  337.7 3.0 collective-permute-start.33
  344.6 4.6 collective-permute-done.22
  351.6 3.8 collective-permute-done.23
  356.5 5.0 collective-permute-done.24
  363.6 3.8 collective-permute-done.25
  368.6 4.0 collective-permute-done.26
  373.1 2.4 fusion.2
  377.3 2.5 fusion
  381.3 2.0 multiply_reduce_fusion
  383.6 11.7 %collective-permute-done.49 = bf16[768,768]{1,0:T(8,128)(2,1)S(1)} collective-permute-done((bf16[768,768]{1,0:T(8,128)(2,1)S(1)}, bf16[768,768]{1,0:T(8,128)(2,1)S(1)}, u32[]{:S(2)}, u32[]{:S(2)}) %collective-permute-start.49) | collective-permute-done | bytes 1179680 | tf_op jit(solution)/shard_map/ppermute | solution.py:478
  395.6 3.7 collective-permute-start.50
  399.3 8.4 %collective-permute-done.39 = bf16[192,3840]{1,0:T(8,128)(2,1)S(1)} collective-permute-done((bf16[192,3840]{1,0:T(8,128)(2,1)S(1)}, bf16[192,3840]{1,0:T(8,128)(2,1)S(1)}, u32[]{:S(2)}, u32[]{:S(2)}) %collective-permute-start.39) | collective-permute-done | bytes 1474592 | tf_op jit(solution)/shard_map/ppermute | solution.py:478
  410.2 3.8 collective-permute-done.50
  415.4 4.2 collective-permute-done.40
  421.6 2.8 collective-permute-done.51
  424.6 10.5 %collective-permute-done.41 = bf16[48,3840]{1,0:T(8,128)(2,1)S(1)} collective-permute-done((bf16[48,3840]{1,0:T(8,128)(2,1)S(1)}, bf16[48,3840]{1,0:T(8,128)(2,1)S(1)}, u32[]{:S(2)}, u32[]{:S(2)}) %collective-permute-start.41) | collective-permute-done | bytes 368672 | tf_op jit(solution)/shard_map/ppermute | solution.py:478
  435.4 3.0 collective-permute-start.53
  438.4 6.2 %collective-permute-done.42 = bf16[24,3840]{1,0:T(8,128)(2,1)S(1)} collective-permute-done((bf16[24,3840]{1,0:T(8,128)(2,1)S(1)}, bf16[24,3840]{1,0:T(8,128)(2,1)S(1)}, u32[]{:S(2)}, u32[]{:S(2)}) %collective-permute-start.42) | collective-permute-done | bytes 184352 | tf_op jit(solution)/shard_map/ppermute | solution.py:478
  446.7 4.9 collective-permute-done.43
  451.7 2.9 collective-permute-done.54
  456.5 3.1 collective-permute-done.44
  463.1 7.9 %collective-permute-done.55 = bf16[384,768]{1,0:T(8,128)(2,1)S(1)} collective-permute-done((bf16[384,768]{1,0:T(8,128)(2,1)S(1)}, bf16[384,768]{1,0:T(8,128)(2,1)S(1)}, u32[]{:S(2)}, u32[]{:S(2)}) %collective-permute-start.55) | collective-permute-done | bytes 589856 | tf_op jit(solution)/shard_map/ppermute | solution.py:478
  476.6 5.0 collective-permute-done.18
  482.2 3.4 collective-permute-done.19
  491.5 5.9 %collective-permute-done.46 = bf16[192,3840]{1,0:T(8,128)(2,1)S(1)} collective-permute-done((bf16[192,3840]{1,0:T(8,128)(2,1)S(1)}, bf16[192,3840]{1,0:T(8,128)(2,1)S(1)}, u32[]{:S(2)}, u32[]{:S(2)}) %collective-permute-start.46) | collective-permute-done | bytes 1474592 | tf_op jit(solution)/shard_map/ppermute | solution.py:478
  505.6 16.0 %collective-permute-done.14 = bf16[256,768]{1,0:T(8,128)(2,1)S(1)} collective-permute-done((bf16[256,768]{1,0:T(8,128)(2,1)S(1)}, bf16[256,768]{1,0:T(8,128)(2,1)S(1)}, u32[]{:S(2)}, u32[]{:S(2)}) %collective-permute-start.14) | collective-permute-done | bytes 393248 | tf_op jit(solution)/shard_map/ppermute | solution.py:478
  523.2 3.9 copy.85
  527.0 3.9 copy.86
  530.9 5.1 fusion.7
  536.0 3.8 copy.87
  539.8 3.8 copy.88
  543.7 5.4 convert_bitcast_fusion
  549.1 8.3 %copy.89 = f32[768,3,2,3,128]{0,4,3,2,1:T(8,128)} copy(f32[768,3,2,3,128]{4,0,2,1,3:T(8,128)} %convert_bitcast_fusion) | data formatting | bytes 14155776 | tf_op jit(solution)/shard_map/convert_element_type | solution.py:668
  557.4 8.0 %copy.93 = f32[768,2304]{1,0:T(8,128)} copy(f32[768,2304]{0,1:T(8,128)} %bitcast.240) | data formatting | bytes 14155776
  565.4 3.2 broadcast_select_fusion.3
  568.6 4.5 maximum_convert_fusion
  573.1 2.5 broadcast_select_fusion.1
  575.6 5.0 fusion.1
  (394 shorter events, 119.3 us)
Async XLA Ops:
  3.1 25.5 %collective-permute-start = (bf16[256,768]{1,0:T(8,128)(2,1)S(1)}, bf16[256,768]{1,0:T(8,128)(2,1)S(1)}, u32[]{:S(2)}, u32[]{:S(2)}) collective-permute-start(bf16[256,768]{1,0:T(8,128)(2,1)S(1)} %get-tuple-element.160), channel_id=1, source_target_pairs={{0,2},{1,3},{2,0},{3,1},{4,6},{5,7},{6,4},{7,5},{8,10},{9,11},{10,... | collective-permute-start | bytes 1179656 | tf_op jit(solution)/shard_map/ppermute | solution.py:478
  6.1 22.5 %collective-permute-start.1 = (bf16[256,768]{1,0:T(8,128)(2,1)S(1)}, bf16[256,768]{1,0:T(8,128)(2,1)S(1)}, u32[]{:S(2)}, u32[]{:S(2)}) collective-permute-start(bf16[256,768]{1,0:T(8,128)(2,1)S(1)} %get-tuple-element.163), channel_id=1, source_target_pairs={{0,4},{1,5},{2,6},{3,7},{4,0},{5,1},{6,2},{7,3},{8,12},{9,13},{10,... | collective-permute-start | bytes 1179656 | tf_op jit(solution)/shard_map/ppermute | solution.py:478
  7.6 21.0 %collective-permute-start.2 = (bf16[256,768]{1,0:T(8,128)(2,1)S(1)}, bf16[256,768]{1,0:T(8,128)(2,1)S(1)}, u32[]{:S(2)}, u32[]{:S(2)}) collective-permute-start(bf16[256,768]{1,0:T(8,128)(2,1)S(1)} %get-tuple-element.159), channel_id=1, source_target_pairs={{0,6},{1,7},{2,4},{3,5},{4,2},{5,3},{6,0},{7,1},{8,14},{9,15},{10,... | collective-permute-start | bytes 1179656 | tf_op jit(solution)/shard_map/ppermute | solution.py:478
  29.5 80.5 %copy-start.2 = (bf16[4,256,768]{2,1,0:T(8,128)(2,1)}, bf16[4,256,768]{2,1,0:T(8,128)(2,1)S(1)}, u32[]{:S(2)}) copy-start(bf16[4,256,768]{2,1,0:T(8,128)(2,1)S(1)} %get-tuple-element.114.refs_2_) | copy-start | bytes 4718596
  29.5 12.2 %collective-permute-start.3 = (bf16[4,256,768]{2,1,0:T(8,128)(2,1)S(1)}, bf16[4,256,768]{2,1,0:T(8,128)(2,1)S(1)}, u32[]{:S(2)}, u32[]{:S(2)}) collective-permute-start(bf16[4,256,768]{2,1,0:T(8,128)(2,1)S(1)} %get-tuple-element.114.refs_2_), channel_id=1, source_target_pairs={{0,1},{1,0},{2,3},{3,2},{4,5},{5,4},{6,7},{7,6},{8,9},{9,8},{10,11... | collective-permute-start | bytes 4718600 | tf_op jit(solution)/shard_map/ppermute | solution.py:478
  105.8 21.6 %collective-permute-start.4 = (bf16[4,256,384]{2,1,0:T(8,128)(2,1)S(1)}, bf16[4,256,384]{2,1,0:T(8,128)(2,1)S(1)}, u32[]{:S(2)}, u32[]{:S(2)}) collective-permute-start(bf16[4,256,384]{2,1,0:T(8,128)(2,1)S(1)} %get-tuple-element.146), channel_id=1, source_target_pairs={{0,1},{1,0},{2,3},{3,2},{4,5},{5,4},{6,7},{7,6},{8,9},{9,8},{10,11... | collective-permute-start | bytes 2359304 | tf_op jit(solution)/shard_map/ppermute | solution.py:478
  106.4 12.1 %collective-permute-start.5 = (bf16[256,768]{1,0:T(8,128)(2,1)S(1)}, bf16[256,768]{1,0:T(8,128)(2,1)S(1)}, u32[]{:S(2)}, u32[]{:S(2)}) collective-permute-start(bf16[256,768]{1,0:T(8,128)(2,1)S(1)} %get-tuple-element.158), channel_id=1, source_target_pairs={{0,2},{1,3},{2,0},{3,1},{4,6},{5,7},{6,4},{7,5},{8,10},{9,11},{10,... | collective-permute-start | bytes 1179656 | tf_op jit(solution)/shard_map/ppermute | solution.py:478
  106.5 19.5 %collective-permute-start.6 = (bf16[256,768]{1,0:T(8,128)(2,1)S(1)}, bf16[256,768]{1,0:T(8,128)(2,1)S(1)}, u32[]{:S(2)}, u32[]{:S(2)}) collective-permute-start(bf16[256,768]{1,0:T(8,128)(2,1)S(1)} %get-tuple-element.157), channel_id=1, source_target_pairs={{0,4},{1,5},{2,6},{3,7},{4,0},{5,1},{6,2},{7,3},{8,12},{9,13},{10,... | collective-permute-start | bytes 1179656 | tf_op jit(solution)/shard_map/ppermute | solution.py:478
  106.6 19.4 %collective-permute-start.7 = (bf16[256,768]{1,0:T(8,128)(2,1)S(1)}, bf16[256,768]{1,0:T(8,128)(2,1)S(1)}, u32[]{:S(2)}, u32[]{:S(2)}) collective-permute-start(bf16[256,768]{1,0:T(8,128)(2,1)S(1)} %get-tuple-element.156), channel_id=1, source_target_pairs={{0,6},{1,7},{2,4},{3,5},{4,2},{5,3},{6,0},{7,1},{8,14},{9,15},{10,... | collective-permute-start | bytes 1179656 | tf_op jit(solution)/shard_map/ppermute | solution.py:478
  110.6 54.3 %copy-start.49 = (f32[1,2,4,128]{3,1,2,0:T(2,128)}, f32[1,2,4,128]{3,1,2,0:T(2,128)S(1)}, u32[]{:S(2)}) copy-start(f32[1,2,4,128]{3,1,2,0:T(2,128)S(1)} %copy.101) | copy-start | bytes 12292
  128.4 36.5 %copy-start.39 = (bf16[256,768]{1,0:T(8,128)(2,1)S(1)}, bf16[256,768]{1,0:T(8,128)(2,1)}, u32[]{:S(2)}) copy-start(bf16[256,768]{1,0:T(8,128)(2,1)} %copy-done.38) | copy-start | bytes 1179652
  128.4 36.6 %copy-start.41 = (bf16[256,768]{1,0:T(8,128)(2,1)S(1)}, bf16[256,768]{1,0:T(8,128)(2,1)}, u32[]{:S(2)}) copy-start(bf16[256,768]{1,0:T(8,128)(2,1)} %copy-done.40) | copy-start | bytes 1179652
  128.4 36.6 %copy-start.43 = (bf16[256,768]{1,0:T(8,128)(2,1)S(1)}, bf16[256,768]{1,0:T(8,128)(2,1)}, u32[]{:S(2)}) copy-start(bf16[256,768]{1,0:T(8,128)(2,1)} %copy-done.42) | copy-start | bytes 1179652
  176.9 196.2 %collective-permute-start.48 = (bf16[1536,768]{1,0:T(8,128)(2,1)}, bf16[1536,768]{1,0:T(8,128)(2,1)}, u32[]{:S(2)}, u32[]{:S(2)}) collective-permute-start(bf16[1536,768]{1,0:T(8,128)(2,1)} %dynamic-slice_bitcast_fusion.1), channel_id=1, source_target_pairs={{0,1},{1,0},{2,3},{3,2},{4,5},{5,4},{6,7},{7,6},{8,9},{9,8},{10,11... | collective-permute-start | bytes 7077896 | tf_op jit(solution)/shard_map/ppermute | solution.py:478
  178.0 36.5 %collective-permute-start.11 = (bf16[4,256,384]{1,2,0:T(8,128)(2,1)}, bf16[4,256,384]{1,2,0:T(8,128)(2,1)}, u32[]{:S(2)}, u32[]{:S(2)}) collective-permute-start(bf16[4,256,384]{1,2,0:T(8,128)(2,1)} %copy.78), channel_id=1, source_target_pairs={{0,1},{1,0},{2,3},{3,2},{4,5},{5,4},{6,7},{7,6},{8,9},{9,8},{10,11... | collective-permute-start | bytes 2359304 | tf_op jit(solution)/shard_map/ppermute | solution.py:478
  179.8 22.2 %collective-permute-start.8 = (bf16[256,768]{1,0:T(8,128)(2,1)}, bf16[256,768]{1,0:T(8,128)(2,1)}, u32[]{:S(2)}, u32[]{:S(2)}) collective-permute-start(bf16[256,768]{1,0:T(8,128)(2,1)} %get-tuple-element.153), channel_id=1, source_target_pairs={{0,2},{1,3},{2,0},{3,1},{4,6},{5,7},{6,4},{7,5},{8,10},{9,11},{10,... | collective-permute-start | bytes 1179656 | tf_op jit(solution)/shard_map/ppermute | solution.py:478
  181.5 23.1 %collective-permute-start.9 = (bf16[256,768]{1,0:T(8,128)(2,1)}, bf16[256,768]{1,0:T(8,128)(2,1)}, u32[]{:S(2)}, u32[]{:S(2)}) collective-permute-start(bf16[256,768]{1,0:T(8,128)(2,1)} %get-tuple-element.152), channel_id=1, source_target_pairs={{0,4},{1,5},{2,6},{3,7},{4,0},{5,1},{6,2},{7,3},{8,12},{9,13},{10,... | collective-permute-start | bytes 1179656 | tf_op jit(solution)/shard_map/ppermute | solution.py:478
  199.4 177.9 %collective-permute-start.38 = (bf16[384,3840]{1,0:T(8,128)(2,1)}, bf16[384,3840]{1,0:T(8,128)(2,1)}, u32[]{:S(2)}, u32[]{:S(2)}) collective-permute-start(bf16[384,3840]{1,0:T(8,128)(2,1)} %dynamic-slice_bitcast_fusion), channel_id=1, source_target_pairs={{0,1},{1,0},{2,3},{3,2},{4,5},{5,4},{6,7},{7,6},{8,9},{9,8},{10,11... | collective-permute-start | bytes 8847368 | tf_op jit(solution)/shard_map/ppermute | solution.py:478
  202.0 12.5 %collective-permute-start.10 = (bf16[256,768]{1,0:T(8,128)(2,1)S(1)}, bf16[256,768]{1,0:T(8,128)(2,1)S(1)}, u32[]{:S(2)}, u32[]{:S(2)}) collective-permute-start(bf16[256,768]{1,0:T(8,128)(2,1)S(1)} %copy-done.44), channel_id=1, source_target_pairs={{0,6},{1,7},{2,4},{3,5},{4,2},{5,3},{6,0},{7,1},{8,14},{9,15},{10,... | collective-permute-start | bytes 1179656 | tf_op jit(solution)/shard_map/ppermute | solution.py:478
  301.3 39.4 %collective-permute-start.21 = (bf16[384,768]{1,0:T(8,128)(2,1)S(1)}, bf16[384,768]{1,0:T(8,128)(2,1)S(1)}, u32[]{:S(2)}, u32[]{:S(2)}) collective-permute-start(bf16[384,768]{1,0:T(8,128)(2,1)S(1)} %dynamic-slice_bitcast_fusion.6), channel_id=1, source_target_pairs={{0,4},{1,5},{2,6},{3,7},{4,0},{5,1},{6,2},{7,3},{8,12},{9,13},{10,... | collective-permute-start | bytes 1769480 | tf_op jit(solution)/shard_map/ppermute | solution.py:478
  305.3 17.3 %collective-permute-start.29 = (bf16[384,384]{1,0:T(8,128)(2,1)S(1)}, bf16[384,384]{1,0:T(8,128)(2,1)S(1)}, u32[]{:S(2)}, u32[]{:S(2)}) collective-permute-start(bf16[384,384]{1,0:T(8,128)(2,1)S(1)} %dynamic-slice_bitcast_fusion.15), channel_id=1, source_target_pairs={{0,4},{1,5},{2,6},{3,7},{4,0},{5,1},{6,2},{7,3},{8,12},{9,13},{10,... | collective-permute-start | bytes 884744 | tf_op jit(solution)/shard_map/ppermute | solution.py:478
  313.0 60.1 %slice-start.2 = ((s8[4718592]{0:T(1024)(128)(4,1)}), s8[4194304]{0:T(1024)(128)(4,1)S(1)}, s32[]{:S(2)}) async-start(s8[4718592]{0:T(1024)(128)(4,1)} %bitcast.262), calls=%async_computation.2 | async-start | bytes 8388608
  313.2 67.2 %collective-permute-start.12 = (bf16[1024,768]{1,0:T(8,128)(2,1)S(1)}, bf16[1024,768]{1,0:T(8,128)(2,1)S(1)}, u32[]{:S(2)}, u32[]{:S(2)}) collective-permute-start(bf16[1024,768]{1,0:T(8,128)(2,1)S(1)} %slice.248), channel_id=1, source_target_pairs={{0,1},{1,0},{2,3},{3,2},{4,5},{5,4},{6,7},{7,6},{8,9},{9,8},{10,11... | collective-permute-start | bytes 4718600 | tf_op jit(solution)/shard_map/ppermute | solution.py:478
  322.7 5.2 collective-permute-start.30
  328.0 4.4 collective-permute-start.31
  332.5 5.2 collective-permute-start.32
  337.7 4.9 collective-permute-start.33
  340.9 8.4 %collective-permute-start.22 = (bf16[192,768]{1,0:T(8,128)(2,1)S(1)}, bf16[192,768]{1,0:T(8,128)(2,1)S(1)}, u32[]{:S(2)}, u32[]{:S(2)}) collective-permute-start(bf16[192,768]{1,0:T(8,128)(2,1)S(1)} %dynamic-slice_bitcast_fusion.16), channel_id=1, source_target_pairs={{0,2},{1,3},{2,0},{3,1},{4,6},{5,7},{6,4},{7,5},{8,10},{9,11},{10,... | collective-permute-start | bytes 884744 | tf_op jit(solution)/shard_map/ppermute | solution.py:478
  342.7 8.5 %collective-permute-start.34 = (bf16[96,384]{1,0:T(8,128)(2,1)S(1)}, bf16[96,384]{1,0:T(8,128)(2,1)S(1)}, u32[]{:S(2)}, u32[]{:S(2)}) collective-permute-start(bf16[96,384]{1,0:T(8,128)(2,1)S(1)} %pad_maximum_fusion.19), channel_id=1, source_target_pairs={{0,8},{8,0},{16,24},{24,16},{1,9},{9,1},{17,25},{25,17},{2,10},{10... | collective-permute-start | bytes 221192 | tf_op jit(solution)/shard_map/ppermute | solution.py:478
  349.4 6.0 %collective-permute-start.23 = (bf16[96,768]{1,0:T(8,128)(2,1)S(1)}, bf16[96,768]{1,0:T(8,128)(2,1)S(1)}, u32[]{:S(2)}, u32[]{:S(2)}) collective-permute-start(bf16[96,768]{1,0:T(8,128)(2,1)S(1)} %dynamic-slice_bitcast_fusion.20), channel_id=1, source_target_pairs={{0,8},{8,0},{16,24},{24,16},{1,9},{9,1},{17,25},{25,17},{2,10},{10... | collective-permute-start | bytes 442376 | tf_op jit(solution)/shard_map/ppermute | solution.py:478
  351.3 5.2 collective-permute-start.35
  355.5 6.1 %collective-permute-start.24 = (bf16[48,768]{1,0:T(8,128)(2,1)S(1)}, bf16[48,768]{1,0:T(8,128)(2,1)S(1)}, u32[]{:S(2)}, u32[]{:S(2)}) collective-permute-start(bf16[48,768]{1,0:T(8,128)(2,1)S(1)} %dynamic-slice_bitcast_fusion.22), channel_id=1, source_target_pairs={{0,16},{8,24},{16,0},{24,8},{1,17},{9,25},{17,1},{25,9},{2,18},{10... | collective-permute-start | bytes 221192 | tf_op jit(solution)/shard_map/ppermute | solution.py:478
  361.6 5.8 collective-permute-start.25
  361.7 6.8 %collective-permute-start.36 = (bf16[384,384]{1,0:T(8,128)(2,1)S(1)}, bf16[384,384]{1,0:T(8,128)(2,1)S(1)}, u32[]{:S(2)}, u32[]{:S(2)}) collective-permute-start(bf16[384,384]{1,0:T(8,128)(2,1)S(1)} %pad_maximum_fusion.15), channel_id=1, source_target_pairs={{0,4},{1,5},{2,6},{3,7},{4,0},{5,1},{6,2},{7,3},{8,12},{9,13},{10,... | collective-permute-start | bytes 884744 | tf_op jit(solution)/shard_map/ppermute | solution.py:478
  367.4 5.2 collective-permute-start.26
  372.7 88.1 %collective-permute-start.27 = (bf16[192,768]{1,0:T(8,128)(2,1)S(1)}, bf16[192,768]{1,0:T(8,128)(2,1)S(1)}, u32[]{:S(2)}, u32[]{:S(2)}) collective-permute-start(bf16[192,768]{1,0:T(8,128)(2,1)S(1)} %pad_maximum_fusion.14), channel_id=1, source_target_pairs={{0,2},{1,3},{2,0},{3,1},{4,6},{5,7},{6,4},{7,5},{8,10},{9,11},{10,... | collective-permute-start | bytes 884744 | tf_op jit(solution)/shard_map/ppermute | solution.py:478
  375.6 19.6 %collective-permute-start.49 = (bf16[768,768]{1,0:T(8,128)(2,1)S(1)}, bf16[768,768]{1,0:T(8,128)(2,1)S(1)}, u32[]{:S(2)}, u32[]{:S(2)}) collective-permute-start(bf16[768,768]{1,0:T(8,128)(2,1)S(1)} %dynamic-slice_bitcast_fusion.3), channel_id=1, source_target_pairs={{0,2},{1,3},{2,0},{3,1},{4,6},{5,7},{6,4},{7,5},{8,10},{9,11},{10,... | collective-permute-start | bytes 3538952 | tf_op jit(solution)/shard_map/ppermute | solution.py:478
  380.0 27.6 %collective-permute-start.39 = (bf16[192,3840]{1,0:T(8,128)(2,1)S(1)}, bf16[192,3840]{1,0:T(8,128)(2,1)S(1)}, u32[]{:S(2)}, u32[]{:S(2)}) collective-permute-start(bf16[192,3840]{1,0:T(8,128)(2,1)S(1)} %dynamic-slice_bitcast_fusion.2), channel_id=1, source_target_pairs={{0,4},{1,5},{2,6},{3,7},{4,0},{5,1},{6,2},{7,3},{8,12},{9,13},{10,... | collective-permute-start | bytes 4423688 | tf_op jit(solution)/shard_map/ppermute | solution.py:478
  383.5 37.6 %collective-permute-start.16 = (f32[9216]{0:T(1024)S(1)}, f32[9216]{0:T(1024)S(1)}, u32[]{:S(2)}, u32[]{:S(2)}) collective-permute-start(f32[9216]{0:T(1024)S(1)} %constant_dynamic-update-slice_fusion.6), channel_id=1, source_target_pairs={{0,1},{1,0},{2,3},{3,2},{4,5},{5,4},{6,7},{7,6},{8,9},{9,8},{10,11... | collective-permute-start | bytes 110600 | tf_op jit(solution)/shard_map/ppermute | solution.py:478
  395.6 18.4 %collective-permute-start.50 = (bf16[384,768]{1,0:T(8,128)(2,1)S(1)}, bf16[384,768]{1,0:T(8,128)(2,1)S(1)}, u32[]{:S(2)}, u32[]{:S(2)}) collective-permute-start(bf16[384,768]{1,0:T(8,128)(2,1)S(1)} %dynamic-slice_bitcast_fusion.5), channel_id=1, source_target_pairs={{0,4},{1,5},{2,6},{3,7},{4,0},{5,1},{6,2},{7,3},{8,12},{9,13},{10,... | collective-permute-start | bytes 1769480 | tf_op jit(solution)/shard_map/ppermute | solution.py:478
  408.1 11.5 %collective-permute-start.40 = (bf16[96,3840]{1,0:T(8,128)(2,1)S(1)}, bf16[96,3840]{1,0:T(8,128)(2,1)S(1)}, u32[]{:S(2)}, u32[]{:S(2)}) collective-permute-start(bf16[96,3840]{1,0:T(8,128)(2,1)S(1)} %dynamic-slice_bitcast_fusion.4), channel_id=1, source_target_pairs={{0,2},{1,3},{2,0},{3,1},{4,6},{5,7},{6,4},{7,5},{8,10},{9,11},{10,... | collective-permute-start | bytes 2211848 | tf_op jit(solution)/shard_map/ppermute | solution.py:478
  414.2 10.2 %collective-permute-start.51 = (bf16[192,768]{1,0:T(8,128)(2,1)S(1)}, bf16[192,768]{1,0:T(8,128)(2,1)S(1)}, u32[]{:S(2)}, u32[]{:S(2)}) collective-permute-start(bf16[192,768]{1,0:T(8,128)(2,1)S(1)} %dynamic-slice_bitcast_fusion.14), channel_id=1, source_target_pairs={{0,8},{8,0},{16,24},{24,16},{1,9},{9,1},{17,25},{25,17},{2,10},{10... | collective-permute-start | bytes 884744 | tf_op jit(solution)/shard_map/ppermute | solution.py:478
  419.8 15.3 %collective-permute-start.41 = (bf16[48,3840]{1,0:T(8,128)(2,1)S(1)}, bf16[48,3840]{1,0:T(8,128)(2,1)S(1)}, u32[]{:S(2)}, u32[]{:S(2)}) collective-permute-start(bf16[48,3840]{1,0:T(8,128)(2,1)S(1)} %dynamic-slice_bitcast_fusion.13), channel_id=1, source_target_pairs={{0,8},{8,0},{16,24},{24,16},{1,9},{9,1},{17,25},{25,17},{2,10},{10... | collective-permute-start | bytes 1105928 | tf_op jit(solution)/shard_map/ppermute | solution.py:478
  421.1 41.4 %collective-permute-start.17 = (f32[9216]{0:T(1024)S(1)}, f32[9216]{0:T(1024)S(1)}, u32[]{:S(2)}, u32[]{:S(2)}) collective-permute-start(f32[9216]{0:T(1024)S(1)} %add.507), channel_id=1, source_target_pairs={{0,2},{1,3},{2,0},{3,1},{4,6},{5,7},{6,4},{7,5},{8,10},{9,11},{10,... | collective-permute-start | bytes 110600 | tf_op jit(solution)/shard_map/ppermute | solution.py:478
  424.5 10.8 %collective-permute-start.52 = (bf16[96,768]{1,0:T(8,128)(2,1)S(1)}, bf16[96,768]{1,0:T(8,128)(2,1)S(1)}, u32[]{:S(2)}, u32[]{:S(2)}) collective-permute-start(bf16[96,768]{1,0:T(8,128)(2,1)S(1)} %dynamic-slice_bitcast_fusion.18), channel_id=1, source_target_pairs={{0,16},{8,24},{16,0},{24,8},{1,17},{9,25},{17,1},{25,9},{2,18},{10... | collective-permute-start | bytes 442376 | tf_op jit(solution)/shard_map/ppermute | solution.py:478
  435.3 9.3 %collective-permute-start.42 = (bf16[24,3840]{1,0:T(8,128)(2,1)S(1)}, bf16[24,3840]{1,0:T(8,128)(2,1)S(1)}, u32[]{:S(2)}, u32[]{:S(2)}) collective-permute-start(bf16[24,3840]{1,0:T(8,128)(2,1)S(1)} %dynamic-slice_bitcast_fusion.17), channel_id=1, source_target_pairs={{0,16},{8,24},{16,0},{24,8},{1,17},{9,25},{17,1},{25,9},{2,18},{10... | collective-permute-start | bytes 552968 | tf_op jit(solution)/shard_map/ppermute | solution.py:478
  435.4 10.8 %collective-permute-start.53 = (bf16[96,768]{1,0:T(8,128)(2,1)S(1)}, bf16[96,768]{1,0:T(8,128)(2,1)S(1)}, u32[]{:S(2)}, u32[]{:S(2)}) collective-permute-start(bf16[96,768]{1,0:T(8,128)(2,1)S(1)} %fusion.46), channel_id=1, source_target_pairs={{0,16},{8,24},{16,0},{24,8},{1,17},{9,25},{17,1},{25,9},{2,18},{10... | collective-permute-start | bytes 442376 | tf_op jit(solution)/shard_map/ppermute | solution.py:478
  444.7 6.9 %collective-permute-start.43 = (bf16[24,3840]{1,0:T(8,128)(2,1)S(1)}, bf16[24,3840]{1,0:T(8,128)(2,1)S(1)}, u32[]{:S(2)}, u32[]{:S(2)}) collective-permute-start(bf16[24,3840]{1,0:T(8,128)(2,1)S(1)} %fusion.45), channel_id=1, source_target_pairs={{0,16},{8,24},{16,0},{24,8},{1,17},{9,25},{17,1},{25,9},{2,18},{10... | collective-permute-start | bytes 552968 | tf_op jit(solution)/shard_map/ppermute | solution.py:478
  446.2 8.4 %collective-permute-start.54 = (bf16[192,768]{1,0:T(8,128)(2,1)S(1)}, bf16[192,768]{1,0:T(8,128)(2,1)S(1)}, u32[]{:S(2)}, u32[]{:S(2)}) collective-permute-start(bf16[192,768]{1,0:T(8,128)(2,1)S(1)} %pad_maximum_fusion.16), channel_id=1, source_target_pairs={{0,8},{8,0},{16,24},{24,16},{1,9},{9,1},{17,25},{25,17},{2,10},{10... | collective-permute-start | bytes 884744 | tf_op jit(solution)/shard_map/ppermute | solution.py:478
  451.7 8.0 %collective-permute-start.44 = (bf16[48,3840]{1,0:T(8,128)(2,1)S(1)}, bf16[48,3840]{1,0:T(8,128)(2,1)S(1)}, u32[]{:S(2)}, u32[]{:S(2)}) collective-permute-start(bf16[48,3840]{1,0:T(8,128)(2,1)S(1)} %pad_maximum_fusion.13), channel_id=1, source_target_pairs={{0,8},{8,0},{16,24},{24,16},{1,9},{9,1},{17,25},{25,17},{2,10},{10... | collective-permute-start | bytes 1105928 | tf_op jit(solution)/shard_map/ppermute | solution.py:478
  454.8 16.3 %collective-permute-start.55 = (bf16[384,768]{1,0:T(8,128)(2,1)S(1)}, bf16[384,768]{1,0:T(8,128)(2,1)S(1)}, u32[]{:S(2)}, u32[]{:S(2)}) collective-permute-start(bf16[384,768]{1,0:T(8,128)(2,1)S(1)} %pad_maximum_fusion.12), channel_id=1, source_target_pairs={{0,4},{1,5},{2,6},{3,7},{4,0},{5,1},{6,2},{7,3},{8,12},{9,13},{10,... | collective-permute-start | bytes 1769480 | tf_op jit(solution)/shard_map/ppermute | solution.py:478
  459.8 14.5 %collective-permute-start.45 = (bf16[96,3840]{1,0:T(8,128)(2,1)S(1)}, bf16[96,3840]{1,0:T(8,128)(2,1)S(1)}, u32[]{:S(2)}, u32[]{:S(2)}) collective-permute-start(bf16[96,3840]{1,0:T(8,128)(2,1)S(1)} %pad_maximum_fusion.10), channel_id=1, source_target_pairs={{0,2},{1,3},{2,0},{3,1},{4,6},{5,7},{6,4},{7,5},{8,10},{9,11},{10,... | collective-permute-start | bytes 2211848 | tf_op jit(solution)/shard_map/ppermute | solution.py:478
  460.9 25.8 %collective-permute-start.28 = (bf16[384,768]{1,0:T(8,128)(2,1)S(1)}, bf16[384,768]{1,0:T(8,128)(2,1)S(1)}, u32[]{:S(2)}, u32[]{:S(2)}) collective-permute-start(bf16[384,768]{1,0:T(8,128)(2,1)S(1)} %pad_maximum_fusion.11), channel_id=1, source_target_pairs={{0,4},{1,5},{2,6},{3,7},{4,0},{5,1},{6,2},{7,3},{8,12},{9,13},{10,... | collective-permute-start | bytes 1769480 | tf_op jit(solution)/shard_map/ppermute | solution.py:478
  462.5 19.0 %collective-permute-start.18 = (f32[9216]{0:T(1024)S(1)}, f32[9216]{0:T(1024)S(1)}, u32[]{:S(2)}, u32[]{:S(2)}) collective-permute-start(f32[9216]{0:T(1024)S(1)} %add.508), channel_id=1, source_target_pairs={{0,4},{1,5},{2,6},{3,7},{4,0},{5,1},{6,2},{7,3},{8,12},{9,13},{10,... | collective-permute-start | bytes 110600 | tf_op jit(solution)/shard_map/ppermute | solution.py:478
  471.3 17.0 %collective-permute-start.56 = (bf16[768,768]{1,0:T(8,128)(2,1)S(1)}, bf16[768,768]{1,0:T(8,128)(2,1)S(1)}, u32[]{:S(2)}, u32[]{:S(2)}) collective-permute-start(bf16[768,768]{1,0:T(8,128)(2,1)S(1)} %pad_maximum_fusion.9), channel_id=1, source_target_pairs={{0,2},{1,3},{2,0},{3,1},{4,6},{5,7},{6,4},{7,5},{8,10},{9,11},{10,... | collective-permute-start | bytes 3538952 | tf_op jit(solution)/shard_map/ppermute | solution.py:478
  474.7 22.7 %collective-permute-start.46 = (bf16[192,3840]{1,0:T(8,128)(2,1)S(1)}, bf16[192,3840]{1,0:T(8,128)(2,1)S(1)}, u32[]{:S(2)}, u32[]{:S(2)}) collective-permute-start(bf16[192,3840]{1,0:T(8,128)(2,1)S(1)} %pad_maximum_fusion.7), channel_id=1, source_target_pairs={{0,4},{1,5},{2,6},{3,7},{4,0},{5,1},{6,2},{7,3},{8,12},{9,13},{10,... | collective-permute-start | bytes 4423688 | tf_op jit(solution)/shard_map/ppermute | solution.py:478
  481.6 4.0 collective-permute-start.19
  481.7 22.6 %collective-permute-start.13 = (bf16[256,768]{1,0:T(8,128)(2,1)S(1)}, bf16[256,768]{1,0:T(8,128)(2,1)S(1)}, u32[]{:S(2)}, u32[]{:S(2)}) collective-permute-start(bf16[256,768]{1,0:T(8,128)(2,1)S(1)} %get-tuple-element.150), channel_id=1, source_target_pairs={{0,2},{1,3},{2,0},{3,1},{4,6},{5,7},{6,4},{7,5},{8,10},{9,11},{10,... | collective-permute-start | bytes 1179656 | tf_op jit(solution)/shard_map/ppermute | solution.py:478
  485.5 16.1 %collective-permute-start.20 = (f32[9216]{0:T(1024)S(1)}, f32[9216]{0:T(1024)S(1)}, u32[]{:S(2)}, u32[]{:S(2)}) collective-permute-start(f32[9216]{0:T(1024)S(1)} %add.510), channel_id=1, source_target_pairs={{0,16},{8,24},{16,0},{24,8},{1,17},{9,25},{17,1},{25,9},{2,18},{10... | collective-permute-start | bytes 110600 | tf_op jit(solution)/shard_map/ppermute | solution.py:478
  488.3 38.7 %collective-permute-start.37 = (bf16[768,1152]{1,0:T(8,128)(2,1)}, bf16[768,1152]{1,0:T(8,128)(2,1)}, u32[]{:S(2)}, u32[]{:S(2)}) collective-permute-start(bf16[768,1152]{1,0:T(8,128)(2,1)} %maximum_maximum_fusion), channel_id=1, source_target_pairs={{0,1},{1,0},{2,3},{3,2},{4,5},{5,4},{6,7},{7,6},{8,9},{9,8},{10,11... | collective-permute-start | bytes 5308424 | tf_op jit(solution)/shard_map/ppermute | solution.py:478
  491.0 74.4 %collective-permute-start.57 = (bf16[1536,768]{1,0:T(8,128)(2,1)}, bf16[1536,768]{1,0:T(8,128)(2,1)}, u32[]{:S(2)}, u32[]{:S(2)}) collective-permute-start(bf16[1536,768]{1,0:T(8,128)(2,1)} %pad_maximum_fusion.3), channel_id=1, source_target_pairs={{0,1},{1,0},{2,3},{3,2},{4,5},{5,4},{6,7},{7,6},{8,9},{9,8},{10,11... | collective-permute-start | bytes 7077896 | tf_op jit(solution)/shard_map/ppermute | solution.py:478
  499.6 73.4 %collective-permute-start.47 = (bf16[384,3840]{1,0:T(8,128)(2,1)}, bf16[384,3840]{1,0:T(8,128)(2,1)}, u32[]{:S(2)}, u32[]{:S(2)}) collective-permute-start(bf16[384,3840]{1,0:T(8,128)(2,1)} %pad_maximum_fusion.2), channel_id=1, source_target_pairs={{0,1},{1,0},{2,3},{3,2},{4,5},{5,4},{6,7},{7,6},{8,9},{9,8},{10,11... | collective-permute-start | bytes 8847368 | tf_op jit(solution)/shard_map/ppermute | solution.py:478
  501.7 20.0 %collective-permute-start.14 = (bf16[256,768]{1,0:T(8,128)(2,1)S(1)}, bf16[256,768]{1,0:T(8,128)(2,1)S(1)}, u32[]{:S(2)}, u32[]{:S(2)}) collective-permute-start(bf16[256,768]{1,0:T(8,128)(2,1)S(1)} %get-tuple-element.149), channel_id=1, source_target_pairs={{0,4},{1,5},{2,6},{3,7},{4,0},{5,1},{6,2},{7,3},{8,12},{9,13},{10,... | collective-permute-start | bytes 1179656 | tf_op jit(solution)/shard_map/ppermute | solution.py:478
  504.3 18.1 %collective-permute-start.15 = (bf16[256,768]{1,0:T(8,128)(2,1)S(1)}, bf16[256,768]{1,0:T(8,128)(2,1)S(1)}, u32[]{:S(2)}, u32[]{:S(2)}) collective-permute-start(bf16[256,768]{1,0:T(8,128)(2,1)S(1)} %get-tuple-element.148), channel_id=1, source_target_pairs={{0,6},{1,7},{2,4},{3,5},{4,2},{5,3},{6,0},{7,1},{8,14},{9,15},{10,... | collective-permute-start | bytes 1179656 | tf_op jit(solution)/shard_map/ppermute | solution.py:478
  (62 other events, 492.9 us)

commit v3 on v2

--- a/solution.py
+++ b/solution.py
@@ -311,7 +311,7 @@
     act_ref, hidden_ref, grad_upper_ref, layer_ref, grad_resid_ref, grad_attn_ref = refs[:6]
     refs = refs[6:]
     grad_mixed_refs, refs = refs[:parts], refs[parts:]
-    sums_ref, up_sum_ref, cot_sc, layer_sc, back_sc = refs
+    sums_ref, up_sum_ref, layer_sc, back_sc = refs
     first = pl.program_id(0) == 0
 
     @pl.when(first)
@@ -409,7 +409,6 @@
             + [head_slab] * parts
             + [pl.BlockSpec((8, model), still), pl.BlockSpec((8, wide), still)],
             scratch_shapes=[
-                pltpu.VMEM((8, 128), F32),
                 pltpu.VMEM((size, model), F32),
                 pltpu.VMEM((size, model), F32),
             ],
@@ -438,6 +437,90 @@
         vectors["out_bias"], vectors["gain"], vectors["shift"], up_bias, vectors["down_bias"],
     )
     return out[:6], out[6 : 6 + parts], out[6 + parts], out[7 + parts]
+
+
+def join_kernel(splits, bit_ref, mine_ref, other_ref, *out_refs):
+    mine = pl.program_id(0) == bit_ref[0]
+    begin = 0
+    for out_ref, count in zip(out_refs, splits):
+        lanes = slice(begin, begin + count)
+        out_ref[...] = jnp.where(mine, mine_ref[:, lanes], other_ref[:, lanes]).astype(F32)
+        begin += count
+
+
+def join(mine, other, bit, splits):
+    count, columns = mine.shape
+    tall = next(t for t in (192, 96, 48, count) if count % t == 0)
+    steps = count // tall
+
+    def mine_map(h, i, b):
+        return jnp.where(h == b[0], i, jnp.where(h < b[0], 0, steps - 1)), 0
+
+    def other_map(h, i, b):
+        return jnp.where(h != b[0], i, jnp.where(h < 1 - b[0], 0, steps - 1)), 0
+
+    return pl.pallas_call(
+        functools.partial(join_kernel, splits),
+        grid_spec=pltpu.PrefetchScalarGridSpec(
+            num_scalar_prefetch=1,
+            grid=(2, steps),
+            in_specs=[
+                pl.BlockSpec((tall, columns), mine_map),
+                pl.BlockSpec((tall, columns), other_map),
+            ],
+            out_specs=[
+                pl.BlockSpec((tall, n), lambda h, i, b: (h * steps + i, 0)) for n in splits
+            ],
+        ),
+        out_shape=[jax.ShapeDtypeStruct((2 * count, n), F32) for n in splits],
+        compiler_params=pltpu.CompilerParams(
+            dimension_semantics=("arbitrary", "arbitrary"), vmem_limit_bytes=VMEM_LIMIT
+        ),
+        cost_estimate=pl.CostEstimate(
+            flops=2 * count * columns, transcendentals=0, bytes_accessed=12 * count * columns
+        ),
+        name="join",
+    )(bit.reshape(1), mine, other)
+
+
+def spread_kernel(parts, spans, part_ref, *refs):
+    out_ref, refs = refs[-1], refs[:-1]
+    part = part_ref[0]
+    begin = 0
+    for which in range(3):
+        for p in range(parts):
+            for g, span in enumerate(spans):
+                piece = None
+                for s in range(parts):
+                    here = refs[s * len(spans) + g][:, which * span : (which + 1) * span]
+                    piece = here if piece is None else jnp.where((part ^ p) == s, here, piece)
+                out_ref[:, begin : begin + span] = piece.astype(F32)
+                begin += span
+
+
+def spread(pieces, part, spans):
+    parts = len(pieces)
+    count = pieces[0][0].shape[0]
+    tall = next(t for t in (192, 96, 48, count) if count % t == 0)
+    flat = [p for piece in pieces for p in piece]
+    columns = 3 * parts * sum(spans)
+    return pl.pallas_call(
+        functools.partial(spread_kernel, parts, spans),
+        grid_spec=pltpu.PrefetchScalarGridSpec(
+            num_scalar_prefetch=1,
+            grid=(count // tall,),
+            in_specs=[pl.BlockSpec((tall, p.shape[1]), lambda i, b: (i, 0)) for p in flat],
+            out_specs=pl.BlockSpec((tall, columns), lambda i, b: (i, 0)),
+        ),
+        out_shape=jax.ShapeDtypeStruct((count, columns), F32),
+        compiler_params=pltpu.CompilerParams(
+            dimension_semantics=("arbitrary",), vmem_limit_bytes=VMEM_LIMIT
+        ),
+        cost_estimate=pl.CostEstimate(
+            flops=count * columns, transcendentals=0, bytes_accessed=6 * count * columns
+        ),
+        name="spread",
+    )(part.reshape(1), *flat)
 
 
 def row_layout(sizes, prefixes, lens, padding, length, size):
@@ -568,13 +651,12 @@
     def as_row(vector):
         return vector.astype(F32).reshape(1, -1)
 
-    group = 2 if heads % 2 == 0 else heads
-    starts = list(range(0, heads, group))
-    span = group * HEAD_DIM
+    groups = [(0, 4), (4, 2)] if heads == 6 else [(0, heads)]
+    spans = [count * HEAD_DIM for _, count in groups]
     w_mine = jnp.concatenate([my_columns(n) for n in range(3)], axis=1)
     w_groups = [
-        jnp.concatenate([my_columns(n, h * HEAD_DIM, span) for n in range(3)], axis=1)
-        for h in starts
+        jnp.concatenate([my_columns(n, h * HEAD_DIM, c * HEAD_DIM) for n in range(3)], axis=1)
+        for h, c in groups
     ]
     bias_q = lax.dynamic_slice_in_dim(query_bias, part * width, width, 0)
     bias_v = lax.dynamic_slice_in_dim(value_bias, part * width, width, 0)
@@ -589,6 +671,7 @@
     mixed_all, out_t, lse = attention_forward(
         phys, flags, query_t, key, value_t, info, heads
     )
+    mixed_all, own_cotangent = lax.optimization_barrier((mixed_all, own_cotangent))
     mixed_parts = []
     for s in range(parts):
         piece = mixed_all[s * rows : (s + 1) * rows]
@@ -619,11 +702,9 @@
     row_steps = [(row_axis, m, (row_place // m) % 2) for m in bits(lax.axis_size(row_axis))]
     own_steps = [("pos", m * parts, (owner // m) % 2) for m in bits(rows)]
     part_steps = [("pos", m, (part // m) % 2) for m in bits(parts)]
-    one_way = part_steps + own_steps + row_steps
-    other_way = part_steps + own_steps[::-1] + row_steps
 
     grad_w_down = matmul(flat(hidden), flat(own_cotangent), TN).astype(BF16)
-    share_down = halve(grad_w_down, one_way)
+    share_down = halve(grad_w_down, part_steps)
     stacked = jnp.stack(mixed_parts)
     mixed = jnp.concatenate([flat(take(stacked, g ^ part)) for g in range(parts)], axis=1)
     grad_w_up = jnp.concatenate(
@@ -633,17 +714,30 @@
         ],
         axis=1,
     )
-    share_up = halve(grad_w_up, other_way)
-
-    grads = [
-        attention_backward(
-            phys, flags, query_t, grad_t, out_t, lse, info, key, key_t, value, group, h
+    share_up = halve(grad_w_up, part_steps)
+    rest_down, rest_up = own_steps + row_steps, own_steps[::-1] + row_steps
+
+    grads = []
+    stage = 0
+    for h, count in groups:
+        grad_t, share_down, share_up, grads, layer_home = lax.optimization_barrier(
+            (grad_t, share_down, share_up, grads, layer_home)
         )
-        for h in starts
-    ]
-    sum_w_down = double(share_down, one_way).astype(F32)
-    sum_up = double(share_up, other_way)
-    sum_w_up, sum_w_out = sum_up[:, : w_up.shape[1]].astype(F32), sum_up[:, w_up.shape[1] :].astype(F32)
+        grads = grads + [
+            attention_backward(
+                phys, flags, query_t, grad_t, out_t, lse, info, key, key_t, value, count, h
+            )
+        ]
+        share_down = halve(share_down, rest_down[stage : stage + 1])
+        share_up = halve(share_up, rest_up[stage : stage + 1])
+        stage += 1
+    share_down = double(halve(share_down, rest_down[stage:]), part_steps[1:] + rest_down)
+    share_up = double(halve(share_up, rest_up[stage:]), part_steps[1:] + rest_up)
+    axis, mask, bit = part_steps[0]
+    (sum_w_down,) = join(share_down, swap(share_down, axis, mask), bit, (model,))
+    sum_w_up, sum_w_out = join(
+        share_up, swap(share_up, axis, mask), bit, (w_up.shape[1], model)
+    )
 
     grad_act = sum(matmul(flat(g), w, NT) for g, w in zip(grads, w_groups))
     grad_act_own = grad_act[:local]
@@ -655,20 +749,22 @@
     grad_input_norm, grad_attn_gain, grad_attn_shift = norm_one_pull(grad_act_own)
     tokens_grad = (flat(grad_resid) + grad_input_norm).astype(BF16).reshape(rows, size, model)
 
-    steps = other_way[len(part_steps) :]
     summed = []
-    for batch in (grads[:-1], grads[-1:]):
-        if batch:
-            share = jnp.concatenate([matmul(flat(act_one), flat(g), TN).astype(BF16) for g in batch], axis=1)
-            summed.append(double(halve(share, steps), steps))
-    summed_mine = jnp.concatenate(summed, axis=1)
-    pieces = [summed_mine] + [swap(summed_mine, "pos", s) for s in range(1, parts)]
-    pieces = jnp.stack(pieces).reshape(parts, model, len(starts), 3, span)
-    pieces = jnp.stack([take(pieces, g ^ part) for g in range(parts)], axis=3)
-    sum_w_qkv = pieces.transpose(0, 2, 3, 1, 4).reshape(model, 3 * model).astype(F32)
-
-    grad_query_mine = jnp.concatenate([jnp.sum(flat(g)[:, :span].astype(F32), axis=0) for g in grads])
-    grad_value_mine = jnp.concatenate([jnp.sum(flat(g)[:, 2 * span :].astype(F32), axis=0) for g in grads])
+    for g in grads:
+        share = matmul(flat(act_one), flat(g), TN).astype(BF16)
+        summed.append(double(halve(share, rest_up), rest_up))
+    pieces = [summed] + [[swap(g, "pos", s) for g in summed] for s in range(1, parts)]
+    sum_w_qkv = spread(pieces, part, spans)
+
+    def column_sums(which):
+        return jnp.concatenate(
+            [
+                jnp.sum(flat(g)[:, which * n : (which + 1) * n].astype(F32), axis=0)
+                for g, n in zip(grads, spans)
+            ]
+        )
+
+    grad_query_mine, grad_value_mine = column_sums(0), column_sums(2)
 
     def placed(values):
         return lax.dynamic_update_slice_in_dim(jnp.zeros((model,), F32), values, part * width, 0)
@@ -683,7 +779,7 @@
             up_sum[0],
         ]
     )
-    for axis, mask, _ in one_way:
+    for axis, mask, _ in part_steps + rest_down:
         small = small + swap(small, axis, mask)
     vectors = small[: 8 * model].reshape(8, model)
     return (

time: 589 us -> 541 us (0.919)
  local copies, waits for them, and re-layouts: 83.2 us -> 52.5 us
  other arithmetic: 66.2 us -> 43.2 us
  starting transfers between devices: 52.2 us -> 70.3 us
  waiting for transfers between devices: 168 us -> 153 us
  Pallas kernels: 171 us -> 179 us
    pallas_call x0 -> x3, Pallas kernels: none -> 24.6 us  [the longest x2 19.2 us: join(): pl.pallas_call(functools.partial(join_kernel, splits), grid_spec=pltpu.Pr...]
    ppermute x58 -> x59, starting transfers between devices: 52.2 us -> 70.3 us  [swap(): return lax.ppermute(values, axis, [(i, i ^ mask) for i in range(count)])]
    convert_element_type x4 -> x0, other arithmetic: 16.5 us -> none  [the longest x1 5.43 us: per_device(): pieces.transpose(0, 2, 3, 1, 4).reshape(model, 3 * model).astype(F32)]
    ppermute x58 -> x59, waiting for transfers between devices: 168 us -> 153 us  [swap(): return lax.ppermute(values, axis, [(i, i ^ mask) for i in range(count)])]
    pallas_call x3 -> x2, Pallas kernels: 73.7 us -> 60.8 us  [attention_backward(): pl.pallas_call(functools.partial(backward_kernel, heads, first, blocks),...]
    convert_element_type x1 -> x0, local copies, waits for them, and re-layouts: 8.29 us -> none  [per_device(): pieces.transpose(0, 2, 3, 1, 4).reshape(model, 3 * model).astype(F32)]
    dynamic_slice x6 -> x4, local copies, waits for them, and re-layouts: 8.73 us -> 1.05 us  [take(): return lax.dynamic_index_in_dim(values, index, 0, keepdims=False)]
    convert_element_type x18, other arithmetic: 6.69 us -> 13.1 us  [halve(): (take(two, bit).astype(F32) + arrived.astype(F32)).astype(values.dtype)]
  transfers between devices with their start and end apart: 58 -> 59, of which waited for: 32 -> 24; matrix products, arithmetic and copies ran while one was open for 26% -> 14% of each run, Pallas kernels for 13% -> 21%
where the time goes in v3:
time: 541 us; the launch traced here: 535 us
  Pallas kernels  179 us (33%)
  waiting for transfers between devices  153 us (28%)
  starting transfers between devices  70.3 us (13%)
  local copies, waits for them, and re-layouts  52.5 us (10%)
  other arithmetic  43.2 us (8%)
  matrix products  28.7 us (5%)
  between operations  8.32 us (2%)
    ppermute x59, waiting for transfers between devices, swap(): return lax.ppermute(values, axis, [(i, i ^ mask) for i in range(count)])  153 us
    ppermute x59, starting transfers between devices, swap(): return lax.ppermute(values, axis, [(i, i ^ mask) for i in range(count)])  70.3 us
    pallas_call x2, Pallas kernels, attention_backward(): pl.pallas_call(functools.partial(backward_kernel, heads, first, blocks),...  60.8 us
    pallas_call x1, Pallas kernels, attention_forward(): pl.pallas_call(functools.partial(forward_kernel, heads, blocks), grid_spe...  44.7 us
    pallas_call x1, Pallas kernels, feed(): pl.pallas_call(body, grid_spec=pltpu.PrefetchScalarGridSpec(num_scalar_pr...  36.6 us
    dot_general x7, matrix products, matmul(): return lax.dot_general(left, right, dims, preferred_element_type=F32)  28.7 us
    pallas_call x2, Pallas kernels, join(): pl.pallas_call(functools.partial(join_kernel, splits), grid_spec=pltpu.Pr...  19.2 us
    unnamed x112, local copies, waits for them, and re-layouts  14.1 us
  transfers between devices with their start and end apart: 59, of which 24 were waited for; matrix products, arithmetic and copies ran while one was open for 14% of the time, Pallas kernels for 21%

profile of v3, /device:TPU:0, one launch (start us, length us, event | category | flops | bytes accessed | tf_op | source)
XLA Modules:
  0.0 534.8 jit_solution(5317676957080510596)
XLA Ops:
  0.7 2.2 dynamic-slice_bitcast_fusion.10
  3.0 3.0 collective-permute-start
  16.0 1.9 select_select_fusion
  23.0 1.9 collective-permute-done.1
  32.9 2.7 fusion.43
  49.3 12.5 %project.1 = (bf16[8,256,768]{2,1,0:T(8,128)(2,1)}, bf16[8,384,256]{2,1,0:T(8,128)(2,1)}, bf16[8,256,384]{2,1,0:T(8,128)(2,1)}, bf16[8,384,256]{2,1,0:T(8,128)(2...) custom-call(bf16[8,256,768]{2,1,0:T(8,128)(2,1)} %copy-done.36, f32[1,768]{1,0:T(1,128)} %reshape.564.gain_ref, ...), custom_call_target="tpu_custom_call" | custom-call | flops 3623878656 | bytes 14155776 | tf_op jit(solution)/shard_map/project/pallas_call | solution.py:274
  61.8 44.7 %attention_forward.1 = (bf16[8,256,384]{2,1,0:T(8,128)(2,1)}, f32[8,384,256]{2,1,0:T(8,128)}, f32[8,8,256]{2,1,0:T(8,128)}) custom-call(s32[8]{0:T(128)} %fusion.62.phys_ref, s32[64]{0:T(128)} %reshape.607.flag_ref, bf16[8,384,256]{2,1,0:T(8,128)(2,1)} %get-tuple-element.50.query_t_ref, bf16[8,256,384]{2,1,0:T(8,128)(2,1)} %get-tuple-element.51.key_ref, ...), custom_call_target="tpu_custom_call" | custom-call | flops 7247757312 | bytes 12582912 | tf_op jit(solution)/shard_map/attention_forward/pallas_call | solution.py:125
  113.7 36.6 %feed.1 = (bf16[4,256,768]{2,1,0:T(8,128)(2,1)}, bf16[4,256,3072]{2,1,0:T(8,128)(2,1)}, bf16[4,256,3072]{2,1,0:T(8,128)(2,1)}, bf16[4,256,768]{2,1,0:T(8,128)(2,...) custom-call(s32[1]{0:T(128)} %bitcast.p_ref.part_ref, ...), custom_call_target="tpu_custom_call" | custom-call | flops 21743271936 | bytes 25165824 | tf_op jit(solution)/shard_map/feed/pallas_call | solution.py:391
  150.3 8.9 %bitcast_convert_fusion.1 = bf16[3072,768]{1,0:T(8,128)(2,1)S(1)} fusion(bf16[4,256,3072]{2,1,0:T(8,128)(2,1)} %get-tuple-element.59, bf16[4,256,768]{2,1,0:T(8,128)(2,1)S(1)} %copy-done.16), kind=kOutput, calls=%fused_computation.1 | convolution fusion | flops 4834197504 | bytes 12582912 | tf_op jit(solution)/shard_map/dot_general | solution.py:32
  162.5 5.4 %bitcast_convert_fusion = bf16[768,3072]{1,0:T(8,128)(2,1)S(1)} fusion(bf16[4,256,768]{2,1,0:T(8,128)(2,1)S(1)} %copy-done.50, bf16[4,256,3072]{2,1,0:T(8,128)(2,1)S(1)} %copy-done.49), kind=kOutput, calls=%fused_computation | convolution fusion | flops 4834197504 | bytes 12582912 | tf_op jit(solution)/shard_map/dot_general | solution.py:32
  169.4 2.5 fusion.9
  173.5 2.0 dynamic-slice_bitcast_fusion
  177.1 1.8 constant_dynamic-slice_fusion.2
  178.9 2.5 constant_dynamic-slice_fusion.5
  185.8 3.0 collective-permute-start.12
  190.9 4.6 collective-permute-done.11
  195.4 3.2 collective-permute-start.13
  199.4 1.8 bitcast_dynamic-update-slice_fusion.4
  201.2 6.6 %collective-permute-done.13 = bf16[256,768]{1,0:T(8,128)(2,1)S(1)} collective-permute-done((bf16[256,768]{1,0:T(8,128)(2,1)}, bf16[256,768]{1,0:T(8,128)(2,1)S(1)}, u32[]{:S(2)}, u32[]{:S(2)}) %collective-permute-start.13) | collective-permute-done | bytes 393248 | tf_op jit(solution)/shard_map/ppermute | solution.py:561
  208.5 2.4 maximum_bitcast_fusion.grad_t_ref
  211.0 3.0 fusion.1
  214.0 4.2 fusion
  220.2 2.6 collective-permute-start.15
  223.7 37.7 %attention_backward.2 = bf16[8,256,768]{2,1,0:T(8,128)(2,1)} custom-call(s32[8]{0:T(128)} %fusion.62.phys_ref, s32[64]{0:T(128)} %reshape.607.flag_ref, bf16[8,384,256]{2,1,0:T(8,128)(2,1)} %get-tuple-element.50.query_t_ref, bf16[8,384,256]{2,1,0:T(8,128)(2,1)} %maximum_bitcast_fusion.grad_t_ref, f32[8,384,256]{2,1,0:T(8,128)} %get-tuple-element.67.out_t_ref, ...), custom_call_target="tpu_custom_call" | custom-call | flops 12079595520 | bytes 10485760 | tf_op jit(solution)/shard_map/attention_backward/pallas_call | solution.py:234
  261.5 3.1 fusion.4
  266.3 23.1 %attention_backward.3 = bf16[8,256,384]{2,1,0:T(8,128)(2,1)} custom-call(s32[8]{0:T(128)} %fusion.62.phys_ref, s32[64]{0:T(128)} %reshape.607.flag_ref, bf16[8,384,256]{2,1,0:T(8,128)(2,1)} %get-tuple-element.50.query_t_ref, bf16[8,384,256]{2,1,0:T(8,128)(2,1)} %maximum_bitcast_fusion.grad_t_ref, f32[8,384,256]{2,1,0:T(8,128)} %get-tuple-element.67.out_t_ref, ...), custom_call_target="tpu_custom_call" | custom-call | flops 6039797760 | bytes 5242880 | tf_op jit(solution)/shard_map/attention_backward/pallas_call | solution.py:234
  289.4 5.7 %bitcast_convert_fusion.2 = bf16[768,768]{1,0:T(8,128)(2,1)S(1)} fusion(bf16[8,256,768]{2,1,0:T(8,128)(2,1)} %get-tuple-element.78, bf16[8,256,768]{2,1,0:T(8,128)(2,1)} %attention_backward.2), kind=kOutput, calls=%fused_computation.25 | convolution fusion | flops 2416508928 | bytes 7471104 | tf_op jit(solution)/shard_map/dot_general | solution.py:32
  295.1 1.8 fusion.13
  297.3 2.7 fusion.14
  300.0 1.8 convolution_add_fusion
  302.2 2.1 collective-permute-start.33
  305.3 2.1 collective-permute-start.51
  307.7 17.0 %collective-permute-done.33 = bf16[384,384]{1,0:T(8,128)(2,1)S(1)} collective-permute-done((bf16[384,384]{1,0:T(8,128)(2,1)S(1)}, bf16[384,384]{1,0:T(8,128)(2,1)S(1)}, u32[]{:S(2)}, u32[]{:S(2)}) %collective-permute-start.33) | collective-permute-done | bytes 294944 | tf_op jit(solution)/shard_map/ppermute | solution.py:561
  326.0 4.0 collective-permute-done.34
  330.1 2.2 collective-permute-start.35
  332.4 2.2 collective-permute-done.35
  334.7 9.9 %collective-permute-start.36 = (bf16[48,384]{1,0:T(8,128)(2,1)S(1)}, bf16[48,384]{1,0:T(8,128)(2,1)S(1)}, u32[]{:S(2)}, u32[]{:S(2)}) collective-permute-start(bf16[48,384]{1,0:T(8,128)(2,1)S(1)} %dynamic-slice_bitcast_fusion.23), channel_id=1, source_target_pairs={{0,16},{8,24},{16,0},{24,8},{1,17},{9,25},{17,1},{25,9},{2,18},{10... | collective-permute-start | bytes 110600 | tf_op jit(solution)/shard_map/ppermute | solution.py:561
  346.6 3.0 collective-permute-start.37
  349.8 2.1 collective-permute-start.26
  352.2 2.1 collective-permute-start.52
  354.3 2.8 collective-permute-done.38
  357.2 2.1 collective-permute-start.39
  359.6 2.8 collective-permute-done.39
  366.7 8.6 %collective-permute-done.27 = bf16[96,768]{1,0:T(8,128)(2,1)S(1)} collective-permute-done((bf16[96,768]{1,0:T(8,128)(2,1)S(1)}, bf16[96,768]{1,0:T(8,128)(2,1)S(1)}, u32[]{:S(2)}, u32[]{:S(2)}) %collective-permute-start.27) | collective-permute-done | bytes 147488 | tf_op jit(solution)/shard_map/ppermute | solution.py:561
  375.8 2.7 collective-permute-start.54
  378.5 3.8 collective-permute-done.28
  382.5 3.0 collective-permute-start.45
  385.7 3.0 collective-permute-done.54
  391.1 3.0 collective-permute-done.45
  394.7 8.7 %collective-permute-done.30 = bf16[96,768]{1,0:T(8,128)(2,1)S(1)} collective-permute-done((bf16[96,768]{1,0:T(8,128)(2,1)S(1)}, bf16[96,768]{1,0:T(8,128)(2,1)S(1)}, u32[]{:S(2)}, u32[]{:S(2)}) %collective-permute-start.30) | collective-permute-done | bytes 147488 | tf_op jit(solution)/shard_map/ppermute | solution.py:561
  403.7 2.7 collective-permute-start.56
  406.6 1.8 multiply_reduce_fusion
  408.5 7.1 %collective-permute-done.47 = bf16[48,3840]{1,0:T(8,128)(2,1)S(1)} collective-permute-done((bf16[48,3840]{1,0:T(8,128)(2,1)S(1)}, bf16[48,3840]{1,0:T(8,128)(2,1)S(1)}, u32[]{:S(2)}, u32[]{:S(2)}) %collective-permute-start.47) | collective-permute-done | bytes 368672 | tf_op jit(solution)/shard_map/ppermute | solution.py:561
  416.1 15.6 %collective-permute-done.48 = bf16[96,3840]{1,0:T(8,128)(2,1)S(1)} collective-permute-done((bf16[96,3840]{1,0:T(8,128)(2,1)S(1)}, bf16[96,3840]{1,0:T(8,128)(2,1)S(1)}, u32[]{:S(2)}, u32[]{:S(2)}) %collective-permute-start.48) | collective-permute-done | bytes 737312 | tf_op jit(solution)/shard_map/ppermute | solution.py:561
  435.2 1.8 collective-permute-start.57
  437.0 26.1 %collective-permute-done.49 = bf16[192,3840]{1,0:T(8,128)(2,1)S(1)} collective-permute-done((bf16[192,3840]{1,0:T(8,128)(2,1)S(1)}, bf16[192,3840]{1,0:T(8,128)(2,1)S(1)}, u32[]{:S(2)}, u32[]{:S(2)}) %collective-permute-start.49) | collective-permute-done | bytes 1474592 | tf_op jit(solution)/shard_map/ppermute | solution.py:561
  469.5 14.1 %collective-permute-done.22 = f32[9216]{0:T(1024)S(1)} collective-permute-done((f32[9216]{0:T(1024)S(1)}, f32[9216]{0:T(1024)S(1)}, u32[]{:S(2)}, u32[]{:S(2)}) %collective-permute-start.22) | collective-permute-done | bytes 36896 | tf_op jit(solution)/shard_map/ppermute | solution.py:561
  485.4 2.1 collective-permute-done.23
  488.4 1.8 collective-permute-start.24
  490.5 3.2 collective-permute-done.24
  498.3 9.4 %collective-permute-done.19 = bf16[256,768]{1,0:T(8,128)(2,1)S(1)} collective-permute-done((bf16[256,768]{1,0:T(8,128)(2,1)S(1)}, bf16[256,768]{1,0:T(8,128)(2,1)S(1)}, u32[]{:S(2)}, u32[]{:S(2)}) %collective-permute-start.19) | collective-permute-done | bytes 393248 | tf_op jit(solution)/shard_map/ppermute | solution.py:561
  509.8 5.5 %spread.1 = f32[768,2304]{1,0:T(8,128)} custom-call(s32[1]{0:T(128)} %bitcast.p_ref.part_ref, bf16[768,768]{1,0:T(8,128)(2,1)} %copy-done.11, bf16[768,384]{1,0:T(8,128)(2,1)} %copy-done.15, bf16[768,768]{1,0:T(8,128)(2,1)} %collective-permute-done.41.refs_2_, bf16[768,384]{1,0:T(8,128)(2,1)} %copy-done.30), custom_call_target="tpu_custom_call" | custom-call | flops 1769472 | bytes 10616832 | tf_op jit(solution)/shard_map/spread/pallas_call | solution.py:507
  515.2 11.4 %join.3 = f32[3072,768]{1,0:T(8,128)} custom-call(s32[1]{0:T(128)} %bitcast.89.bit_ref, bf16[1536,768]{1,0:T(8,128)(2,1)} %pad_maximum_fusion.2.mine_ref, bf16[1536,768]{1,0:T(8,128)(2,1)} %collective-permute-done.58.other_ref), custom_call_target="tpu_custom_call" | custom-call | flops 2359296 | bytes 14155776 | tf_op jit(solution)/shard_map/join/pallas_call | solution.py:462
  526.6 7.8 %join.2 = (f32[768,3072]{1,0:T(8,128)}, f32[768,768]{1,0:T(8,128)}) custom-call(s32[1]{0:T(128)} %bitcast.89.bit_ref, bf16[384,3840]{1,0:T(8,128)(2,1)} %copy-done.6, bf16[384,3840]{1,0:T(8,128)(2,1)} %collective-permute-done.50.other_ref), custom_call_target="tpu_custom_call" | custom-call | flops 2949120 | bytes 17694720 | tf_op jit(solution)/shard_map/join/pallas_call | solution.py:462
  (346 shorter events, 93.1 us)
Async XLA Ops:
  3.0 20.0 %collective-permute-start = (bf16[256,768]{1,0:T(8,128)(2,1)S(1)}, bf16[256,768]{1,0:T(8,128)(2,1)S(1)}, u32[]{:S(2)}, u32[]{:S(2)}) collective-permute-start(bf16[256,768]{1,0:T(8,128)(2,1)S(1)} %get-tuple-element.130), channel_id=1, source_target_pairs={{0,2},{1,3},{2,0},{3,1},{4,6},{5,7},{6,4},{7,5},{8,10},{9,11},{10,... | collective-permute-start | bytes 1179656 | tf_op jit(solution)/shard_map/ppermute | solution.py:561
  5.9 19.0 %collective-permute-start.1 = (bf16[256,768]{1,0:T(8,128)(2,1)S(1)}, bf16[256,768]{1,0:T(8,128)(2,1)S(1)}, u32[]{:S(2)}, u32[]{:S(2)}) collective-permute-start(bf16[256,768]{1,0:T(8,128)(2,1)S(1)} %get-tuple-element.133), channel_id=1, source_target_pairs={{0,4},{1,5},{2,6},{3,7},{4,0},{5,1},{6,2},{7,3},{8,12},{9,13},{10,... | collective-permute-start | bytes 1179656 | tf_op jit(solution)/shard_map/ppermute | solution.py:561
  7.5 17.5 %collective-permute-start.2 = (bf16[256,768]{1,0:T(8,128)(2,1)S(1)}, bf16[256,768]{1,0:T(8,128)(2,1)S(1)}, u32[]{:S(2)}, u32[]{:S(2)}) collective-permute-start(bf16[256,768]{1,0:T(8,128)(2,1)S(1)} %get-tuple-element.129), channel_id=1, source_target_pairs={{0,6},{1,7},{2,4},{3,5},{4,2},{5,3},{6,0},{7,1},{8,14},{9,15},{10,... | collective-permute-start | bytes 1179656 | tf_op jit(solution)/shard_map/ppermute | solution.py:561
  25.8 14.0 %copy-start.2 = (bf16[4,256,768]{2,1,0:T(8,128)(2,1)}, bf16[4,256,768]{2,1,0:T(8,128)(2,1)S(1)}, u32[]{:S(2)}) copy-start(bf16[4,256,768]{2,1,0:T(8,128)(2,1)S(1)} %get-tuple-element.93.refs_2_) | copy-start | bytes 4718596
  25.8 17.0 %collective-permute-start.3 = (bf16[4,256,768]{2,1,0:T(8,128)(2,1)S(1)}, bf16[4,256,768]{2,1,0:T(8,128)(2,1)S(1)}, u32[]{:S(2)}, u32[]{:S(2)}) collective-permute-start(bf16[4,256,768]{2,1,0:T(8,128)(2,1)S(1)} %get-tuple-element.93.refs_2_), channel_id=1, source_target_pairs={{0,1},{1,0},{2,3},{3,2},{4,5},{5,4},{6,7},{7,6},{8,9},{9,8},{10,11... | collective-permute-start | bytes 4718600 | tf_op jit(solution)/shard_map/ppermute | solution.py:561
  45.8 60.7 %collective-permute-start.6 = (bf16[256,768]{1,0:T(8,128)(2,1)S(1)}, bf16[256,768]{1,0:T(8,128)(2,1)S(1)}, u32[]{:S(2)}, u32[]{:S(2)}) collective-permute-start(bf16[256,768]{1,0:T(8,128)(2,1)S(1)} %get-tuple-element.126), channel_id=1, source_target_pairs={{0,6},{1,7},{2,4},{3,5},{4,2},{5,3},{6,0},{7,1},{8,14},{9,15},{10,... | collective-permute-start | bytes 1179656 | tf_op jit(solution)/shard_map/ppermute | solution.py:561
  47.3 59.3 %collective-permute-start.5 = (bf16[256,768]{1,0:T(8,128)(2,1)S(1)}, bf16[256,768]{1,0:T(8,128)(2,1)S(1)}, u32[]{:S(2)}, u32[]{:S(2)}) collective-permute-start(bf16[256,768]{1,0:T(8,128)(2,1)S(1)} %get-tuple-element.127), channel_id=1, source_target_pairs={{0,4},{1,5},{2,6},{3,7},{4,0},{5,1},{6,2},{7,3},{8,12},{9,13},{10,... | collective-permute-start | bytes 1179656 | tf_op jit(solution)/shard_map/ppermute | solution.py:561
  48.4 58.2 %collective-permute-start.4 = (bf16[256,768]{1,0:T(8,128)(2,1)S(1)}, bf16[256,768]{1,0:T(8,128)(2,1)S(1)}, u32[]{:S(2)}, u32[]{:S(2)}) collective-permute-start(bf16[256,768]{1,0:T(8,128)(2,1)S(1)} %get-tuple-element.128), channel_id=1, source_target_pairs={{0,2},{1,3},{2,0},{3,1},{4,6},{5,7},{6,4},{7,5},{8,10},{9,11},{10,... | collective-permute-start | bytes 1179656 | tf_op jit(solution)/shard_map/ppermute | solution.py:561
  109.8 2.9 collective-permute-start.7
  113.7 36.6 %copy-start.16 = (bf16[4,256,768]{2,1,0:T(8,128)(2,1)S(1)}, bf16[4,256,768]{2,1,0:T(8,128)(2,1)}, u32[]{:S(2)}) copy-start(bf16[4,256,768]{2,1,0:T(8,128)(2,1)} %pad_maximum_fusion.5.refs_3_) | copy-start | bytes 4718596
  150.2 12.3 %copy-start.49 = (bf16[4,256,3072]{2,1,0:T(8,128)(2,1)S(1)}, bf16[4,256,3072]{2,1,0:T(8,128)(2,1)}, u32[]{:S(2)}) copy-start(bf16[4,256,3072]{2,1,0:T(8,128)(2,1)} %get-tuple-element.61) | copy-start | bytes 18874372
  162.0 48.9 %collective-permute-start.9 = (bf16[1536,768]{1,0:T(8,128)(2,1)}, bf16[1536,768]{1,0:T(8,128)(2,1)}, u32[]{:S(2)}, u32[]{:S(2)}) collective-permute-start(bf16[1536,768]{1,0:T(8,128)(2,1)} %dynamic-slice_bitcast_fusion.1), channel_id=1, source_target_pairs={{0,1},{1,0},{2,3},{3,2},{4,5},{5,4},{6,7},{7,6},{8,9},{9,8},{10,11... | collective-permute-start | bytes 7077896 | tf_op jit(solution)/shard_map/ppermute | solution.py:561
  177.0 37.0 %collective-permute-start.10 = (bf16[384,3840]{1,0:T(8,128)(2,1)}, bf16[384,3840]{1,0:T(8,128)(2,1)}, u32[]{:S(2)}, u32[]{:S(2)}) collective-permute-start(bf16[384,3840]{1,0:T(8,128)(2,1)} %dynamic-slice_bitcast_fusion), channel_id=1, source_target_pairs={{0,1},{1,0},{2,3},{3,2},{4,5},{5,4},{6,7},{7,6},{8,9},{9,8},{10,11... | collective-permute-start | bytes 8847368 | tf_op jit(solution)/shard_map/ppermute | solution.py:561
  183.8 11.6 %collective-permute-start.11 = (bf16[256,768]{1,0:T(8,128)(2,1)}, bf16[256,768]{1,0:T(8,128)(2,1)S(1)}, u32[]{:S(2)}, u32[]{:S(2)}) collective-permute-start(bf16[256,768]{1,0:T(8,128)(2,1)} %get-tuple-element.118), channel_id=1, source_target_pairs={{0,2},{1,3},{2,0},{3,1},{4,6},{5,7},{6,4},{7,5},{8,10},{9,11},{10,... | collective-permute-start | bytes 1179656 | tf_op jit(solution)/shard_map/ppermute | solution.py:561
  185.5 23.1 %collective-permute-start.8 = (bf16[4,256,384]{1,2,0:T(8,128)(2,1)}, bf16[4,256,384]{1,2,0:T(8,128)(2,1)}, u32[]{:S(2)}, u32[]{:S(2)}) collective-permute-start(bf16[4,256,384]{1,2,0:T(8,128)(2,1)} %copy.51), channel_id=1, source_target_pairs={{0,1},{1,0},{2,3},{3,2},{4,5},{5,4},{6,7},{7,6},{8,9},{9,8},{10,11... | collective-permute-start | bytes 2359304 | tf_op jit(solution)/shard_map/ppermute | solution.py:561
  185.8 13.6 %collective-permute-start.12 = (bf16[256,768]{1,0:T(8,128)(2,1)}, bf16[256,768]{1,0:T(8,128)(2,1)}, u32[]{:S(2)}, u32[]{:S(2)}) collective-permute-start(bf16[256,768]{1,0:T(8,128)(2,1)} %get-tuple-element.117), channel_id=1, source_target_pairs={{0,4},{1,5},{2,6},{3,7},{4,0},{5,1},{6,2},{7,3},{8,12},{9,13},{10,... | collective-permute-start | bytes 1179656 | tf_op jit(solution)/shard_map/ppermute | solution.py:561
  195.4 12.3 %collective-permute-start.13 = (bf16[256,768]{1,0:T(8,128)(2,1)}, bf16[256,768]{1,0:T(8,128)(2,1)S(1)}, u32[]{:S(2)}, u32[]{:S(2)}) collective-permute-start(bf16[256,768]{1,0:T(8,128)(2,1)} %get-tuple-element.116), channel_id=1, source_target_pairs={{0,6},{1,7},{2,4},{3,5},{4,2},{5,3},{6,0},{7,1},{8,14},{9,15},{10,... | collective-permute-start | bytes 1179656 | tf_op jit(solution)/shard_map/ppermute | solution.py:561
  219.4 42.1 %collective-permute-start.14 = (bf16[768,768]{1,0:T(8,128)(2,1)}, bf16[768,768]{1,0:T(8,128)(2,1)}, u32[]{:S(2)}, u32[]{:S(2)}) collective-permute-start(bf16[768,768]{1,0:T(8,128)(2,1)} %dynamic-slice_bitcast_fusion.3), channel_id=1, source_target_pairs={{0,2},{1,3},{2,0},{3,1},{4,6},{5,7},{6,4},{7,5},{8,10},{9,11},{10,... | collective-permute-start | bytes 3538952 | tf_op jit(solution)/shard_map/ppermute | solution.py:561
  220.2 44.4 %collective-permute-start.15 = (bf16[192,3840]{1,0:T(8,128)(2,1)S(1)}, bf16[192,3840]{1,0:T(8,128)(2,1)}, u32[]{:S(2)}, u32[]{:S(2)}) collective-permute-start(bf16[192,3840]{1,0:T(8,128)(2,1)S(1)} %dynamic-slice_bitcast_fusion.2), channel_id=1, source_target_pairs={{0,4},{1,5},{2,6},{3,7},{4,0},{5,1},{6,2},{7,3},{8,12},{9,13},{10,... | collective-permute-start | bytes 4423688 | tf_op jit(solution)/shard_map/ppermute | solution.py:561
  302.0 104.6 %collective-permute-start.16 = (bf16[1024,768]{1,0:T(8,128)(2,1)S(1)}, bf16[1024,768]{1,0:T(8,128)(2,1)S(1)}, u32[]{:S(2)}, u32[]{:S(2)}) collective-permute-start(bf16[1024,768]{1,0:T(8,128)(2,1)S(1)} %slice.228), channel_id=1, source_target_pairs={{0,1},{1,0},{2,3},{3,2},{4,5},{5,4},{6,7},{7,6},{8,9},{9,8},{10,11... | collective-permute-start | bytes 4718600 | tf_op jit(solution)/shard_map/ppermute | solution.py:561
  302.1 47.5 %collective-permute-start.25 = (bf16[384,768]{1,0:T(8,128)(2,1)S(1)}, bf16[384,768]{1,0:T(8,128)(2,1)S(1)}, u32[]{:S(2)}, u32[]{:S(2)}) collective-permute-start(bf16[384,768]{1,0:T(8,128)(2,1)S(1)} %dynamic-slice_bitcast_fusion.6), channel_id=1, source_target_pairs={{0,4},{1,5},{2,6},{3,7},{4,0},{5,1},{6,2},{7,3},{8,12},{9,13},{10,... | collective-permute-start | bytes 1769480 | tf_op jit(solution)/shard_map/ppermute | solution.py:561
  302.2 22.5 %collective-permute-start.33 = (bf16[384,384]{1,0:T(8,128)(2,1)S(1)}, bf16[384,384]{1,0:T(8,128)(2,1)S(1)}, u32[]{:S(2)}, u32[]{:S(2)}) collective-permute-start(bf16[384,384]{1,0:T(8,128)(2,1)S(1)} %dynamic-slice_bitcast_fusion.15), channel_id=1, source_target_pairs={{0,4},{1,5},{2,6},{3,7},{4,0},{5,1},{6,2},{7,3},{8,12},{9,13},{10,... | collective-permute-start | bytes 884744 | tf_op jit(solution)/shard_map/ppermute | solution.py:561
  304.3 55.0 %collective-permute-start.43 = (bf16[96,3840]{1,0:T(8,128)(2,1)S(1)}, bf16[96,3840]{1,0:T(8,128)(2,1)S(1)}, u32[]{:S(2)}, u32[]{:S(2)}) collective-permute-start(bf16[96,3840]{1,0:T(8,128)(2,1)S(1)} %dynamic-slice_bitcast_fusion.4), channel_id=1, source_target_pairs={{0,2},{1,3},{2,0},{3,1},{4,6},{5,7},{6,4},{7,5},{8,10},{9,11},{10,... | collective-permute-start | bytes 2211848 | tf_op jit(solution)/shard_map/ppermute | solution.py:561
  305.3 46.7 %collective-permute-start.51 = (bf16[384,768]{1,0:T(8,128)(2,1)S(1)}, bf16[384,768]{1,0:T(8,128)(2,1)S(1)}, u32[]{:S(2)}, u32[]{:S(2)}) collective-permute-start(bf16[384,768]{1,0:T(8,128)(2,1)S(1)} %dynamic-slice_bitcast_fusion.5), channel_id=1, source_target_pairs={{0,4},{1,5},{2,6},{3,7},{4,0},{5,1},{6,2},{7,3},{8,12},{9,13},{10,... | collective-permute-start | bytes 1769480 | tf_op jit(solution)/shard_map/ppermute | solution.py:561
  324.8 5.2 collective-permute-start.34
  330.1 4.6 collective-permute-start.35
  334.7 11.9 %collective-permute-start.36 = (bf16[48,384]{1,0:T(8,128)(2,1)S(1)}, bf16[48,384]{1,0:T(8,128)(2,1)S(1)}, u32[]{:S(2)}, u32[]{:S(2)}) collective-permute-start(bf16[48,384]{1,0:T(8,128)(2,1)S(1)} %dynamic-slice_bitcast_fusion.23), channel_id=1, source_target_pairs={{0,16},{8,24},{16,0},{24,8},{1,17},{9,25},{17,1},{25,9},{2,18},{10... | collective-permute-start | bytes 110600 | tf_op jit(solution)/shard_map/ppermute | solution.py:561
  346.6 5.3 collective-permute-start.37
  349.8 13.0 %collective-permute-start.26 = (bf16[192,768]{1,0:T(8,128)(2,1)S(1)}, bf16[192,768]{1,0:T(8,128)(2,1)S(1)}, u32[]{:S(2)}, u32[]{:S(2)}) collective-permute-start(bf16[192,768]{1,0:T(8,128)(2,1)S(1)} %dynamic-slice_bitcast_fusion.16), channel_id=1, source_target_pairs={{0,2},{1,3},{2,0},{3,1},{4,6},{5,7},{6,4},{7,5},{8,10},{9,11},{10,... | collective-permute-start | bytes 884744 | tf_op jit(solution)/shard_map/ppermute | solution.py:561
  351.9 5.2 collective-permute-start.38
  352.2 12.8 %collective-permute-start.52 = (bf16[192,768]{1,0:T(8,128)(2,1)S(1)}, bf16[192,768]{1,0:T(8,128)(2,1)S(1)}, u32[]{:S(2)}, u32[]{:S(2)}) collective-permute-start(bf16[192,768]{1,0:T(8,128)(2,1)S(1)} %dynamic-slice_bitcast_fusion.14), channel_id=1, source_target_pairs={{0,8},{8,0},{16,24},{24,16},{1,9},{9,1},{17,25},{25,17},{2,10},{10... | collective-permute-start | bytes 884744 | tf_op jit(solution)/shard_map/ppermute | solution.py:561
  357.2 5.2 collective-permute-start.39
  359.5 22.9 %collective-permute-start.44 = (bf16[48,3840]{1,0:T(8,128)(2,1)S(1)}, bf16[48,3840]{1,0:T(8,128)(2,1)S(1)}, u32[]{:S(2)}, u32[]{:S(2)}) collective-permute-start(bf16[48,3840]{1,0:T(8,128)(2,1)S(1)} %dynamic-slice_bitcast_fusion.13), channel_id=1, source_target_pairs={{0,8},{8,0},{16,24},{24,16},{1,9},{9,1},{17,25},{25,17},{2,10},{10... | collective-permute-start | bytes 1105928 | tf_op jit(solution)/shard_map/ppermute | solution.py:561
  362.5 23.0 %collective-permute-start.40 = (bf16[384,384]{1,0:T(8,128)(2,1)S(1)}, bf16[384,384]{1,0:T(8,128)(2,1)S(1)}, u32[]{:S(2)}, u32[]{:S(2)}) collective-permute-start(bf16[384,384]{1,0:T(8,128)(2,1)S(1)} %pad_maximum_fusion.15), channel_id=1, source_target_pairs={{0,4},{1,5},{2,6},{3,7},{4,0},{5,1},{6,2},{7,3},{8,12},{9,13},{10,... | collective-permute-start | bytes 884744 | tf_op jit(solution)/shard_map/ppermute | solution.py:561
  363.0 12.4 %collective-permute-start.27 = (bf16[96,768]{1,0:T(8,128)(2,1)S(1)}, bf16[96,768]{1,0:T(8,128)(2,1)S(1)}, u32[]{:S(2)}, u32[]{:S(2)}) collective-permute-start(bf16[96,768]{1,0:T(8,128)(2,1)S(1)} %dynamic-slice_bitcast_fusion.20), channel_id=1, source_target_pairs={{0,8},{8,0},{16,24},{24,16},{1,9},{9,1},{17,25},{25,17},{2,10},{10... | collective-permute-start | bytes 442376 | tf_op jit(solution)/shard_map/ppermute | solution.py:561
  365.1 10.6 %collective-permute-start.53 = (bf16[96,768]{1,0:T(8,128)(2,1)S(1)}, bf16[96,768]{1,0:T(8,128)(2,1)S(1)}, u32[]{:S(2)}, u32[]{:S(2)}) collective-permute-start(bf16[96,768]{1,0:T(8,128)(2,1)S(1)} %dynamic-slice_bitcast_fusion.18), channel_id=1, source_target_pairs={{0,16},{8,24},{16,0},{24,8},{1,17},{9,25},{17,1},{25,9},{2,18},{10... | collective-permute-start | bytes 442376 | tf_op jit(solution)/shard_map/ppermute | solution.py:561
  375.4 6.9 %collective-permute-start.28 = (bf16[48,768]{1,0:T(8,128)(2,1)S(1)}, bf16[48,768]{1,0:T(8,128)(2,1)S(1)}, u32[]{:S(2)}, u32[]{:S(2)}) collective-permute-start(bf16[48,768]{1,0:T(8,128)(2,1)S(1)} %dynamic-slice_bitcast_fusion.22), channel_id=1, source_target_pairs={{0,16},{8,24},{16,0},{24,8},{1,17},{9,25},{17,1},{25,9},{2,18},{10... | collective-permute-start | bytes 221192 | tf_op jit(solution)/shard_map/ppermute | solution.py:561
  375.8 12.9 %collective-permute-start.54 = (bf16[96,768]{1,0:T(8,128)(2,1)S(1)}, bf16[96,768]{1,0:T(8,128)(2,1)S(1)}, u32[]{:S(2)}, u32[]{:S(2)}) collective-permute-start(bf16[96,768]{1,0:T(8,128)(2,1)S(1)} %fusion.35), channel_id=1, source_target_pairs={{0,16},{8,24},{16,0},{24,8},{1,17},{9,25},{17,1},{25,9},{2,18},{10... | collective-permute-start | bytes 442376 | tf_op jit(solution)/shard_map/ppermute | solution.py:561
  382.3 7.6 %collective-permute-start.29 = (bf16[48,768]{1,0:T(8,128)(2,1)S(1)}, bf16[48,768]{1,0:T(8,128)(2,1)S(1)}, u32[]{:S(2)}, u32[]{:S(2)}) collective-permute-start(bf16[48,768]{1,0:T(8,128)(2,1)S(1)} %fusion.39), channel_id=1, source_target_pairs={{0,16},{8,24},{16,0},{24,8},{1,17},{9,25},{17,1},{25,9},{2,18},{10... | collective-permute-start | bytes 221192 | tf_op jit(solution)/shard_map/ppermute | solution.py:561
  382.5 11.6 %collective-permute-start.45 = (bf16[24,3840]{1,0:T(8,128)(2,1)S(1)}, bf16[24,3840]{1,0:T(8,128)(2,1)S(1)}, u32[]{:S(2)}, u32[]{:S(2)}) collective-permute-start(bf16[24,3840]{1,0:T(8,128)(2,1)S(1)} %dynamic-slice_bitcast_fusion.17), channel_id=1, source_target_pairs={{0,16},{8,24},{16,0},{24,8},{1,17},{9,25},{17,1},{25,9},{2,18},{10... | collective-permute-start | bytes 552968 | tf_op jit(solution)/shard_map/ppermute | solution.py:561
  385.7 109.4 %copy-start.15 = (bf16[768,384]{1,0:T(8,128)(2,1)}, bf16[768,384]{1,0:T(8,128)(2,1)S(1)}, u32[]{:S(2)}) copy-start(bf16[768,384]{1,0:T(8,128)(2,1)S(1)} %pad_maximum_fusion.11.refs_1_) | copy-start | bytes 1769476
  388.8 14.8 %collective-permute-start.55 = (bf16[192,768]{1,0:T(8,128)(2,1)S(1)}, bf16[192,768]{1,0:T(8,128)(2,1)S(1)}, u32[]{:S(2)}, u32[]{:S(2)}) collective-permute-start(bf16[192,768]{1,0:T(8,128)(2,1)S(1)} %pad_maximum_fusion.16), channel_id=1, source_target_pairs={{0,8},{8,0},{16,24},{24,16},{1,9},{9,1},{17,25},{25,17},{2,10},{10... | collective-permute-start | bytes 884744 | tf_op jit(solution)/shard_map/ppermute | solution.py:561
  390.0 13.4 %collective-permute-start.30 = (bf16[96,768]{1,0:T(8,128)(2,1)S(1)}, bf16[96,768]{1,0:T(8,128)(2,1)S(1)}, u32[]{:S(2)}, u32[]{:S(2)}) collective-permute-start(bf16[96,768]{1,0:T(8,128)(2,1)S(1)} %pad_maximum_fusion.17), channel_id=1, source_target_pairs={{0,8},{8,0},{16,24},{24,16},{1,9},{9,1},{17,25},{25,17},{2,10},{10... | collective-permute-start | bytes 442376 | tf_op jit(solution)/shard_map/ppermute | solution.py:561
  394.1 12.3 %collective-permute-start.46 = (bf16[24,3840]{1,0:T(8,128)(2,1)S(1)}, bf16[24,3840]{1,0:T(8,128)(2,1)S(1)}, u32[]{:S(2)}, u32[]{:S(2)}) collective-permute-start(bf16[24,3840]{1,0:T(8,128)(2,1)S(1)} %fusion.34), channel_id=1, source_target_pairs={{0,16},{8,24},{16,0},{24,8},{1,17},{9,25},{17,1},{25,9},{2,18},{10... | collective-permute-start | bytes 552968 | tf_op jit(solution)/shard_map/ppermute | solution.py:561
  403.5 31.3 %collective-permute-start.31 = (bf16[192,768]{1,0:T(8,128)(2,1)S(1)}, bf16[192,768]{1,0:T(8,128)(2,1)S(1)}, u32[]{:S(2)}, u32[]{:S(2)}) collective-permute-start(bf16[192,768]{1,0:T(8,128)(2,1)S(1)} %pad_maximum_fusion.14), channel_id=1, source_target_pairs={{0,2},{1,3},{2,0},{3,1},{4,6},{5,7},{6,4},{7,5},{8,10},{9,11},{10,... | collective-permute-start | bytes 884744 | tf_op jit(solution)/shard_map/ppermute | solution.py:561
  403.7 31.2 %collective-permute-start.56 = (bf16[384,768]{1,0:T(8,128)(2,1)S(1)}, bf16[384,768]{1,0:T(8,128)(2,1)S(1)}, u32[]{:S(2)}, u32[]{:S(2)}) collective-permute-start(bf16[384,768]{1,0:T(8,128)(2,1)S(1)} %pad_maximum_fusion.12), channel_id=1, source_target_pairs={{0,4},{1,5},{2,6},{3,7},{4,0},{5,1},{6,2},{7,3},{8,12},{9,13},{10,... | collective-permute-start | bytes 1769480 | tf_op jit(solution)/shard_map/ppermute | solution.py:561
  406.5 9.0 %collective-permute-start.47 = (bf16[48,3840]{1,0:T(8,128)(2,1)S(1)}, bf16[48,3840]{1,0:T(8,128)(2,1)S(1)}, u32[]{:S(2)}, u32[]{:S(2)}) collective-permute-start(bf16[48,3840]{1,0:T(8,128)(2,1)S(1)} %pad_maximum_fusion.13), channel_id=1, source_target_pairs={{0,8},{8,0},{16,24},{24,16},{1,9},{9,1},{17,25},{25,17},{2,10},{10... | collective-permute-start | bytes 1105928 | tf_op jit(solution)/shard_map/ppermute | solution.py:561
  415.7 16.1 %collective-permute-start.48 = (bf16[96,3840]{1,0:T(8,128)(2,1)S(1)}, bf16[96,3840]{1,0:T(8,128)(2,1)S(1)}, u32[]{:S(2)}, u32[]{:S(2)}) collective-permute-start(bf16[96,3840]{1,0:T(8,128)(2,1)S(1)} %pad_maximum_fusion.9), channel_id=1, source_target_pairs={{0,2},{1,3},{2,0},{3,1},{4,6},{5,7},{6,4},{7,5},{8,10},{9,11},{10,... | collective-permute-start | bytes 2211848 | tf_op jit(solution)/shard_map/ppermute | solution.py:561
  432.1 31.0 %collective-permute-start.49 = (bf16[192,3840]{1,0:T(8,128)(2,1)S(1)}, bf16[192,3840]{1,0:T(8,128)(2,1)S(1)}, u32[]{:S(2)}, u32[]{:S(2)}) collective-permute-start(bf16[192,3840]{1,0:T(8,128)(2,1)S(1)} %pad_maximum_fusion.6), channel_id=1, source_target_pairs={{0,4},{1,5},{2,6},{3,7},{4,0},{5,1},{6,2},{7,3},{8,12},{9,13},{10,... | collective-permute-start | bytes 4423688 | tf_op jit(solution)/shard_map/ppermute | solution.py:561
  432.8 1.6 collective-permute-start.20
  434.4 33.5 %collective-permute-start.21 = (f32[9216]{0:T(1024)S(1)}, f32[9216]{0:T(1024)S(1)}, u32[]{:S(2)}, u32[]{:S(2)}) collective-permute-start(f32[9216]{0:T(1024)S(1)} %add.479), channel_id=1, source_target_pairs={{0,2},{1,3},{2,0},{3,1},{4,6},{5,7},{6,4},{7,5},{8,10},{9,11},{10,... | collective-permute-start | bytes 110600 | tf_op jit(solution)/shard_map/ppermute | solution.py:561
  435.2 28.7 %collective-permute-start.57 = (bf16[768,768]{1,0:T(8,128)(2,1)S(1)}, bf16[768,768]{1,0:T(8,128)(2,1)S(1)}, u32[]{:S(2)}, u32[]{:S(2)}) collective-permute-start(bf16[768,768]{1,0:T(8,128)(2,1)S(1)} %pad_maximum_fusion.8), channel_id=1, source_target_pairs={{0,2},{1,3},{2,0},{3,1},{4,6},{5,7},{6,4},{7,5},{8,10},{9,11},{10,... | collective-permute-start | bytes 3538952 | tf_op jit(solution)/shard_map/ppermute | solution.py:561
  463.8 62.8 %collective-permute-start.50 = (bf16[384,3840]{1,0:T(8,128)(2,1)S(1)}, bf16[384,3840]{1,0:T(8,128)(2,1)}, u32[]{:S(2)}, u32[]{:S(2)}) collective-permute-start(bf16[384,3840]{1,0:T(8,128)(2,1)S(1)} %pad_maximum_fusion.1.mine_ref), channel_id=1, source_target_pairs={{0,1},{1,0},{2,3},{3,2},{4,5},{5,4},{6,7},{7,6},{8,9},{9,8},{10,11... | collective-permute-start | bytes 8847368 | tf_op jit(solution)/shard_map/ppermute | solution.py:561
  466.9 48.3 %collective-permute-start.58 = (bf16[1536,768]{1,0:T(8,128)(2,1)}, bf16[1536,768]{1,0:T(8,128)(2,1)}, u32[]{:S(2)}, u32[]{:S(2)}) collective-permute-start(bf16[1536,768]{1,0:T(8,128)(2,1)} %pad_maximum_fusion.2.mine_ref), channel_id=1, source_target_pairs={{0,1},{1,0},{2,3},{3,2},{4,5},{5,4},{6,7},{7,6},{8,9},{9,8},{10,11... | collective-permute-start | bytes 7077896 | tf_op jit(solution)/shard_map/ppermute | solution.py:561
  467.0 21.4 %collective-permute-start.32 = (bf16[384,768]{1,0:T(8,128)(2,1)S(1)}, bf16[384,768]{1,0:T(8,128)(2,1)S(1)}, u32[]{:S(2)}, u32[]{:S(2)}) collective-permute-start(bf16[384,768]{1,0:T(8,128)(2,1)S(1)} %pad_maximum_fusion.10), channel_id=1, source_target_pairs={{0,4},{1,5},{2,6},{3,7},{4,0},{5,1},{6,2},{7,3},{8,12},{9,13},{10,... | collective-permute-start | bytes 1769480 | tf_op jit(solution)/shard_map/ppermute | solution.py:561
  467.9 15.7 %collective-permute-start.22 = (f32[9216]{0:T(1024)S(1)}, f32[9216]{0:T(1024)S(1)}, u32[]{:S(2)}, u32[]{:S(2)}) collective-permute-start(f32[9216]{0:T(1024)S(1)} %add.480), channel_id=1, source_target_pairs={{0,4},{1,5},{2,6},{3,7},{4,0},{5,1},{6,2},{7,3},{8,12},{9,13},{10,... | collective-permute-start | bytes 110600 | tf_op jit(solution)/shard_map/ppermute | solution.py:561
  483.6 4.0 collective-permute-start.23
  484.5 10.6 %collective-permute-start.17 = (bf16[256,768]{1,0:T(8,128)(2,1)S(1)}, bf16[256,768]{1,0:T(8,128)(2,1)S(1)}, u32[]{:S(2)}, u32[]{:S(2)}) collective-permute-start(bf16[256,768]{1,0:T(8,128)(2,1)S(1)} %get-tuple-element.115), channel_id=1, source_target_pairs={{0,2},{1,3},{2,0},{3,1},{4,6},{5,7},{6,4},{7,5},{8,10},{9,11},{10,... | collective-permute-start | bytes 1179656 | tf_op jit(solution)/shard_map/ppermute | solution.py:561
  487.5 9.5 %collective-permute-start.18 = (bf16[256,768]{1,0:T(8,128)(2,1)S(1)}, bf16[256,768]{1,0:T(8,128)(2,1)S(1)}, u32[]{:S(2)}, u32[]{:S(2)}) collective-permute-start(bf16[256,768]{1,0:T(8,128)(2,1)S(1)} %get-tuple-element.114), channel_id=1, source_target_pairs={{0,4},{1,5},{2,6},{3,7},{4,0},{5,1},{6,2},{7,3},{8,12},{9,13},{10,... | collective-permute-start | bytes 1179656 | tf_op jit(solution)/shard_map/ppermute | solution.py:561
  488.4 5.3 collective-permute-start.24
  493.7 16.0 %collective-permute-start.41 = (bf16[768,768]{1,0:T(8,128)(2,1)S(1)}, bf16[768,768]{1,0:T(8,128)(2,1)}, u32[]{:S(2)}, u32[]{:S(2)}) collective-permute-start(bf16[768,768]{1,0:T(8,128)(2,1)S(1)} %pad_maximum_fusion.7.refs_0_), channel_id=1, source_target_pairs={{0,1},{1,0},{2,3},{3,2},{4,5},{5,4},{6,7},{7,6},{8,9},{9,8},{10,11... | collective-permute-start | bytes 3538952 | tf_op jit(solution)/shard_map/ppermute | solution.py:561
  495.1 12.6 %collective-permute-start.42 = (bf16[768,384]{1,0:T(8,128)(2,1)S(1)}, bf16[768,384]{1,0:T(8,128)(2,1)S(1)}, u32[]{:S(2)}, u32[]{:S(2)}) collective-permute-start(bf16[768,384]{1,0:T(8,128)(2,1)S(1)} %pad_maximum_fusion.11.refs_1_), channel_id=1, source_target_pairs={{0,1},{1,0},{2,3},{3,2},{4,5},{5,4},{6,7},{7,6},{8,9},{9,8},{10,11... | collective-permute-start | bytes 1769480 | tf_op jit(solution)/shard_map/ppermute | solution.py:561
  497.1 10.7 %collective-permute-start.19 = (bf16[256,768]{1,0:T(8,128)(2,1)S(1)}, bf16[256,768]{1,0:T(8,128)(2,1)S(1)}, u32[]{:S(2)}, u32[]{:S(2)}) collective-permute-start(bf16[256,768]{1,0:T(8,128)(2,1)S(1)} %get-tuple-element.113), channel_id=1, source_target_pairs={{0,6},{1,7},{2,4},{3,5},{4,2},{5,3},{6,0},{7,1},{8,14},{9,15},{10,... | collective-permute-start | bytes 1179656 | tf_op jit(solution)/shard_map/ppermute | solution.py:561
  515.2 19.2 %copy-start.1 = (s32[4,2]{0,1:T(2,128)S(1)}, s32[4,2]{0,1:T(2,128)}, u32[]{:S(2)}) copy-start(s32[4,2]{0,1:T(2,128)} %param.21) | copy-start | bytes 100
  (46 other events, 139.7 us)

commit v4 on v3

--- a/solution.py
+++ b/solution.py
@@ -439,17 +439,18 @@
     return out[:6], out[6 : 6 + parts], out[6 + parts], out[7 + parts]
 
 
-def join_kernel(splits, bit_ref, mine_ref, other_ref, *out_refs):
+def join_kernel(sources, moves, bit_ref, *refs):
+    mine_refs, other_refs, out_refs = refs[:sources], refs[sources : 2 * sources], refs[2 * sources :]
     mine = pl.program_id(0) == bit_ref[0]
-    begin = 0
-    for out_ref, count in zip(out_refs, splits):
+    for source, begin, out, place, count in moves:
         lanes = slice(begin, begin + count)
-        out_ref[...] = jnp.where(mine, mine_ref[:, lanes], other_ref[:, lanes]).astype(F32)
-        begin += count
-
-
-def join(mine, other, bit, splits):
-    count, columns = mine.shape
+        out_refs[out][:, place : place + count] = jnp.where(
+            mine, mine_refs[source][:, lanes], other_refs[source][:, lanes]
+        ).astype(F32)
+
+
+def join(mine, other, bit, moves, widths):
+    count = mine[0].shape[0]
     tall = next(t for t in (192, 96, 48, count) if count % t == 0)
     steps = count // tall
 
@@ -459,20 +460,19 @@
     def other_map(h, i, b):
         return jnp.where(h != b[0], i, jnp.where(h < 1 - b[0], 0, steps - 1)), 0
 
+    columns = sum(widths)
     return pl.pallas_call(
-        functools.partial(join_kernel, splits),
+        functools.partial(join_kernel, len(mine), moves),
         grid_spec=pltpu.PrefetchScalarGridSpec(
             num_scalar_prefetch=1,
             grid=(2, steps),
-            in_specs=[
-                pl.BlockSpec((tall, columns), mine_map),
-                pl.BlockSpec((tall, columns), other_map),
+            in_specs=[pl.BlockSpec((tall, m.shape[1]), mine_map) for m in mine]
+            + [pl.BlockSpec((tall, m.shape[1]), other_map) for m in mine],
+            out_specs=[
+                pl.BlockSpec((tall, n), lambda h, i, b: (h * steps + i, 0)) for n in widths
             ],
-            out_specs=[
-                pl.BlockSpec((tall, n), lambda h, i, b: (h * steps + i, 0)) for n in splits
-            ],
-        ),
-        out_shape=[jax.ShapeDtypeStruct((2 * count, n), F32) for n in splits],
+        ),
+        out_shape=[jax.ShapeDtypeStruct((2 * count, n), F32) for n in widths],
         compiler_params=pltpu.CompilerParams(
             dimension_semantics=("arbitrary", "arbitrary"), vmem_limit_bytes=VMEM_LIMIT
         ),
@@ -480,7 +480,7 @@
             flops=2 * count * columns, transcendentals=0, bytes_accessed=12 * count * columns
         ),
         name="join",
-    )(bit.reshape(1), mine, other)
+    )(bit.reshape(1), *mine, *other)
 
 
 def spread_kernel(parts, spans, part_ref, *refs):
@@ -569,21 +569,37 @@
     return lax.dynamic_index_in_dim(values, index, 0, keepdims=False)
 
 
-def halve(values, steps):
-    for axis, mask, bit in steps:
-        two = values.reshape(2, values.shape[0] // 2, *values.shape[1:])
-        arrived = swap(take(two, 1 - bit), axis, mask)
-        values = (take(two, bit).astype(F32) + arrived.astype(F32)).astype(values.dtype)
-    return values
-
-
-def double(values, steps):
-    for axis, mask, bit in reversed(steps):
-        arrived = swap(values, axis, mask)
-        first = jnp.where(bit == 0, values, arrived)
-        second = jnp.where(bit == 0, arrived, values)
-        values = jnp.concatenate([first, second], axis=0)
-    return values
+def halve(values, step):
+    axis, mask, bit = step
+    two = values.reshape(2, values.shape[0] // 2, *values.shape[1:])
+    arrived = swap(take(two, 1 - bit), axis, mask)
+    return (take(two, bit).astype(F32) + arrived.astype(F32)).astype(values.dtype)
+
+
+def double(values, step):
+    axis, mask, bit = step
+    arrived = swap(values, axis, mask)
+    first = jnp.where(bit == 0, values, arrived)
+    second = jnp.where(bit == 0, arrived, values)
+    return jnp.concatenate([first, second], axis=0)
+
+
+class Chain:
+    def __init__(self, values, down, up):
+        self.values = values
+        self.left = [(halve, step) for step in down] + [(double, step) for step in up]
+
+    def advance(self):
+        if self.left:
+            move, step = self.left.pop(0)
+            self.values = move(self.values, step)
+
+
+def close(chains, *others):
+    tied, others = lax.optimization_barrier(([c.values for c in chains], others))
+    for chain, values in zip(chains, tied):
+        chain.values = values
+    return others
 
 
 def per_device(
@@ -626,10 +642,12 @@
             ]
         )
 
-    def give_back(values):
-        out = jnp.zeros_like(values)
-        for m in range(rows):
-            slab = swap(values[m], "pos", m * parts) if m else values[m]
+    def send_back(values, m):
+        return swap(values[m], "pos", m * parts) if m else values[m]
+
+    def arrange(slabs):
+        out = jnp.zeros((rows, *slabs[0].shape), slabs[0].dtype)
+        for m, slab in enumerate(slabs):
             out = lax.dynamic_update_index_in_dim(out, slab, owner ^ m, 0)
         return out
 
@@ -687,12 +705,6 @@
         },
         as_row(up_bias),
     )
-    grad_all = jnp.concatenate(
-        [swap(g, "pos", s) if s else g for s, g in enumerate(grad_mixed)], axis=0
-    )
-    grad_t = grad_all.transpose(0, 2, 1)
-    layer_home = give_back(layer_out)
-
     local = rows * size
 
     def flat(values):
@@ -702,59 +714,67 @@
     row_steps = [(row_axis, m, (row_place // m) % 2) for m in bits(lax.axis_size(row_axis))]
     own_steps = [("pos", m * parts, (owner // m) % 2) for m in bits(rows)]
     part_steps = [("pos", m, (part // m) % 2) for m in bits(parts)]
-
-    grad_w_down = matmul(flat(hidden), flat(own_cotangent), TN).astype(BF16)
-    share_down = halve(grad_w_down, part_steps)
+    turning, last = own_steps + row_steps[:1], row_steps[1:]
+
+    def order(turn):
+        turn %= len(turning)
+        return turning[turn:] + turning[:turn] + last
+
+    def chain(values, turn, parted=True):
+        down = order(turn)
+        up = down[::-1] + (part_steps[:0:-1] if parted else [])
+        return Chain(values, (part_steps if parted else []) + down, up)
+
+    wide = w_up.shape[1]
+    cut = wide * 2 // 3
+    near = [m for m in range(1, rows) if m & (m - 1) == 0]
+    far = [m for m in range(1, rows) if m & (m - 1)]
+
+    received = [g if s == 0 else swap(g, "pos", s) for s, g in enumerate(grad_mixed)]
+    layer_slabs = {m: send_back(layer_out, m) for m in [0] + near}
+    down = chain(matmul(flat(hidden), flat(own_cotangent), TN).astype(BF16), 0)
+    received, layer_slabs, layer_out, grad_upper = close(
+        [down], received, layer_slabs, layer_out, grad_upper
+    )
+    down.advance()
+    layer_slabs.update({m: send_back(layer_out, m) for m in far})
     stacked = jnp.stack(mixed_parts)
     mixed = jnp.concatenate([flat(take(stacked, g ^ part)) for g in range(parts)], axis=1)
-    grad_w_up = jnp.concatenate(
-        [
-            matmul(flat(act_two), flat(grad_upper), TN).astype(BF16),
-            matmul(mixed, flat(grad_attn), TN).astype(BF16),
-        ],
-        axis=1,
-    )
-    share_up = halve(grad_w_up, part_steps)
-    rest_down, rest_up = own_steps + row_steps, own_steps[::-1] + row_steps
-
-    grads = []
-    stage = 0
+    grad_up_flat = flat(grad_upper)
+    up_one = chain(matmul(flat(act_two), grad_up_flat[:, :cut], TN).astype(BF16), 1)
+    up_two = chain(
+        jnp.concatenate(
+            [
+                matmul(flat(act_two), grad_up_flat[:, cut:], TN).astype(BF16),
+                matmul(mixed, flat(grad_attn), TN).astype(BF16),
+            ],
+            axis=1,
+        ),
+        2,
+    )
+    chains = [down, up_one, up_two]
+    received, layer_slabs = close(chains, received, layer_slabs)
+    layer_home = arrange([layer_slabs[m] for m in range(rows)])
+    up_one.advance()
+    up_two.advance()
+    for _ in part_steps[1:]:
+        for c in chains:
+            c.advance()
+    grad_t = jnp.concatenate(received, axis=0).transpose(0, 2, 1)
+    grad_t, layer_home = close(chains, grad_t, layer_home)
+
+    grads, shares = [], []
     for h, count in groups:
-        grad_t, share_down, share_up, grads, layer_home = lax.optimization_barrier(
-            (grad_t, share_down, share_up, grads, layer_home)
+        for c in chains + shares:
+            c.advance()
+        grad = attention_backward(
+            phys, flags, query_t, grad_t, out_t, lse, info, key, key_t, value, count, h
         )
-        grads = grads + [
-            attention_backward(
-                phys, flags, query_t, grad_t, out_t, lse, info, key, key_t, value, count, h
-            )
-        ]
-        share_down = halve(share_down, rest_down[stage : stage + 1])
-        share_up = halve(share_up, rest_up[stage : stage + 1])
-        stage += 1
-    share_down = double(halve(share_down, rest_down[stage:]), part_steps[1:] + rest_down)
-    share_up = double(halve(share_up, rest_up[stage:]), part_steps[1:] + rest_up)
-    axis, mask, bit = part_steps[0]
-    (sum_w_down,) = join(share_down, swap(share_down, axis, mask), bit, (model,))
-    sum_w_up, sum_w_out = join(
-        share_up, swap(share_up, axis, mask), bit, (w_up.shape[1], model)
-    )
-
-    grad_act = sum(matmul(flat(g), w, NT) for g, w in zip(grads, w_groups))
-    grad_act_own = grad_act[:local]
-    for s in range(1, parts):
-        sent = grad_act[s * local : (s + 1) * local].astype(BF16)
-        grad_act_own = grad_act_own + swap(sent, "pos", s).astype(F32)
-    inputs = flat(mine).astype(F32)
-    _, norm_one_pull = jax.vjp(layer_norm, inputs, attn_gain.astype(F32), attn_shift.astype(F32))
-    grad_input_norm, grad_attn_gain, grad_attn_shift = norm_one_pull(grad_act_own)
-    tokens_grad = (flat(grad_resid) + grad_input_norm).astype(BF16).reshape(rows, size, model)
-
-    summed = []
-    for g in grads:
-        share = matmul(flat(act_one), flat(g), TN).astype(BF16)
-        summed.append(double(halve(share, rest_up), rest_up))
-    pieces = [summed] + [[swap(g, "pos", s) for g in summed] for s in range(1, parts)]
-    sum_w_qkv = spread(pieces, part, spans)
+        grad, grad_t = close(chains + shares, grad, grad_t)
+        grads.append(grad)
+        shares.append(chain(matmul(flat(act_one), flat(grad), TN).astype(BF16), 0, False))
+        if len(grads) < len(groups):
+            (grad_t,) = close(chains + shares, grad_t)
 
     def column_sums(which):
         return jnp.concatenate(
@@ -764,27 +784,77 @@
             ]
         )
 
-    grad_query_mine, grad_value_mine = column_sums(0), column_sums(2)
-
     def placed(values):
         return lax.dynamic_update_slice_in_dim(jnp.zeros((model,), F32), values, part * width, 0)
 
+    for c in chains + shares:
+        c.advance()
+    grad_act = sum(matmul(flat(g), w, NT) for g, w in zip(grads, w_groups))
+    grad_act_own = grad_act[:local]
+    for s in range(1, parts):
+        sent = grad_act[s * local : (s + 1) * local].astype(BF16)
+        grad_act_own = grad_act_own + swap(sent, "pos", s).astype(F32)
+    sums_q, sums_v = placed(column_sums(0)), placed(column_sums(2))
+    grad_act_own, sums_q, sums_v = close(chains + shares, grad_act_own, sums_q, sums_v)
+
+    for c in chains + shares:
+        c.advance()
+    inputs = flat(mine).astype(F32)
+    _, norm_one_pull = jax.vjp(layer_norm, inputs, attn_gain.astype(F32), attn_shift.astype(F32))
+    grad_input_norm, grad_attn_gain, grad_attn_shift = norm_one_pull(grad_act_own)
+    tokens_grad = (flat(grad_resid) + grad_input_norm).astype(BF16).reshape(rows, size, model)
     small = jnp.concatenate(
         [
             grad_attn_gain,
             grad_attn_shift,
-            placed(grad_query_mine),
-            placed(grad_value_mine),
+            sums_q,
+            sums_v,
             sums[:4].reshape(-1),
             up_sum[0],
         ]
     )
-    for axis, mask, _ in part_steps + rest_down:
+    tokens_grad, small = close(chains + shares, tokens_grad, small)
+
+    small_steps = part_steps + own_steps + row_steps
+    token_slabs = {}
+    waves = [[0] + near, far]
+    while any(c.left for c in chains):
+        for c in chains + shares:
+            c.advance()
+        if small_steps:
+            axis, mask, _ = small_steps.pop(0)
+            small = small + swap(small, axis, mask)
+        if waves:
+            token_slabs.update({m: send_back(tokens_grad, m) for m in waves.pop(0)})
+        small, token_slabs, tokens_grad = close(chains + shares, small, token_slabs, tokens_grad)
+
+    axis, mask, bit = part_steps[0]
+    others = [swap(c.values, axis, mask) for c in chains]
+    for c in shares:
+        c.advance()
+    for axis, mask, _ in small_steps:
         small = small + swap(small, axis, mask)
+    others, small = close(chains + shares, others, small)
+    (sum_w_down,) = join([down.values], others[:1], bit, ((0, 0, 0, 0, model),), (model,))
+    sum_w_up, sum_w_out = join(
+        [up_one.values, up_two.values],
+        others[1:],
+        bit,
+        ((0, 0, 0, 0, cut), (1, 0, 0, cut, wide - cut), (1, wide - cut, 1, 0, model)),
+        (wide, model),
+    )
+    tokens_home = arrange([token_slabs[m] for m in range(rows)])
+    while any(c.left for c in shares):
+        for c in shares:
+            c.advance()
+    summed = [c.values for c in shares]
+    pieces = [summed] + [[swap(g, "pos", s) for g in summed] for s in range(1, parts)]
+    sum_w_qkv = spread(pieces, part, spans)
+
     vectors = small[: 8 * model].reshape(8, model)
     return (
         layer_home,
-        give_back(tokens_grad),
+        tokens_home,
         vectors[0],
         vectors[1],
         sum_w_qkv,

time: 541 us -> 511 us (0.945)
  waiting for transfers between devices: 153 us -> 115 us
  local copies, waits for them, and re-layouts: 52.5 us -> 58.2 us
    ppermute x59 -> x69, waiting for transfers between devices: 153 us -> 115 us  [swap(): return lax.ppermute(values, axis, [(i, i ^ mask) for i in range(count)])]
    dot_general x7 -> x8, matrix products: 28.7 us -> 29.8 us  [matmul(): return lax.dot_general(left, right, dims, preferred_element_type=F32)]
    ppermute x59 -> x69, starting transfers between devices: 70.3 us -> 71.4 us  [swap(): return lax.ppermute(values, axis, [(i, i ^ mask) for i in range(count)])]
    convert_element_type x18 -> x23, other arithmetic: 13.1 us -> 12.3 us  [halve(): (take(two, bit).astype(F32) + arrived.astype(F32)).astype(values.dtype)]
    unnamed x112 -> x144, local copies, waits for them, and re-layouts: 14.1 us -> 14.4 us
  transfers between devices with their start and end apart: 59 -> 69, of which waited for: 24 -> 33; matrix products, arithmetic and copies ran while one was open for 14% -> 17% of each run, Pallas kernels for 21% -> 23%
where the time goes in v4:
time: 511 us; the launch traced here: 505 us
  Pallas kernels  183 us (36%)
  waiting for transfers between devices  115 us (23%)
  starting transfers between devices  71.4 us (14%)
  local copies, waits for them, and re-layouts  58.2 us (11%)
  other arithmetic  39.4 us (8%)
  matrix products  29.8 us (6%)
  between operations  8.48 us (2%)
    ppermute x69, waiting for transfers between devices, swap(): return lax.ppermute(values, axis, [(i, i ^ mask) for i in range(count)])  115 us
    ppermute x69, starting transfers between devices, swap(): return lax.ppermute(values, axis, [(i, i ^ mask) for i in range(count)])  71.4 us
    pallas_call x2, Pallas kernels, attention_backward(): pl.pallas_call(functools.partial(backward_kernel, heads, first, blocks),...  63.3 us
    pallas_call x1, Pallas kernels, attention_forward(): pl.pallas_call(functools.partial(forward_kernel, heads, blocks), grid_spe...  46.6 us
    pallas_call x1, Pallas kernels, feed(): pl.pallas_call(body, grid_spec=pltpu.PrefetchScalarGridSpec(num_scalar_pr...  36.4 us
    dot_general x8, matrix products, matmul(): return lax.dot_general(left, right, dims, preferred_element_type=F32)  29.8 us
    pallas_call x2, Pallas kernels, join(): pl.pallas_call(functools.partial(join_kernel, len(mine), moves), grid_spe...  19.1 us
    unnamed x144, local copies, waits for them, and re-layouts  14.4 us
  transfers between devices with their start and end apart: 69, of which 33 were waited for; matrix products, arithmetic and copies ran while one was open for 17% of the time, Pallas kernels for 23%

profile of v4, /device:TPU:0, one launch (start us, length us, event | category | flops | bytes accessed | tf_op | source)
XLA Modules:
  0.0 505.3 jit_solution(9915758002054642500)
XLA Ops:
  0.7 2.2 dynamic-slice_bitcast_fusion.12
  3.0 3.0 collective-permute-start
  14.6 1.9 select_select_fusion
  23.0 1.9 collective-permute-done.1
  34.2 2.0 fusion.57
  50.0 12.3 %project.1 = (bf16[8,256,768]{2,1,0:T(8,128)(2,1)}, bf16[8,384,256]{2,1,0:T(8,128)(2,1)}, bf16[8,256,384]{2,1,0:T(8,128)(2,1)}, bf16[8,384,256]{2,1,0:T(8,128)(2...) custom-call(bf16[8,256,768]{2,1,0:T(8,128)(2,1)} %copy-done.46, f32[1,768]{1,0:T(1,128)} %reshape.589.gain_ref, ...), custom_call_target="tpu_custom_call" | custom-call | flops 3623878656 | bytes 14155776 | tf_op jit(solution)/shard_map/project/pallas_call | solution.py:274
  62.3 46.6 %attention_forward.1 = (bf16[8,256,384]{2,1,0:T(8,128)(2,1)}, f32[8,384,256]{2,1,0:T(8,128)}, f32[8,8,256]{2,1,0:T(8,128)}) custom-call(s32[8]{0:T(128)} %fusion.76.phys_ref, s32[64]{0:T(128)} %reshape.640.flag_ref, bf16[8,384,256]{2,1,0:T(8,128)(2,1)} %get-tuple-element.142.query_t_ref, bf16[8,256,384]{2,1,0:T(8,128)(2,1)} %get-tuple-element.143.key_ref, ...), custom_call_target="tpu_custom_call" | custom-call | flops 7247757312 | bytes 12582912 | tf_op jit(solution)/shard_map/attention_forward/pallas_call | solution.py:125
  115.4 2.0 constant_dynamic-slice_fusion.2
  117.4 2.3 constant_dynamic-slice_fusion.5
  121.2 36.4 %feed.1 = (bf16[4,256,768]{2,1,0:T(8,128)(2,1)}, bf16[4,256,3072]{2,1,0:T(8,128)(2,1)}, bf16[4,256,3072]{2,1,0:T(8,128)(2,1)}, bf16[4,256,768]{2,1,0:T(8,128)(2,...) custom-call(s32[1]{0:T(128)} %bitcast.p_ref.part_ref, ...), custom_call_target="tpu_custom_call" | custom-call | flops 21743271936 | bytes 25165824 | tf_op jit(solution)/shard_map/feed/pallas_call | solution.py:391
  157.7 2.5 slice_bitcast_fusion.5
  160.1 2.0 collective-permute-start.9
  163.3 8.8 %bitcast_convert_fusion = bf16[3072,768]{1,0:T(8,128)(2,1)S(1)} fusion(bf16[4,256,3072]{2,1,0:T(8,128)(2,1)} %get-tuple-element.149, bf16[4,256,768]{2,1,0:T(8,128)(2,1)S(1)} %copy-done.19), kind=kOutput, calls=%fused_computation | convolution fusion | flops 4834197504 | bytes 12582912 | tf_op jit(solution)/shard_map/dot_general | solution.py:32
  178.3 3.2 fusion.20
  184.1 1.8 fusion.12
  186.2 4.9 fusion.3
  191.0 3.8 fusion
  205.7 2.0 copy-done.11
  209.2 3.2 collective-permute-start.17
  216.5 39.3 %attention_backward.2 = bf16[8,256,768]{2,1,0:T(8,128)(2,1)} custom-call(s32[8]{0:T(128)} %fusion.76.phys_ref, s32[64]{0:T(128)} %reshape.640.flag_ref, bf16[8,384,256]{2,1,0:T(8,128)(2,1)} %get-tuple-element.142.query_t_ref, bf16[8,384,256]{2,1,0:T(8,128)(2,1)} %maximum_bitcast_fusion.grad_t_ref, f32[8,384,256]{2,1,0:T(8,128)} %get-tuple-element.178.out_t_ref, ...), custom_call_target="tpu_custom_call" | custom-call | flops 12079595520 | bytes 10485760 | tf_op jit(solution)/shard_map/attention_backward/pallas_call | solution.py:234
  255.8 2.5 fusion.23
  258.2 2.3 fusion.19
  262.8 2.8 bitcast_convert_fusion.1
  265.6 24.0 %attention_backward.3 = bf16[8,256,384]{2,1,0:T(8,128)(2,1)} custom-call(s32[8]{0:T(128)} %fusion.76.phys_ref, s32[64]{0:T(128)} %reshape.640.flag_ref, bf16[8,384,256]{2,1,0:T(8,128)(2,1)} %get-tuple-element.142.query_t_ref, bf16[8,384,256]{2,1,0:T(8,128)(2,1)} %maximum_bitcast_fusion.grad_t_ref, f32[8,384,256]{2,1,0:T(8,128)} %get-tuple-element.178.out_t_ref, ...), custom_call_target="tpu_custom_call" | custom-call | flops 6039797760 | bytes 5242880 | tf_op jit(solution)/shard_map/attention_backward/pallas_call | solution.py:234
  289.8 2.1 collective-permute-start.20
  291.9 4.8 fusion.25
  296.8 2.1 collective-permute-start.19
  299.3 12.3 %collective-permute-done.20 = bf16[96,1792]{1,0:T(8,128)(2,1)S(1)} collective-permute-done((bf16[96,1792]{1,0:T(8,128)(2,1)S(1)}, bf16[96,1792]{1,0:T(8,128)(2,1)S(1)}, u32[]{:S(2)}, u32[]{:S(2)}) %collective-permute-start.20) | collective-permute-done | bytes 344096 | tf_op jit(solution)/shard_map/ppermute | solution.py:561
  314.1 1.8 fusion.24
  316.2 1.8 convolution_add_fusion
  322.9 8.7 %collective-permute-done.24 = bf16[48,1792]{1,0:T(8,128)(2,1)S(1)} collective-permute-done((bf16[48,1792]{1,0:T(8,128)(2,1)S(1)}, bf16[48,1792]{1,0:T(8,128)(2,1)S(1)}, u32[]{:S(2)}, u32[]{:S(2)}) %collective-permute-start.24) | collective-permute-done | bytes 172064 | tf_op jit(solution)/shard_map/ppermute | solution.py:561
  331.6 3.2 collective-permute-start.22
  335.1 6.2 %collective-permute-done.22 = bf16[192,768]{1,0:T(8,128)(2,1)S(1)} collective-permute-done((bf16[192,768]{1,0:T(8,128)(2,1)S(1)}, bf16[192,768]{1,0:T(8,128)(2,1)S(1)}, u32[]{:S(2)}, u32[]{:S(2)}) %collective-permute-start.22) | collective-permute-done | bytes 294944 | tf_op jit(solution)/shard_map/ppermute | solution.py:561
  343.8 1.9 multiply_reduce_fusion
  348.2 2.8 collective-permute-start.30
  351.2 2.8 collective-permute-start.28
  355.7 5.9 %collective-permute-done.30 = bf16[24,1792]{1,0:T(8,128)(2,1)S(1)} collective-permute-done((bf16[24,1792]{1,0:T(8,128)(2,1)S(1)}, bf16[24,1792]{1,0:T(8,128)(2,1)S(1)}, u32[]{:S(2)}, u32[]{:S(2)}) %collective-permute-start.30) | collective-permute-done | bytes 86048 | tf_op jit(solution)/shard_map/ppermute | solution.py:561
  361.6 2.1 collective-permute-done.29
  363.8 1.8 collective-permute-done.28
  365.9 2.6 collective-permute-start.36
  371.6 2.1 collective-permute-start.34
  373.8 5.3 %collective-permute-done.36 = bf16[48,768]{1,0:T(8,128)(2,1)S(1)} collective-permute-done((bf16[48,768]{1,0:T(8,128)(2,1)S(1)}, bf16[48,768]{1,0:T(8,128)(2,1)S(1)}, u32[]{:S(2)}, u32[]{:S(2)}) %collective-permute-start.36) | collective-permute-done | bytes 73760 | tf_op jit(solution)/shard_map/ppermute | solution.py:561
  381.0 3.6 collective-permute-done.34
  384.7 2.7 collective-permute-done.33
  388.2 2.9 collective-permute-start.44
  395.3 2.3 collective-permute-done.43
  397.6 2.8 collective-permute-done.42
  401.1 5.3 %collective-permute-done.47 = bf16[256,768]{1,0:T(8,128)(2,1)S(1)} collective-permute-done((bf16[256,768]{1,0:T(8,128)(2,1)S(1)}, bf16[256,768]{1,0:T(8,128)(2,1)S(1)}, u32[]{:S(2)}, u32[]{:S(2)}) %collective-permute-start.47) | collective-permute-done | bytes 393248 | tf_op jit(solution)/shard_map/ppermute | solution.py:561
  408.2 2.2 collective-permute-start.51
  413.0 2.1 collective-permute-done.51
  415.2 2.5 collective-permute-done.50
  417.8 2.6 collective-permute-done.49
  420.5 2.8 collective-permute-done.48
  431.0 4.4 collective-permute-done.57
  435.6 5.0 collective-permute-done.56
  440.8 5.8 %collective-permute-done.55 = bf16[192,2048]{1,0:T(8,128)(2,1)S(1)} collective-permute-done((bf16[192,2048]{1,0:T(8,128)(2,1)S(1)}, bf16[192,2048]{1,0:T(8,128)(2,1)S(1)}, u32[]{:S(2)}, u32[]{:S(2)}) %collective-permute-start.55) | collective-permute-done | bytes 786464 | tf_op jit(solution)/shard_map/ppermute | solution.py:561
  446.8 4.6 collective-permute-done.54
  455.6 3.5 collective-permute-done.65
  459.6 4.6 collective-permute-done.61
  464.3 3.8 collective-permute-done.60
  471.3 6.6 %collective-permute-done.66 = bf16[384,384]{1,0:T(8,128)(2,1)S(1)} collective-permute-done((bf16[384,384]{1,0:T(8,128)(2,1)S(1)}, bf16[384,384]{1,0:T(8,128)(2,1)S(1)}, u32[]{:S(2)}, u32[]{:S(2)}) %collective-permute-start.66) | collective-permute-done | bytes 294944 | tf_op jit(solution)/shard_map/ppermute | solution.py:561
  478.9 11.3 %join.3 = f32[3072,768]{1,0:T(8,128)} custom-call(s32[1]{0:T(128)} %bitcast.130.bit_ref, bf16[1536,768]{1,0:T(8,128)(2,1)} %copy-done.6, bf16[1536,768]{1,0:T(8,128)(2,1)} %copy-done.17), custom_call_target="tpu_custom_call" | custom-call | flops 2359296 | bytes 14155776 | tf_op jit(solution)/shard_map/join/pallas_call | solution.py:464
  490.3 7.7 %join.2 = (f32[768,3072]{1,0:T(8,128)}, f32[768,768]{1,0:T(8,128)}) custom-call(s32[1]{0:T(128)} %bitcast.130.bit_ref, bf16[384,2048]{1,0:T(8,128)(2,1)} %copy-done.7, bf16[384,1792]{1,0:T(8,128)(2,1)} %copy-done.8, bf16[384,2048]{1,0:T(8,128)(2,1)} %copy-done.28, bf16[384,1792]{1,0:T(8,128)(2,1)} %copy-done.32), custom_call_target="tpu_custom_call" | custom-call | flops 2949120 | bytes 17694720 | tf_op jit(solution)/shard_map/join/pallas_call | solution.py:464
  499.6 5.5 %spread.1 = f32[768,2304]{1,0:T(8,128)} custom-call(s32[1]{0:T(128)} %bitcast.p_ref.part_ref, bf16[768,768]{1,0:T(8,128)(2,1)} %pad_maximum_fusion.8.refs_0_, bf16[768,384]{1,0:T(8,128)(2,1)} %copy-done.18, bf16[768,768]{1,0:T(8,128)(2,1)} %copy-done.33, bf16[768,384]{1,0:T(8,128)(2,1)} %collective-permute-done.68.refs_3_), custom_call_target="tpu_custom_call" | custom-call | flops 1769472 | bytes 10616832 | tf_op jit(solution)/shard_map/spread/pallas_call | solution.py:507
  (422 shorter events, 118.5 us)
Async XLA Ops:
  3.0 20.0 %collective-permute-start = (bf16[256,768]{1,0:T(8,128)(2,1)S(1)}, bf16[256,768]{1,0:T(8,128)(2,1)S(1)}, u32[]{:S(2)}, u32[]{:S(2)}) collective-permute-start(bf16[256,768]{1,0:T(8,128)(2,1)S(1)} %get-tuple-element.312), channel_id=1, source_target_pairs={{0,2},{1,3},{2,0},{3,1},{4,6},{5,7},{6,4},{7,5},{8,10},{9,11},{10,... | collective-permute-start | bytes 1179656 | tf_op jit(solution)/shard_map/ppermute | solution.py:561
  5.9 19.0 %collective-permute-start.1 = (bf16[256,768]{1,0:T(8,128)(2,1)S(1)}, bf16[256,768]{1,0:T(8,128)(2,1)S(1)}, u32[]{:S(2)}, u32[]{:S(2)}) collective-permute-start(bf16[256,768]{1,0:T(8,128)(2,1)S(1)} %get-tuple-element.315), channel_id=1, source_target_pairs={{0,4},{1,5},{2,6},{3,7},{4,0},{5,1},{6,2},{7,3},{8,12},{9,13},{10,... | collective-permute-start | bytes 1179656 | tf_op jit(solution)/shard_map/ppermute | solution.py:561
  7.4 17.5 %collective-permute-start.2 = (bf16[256,768]{1,0:T(8,128)(2,1)S(1)}, bf16[256,768]{1,0:T(8,128)(2,1)S(1)}, u32[]{:S(2)}, u32[]{:S(2)}) collective-permute-start(bf16[256,768]{1,0:T(8,128)(2,1)S(1)} %get-tuple-element.311), channel_id=1, source_target_pairs={{0,6},{1,7},{2,4},{3,5},{4,2},{5,3},{6,0},{7,1},{8,14},{9,15},{10,... | collective-permute-start | bytes 1179656 | tf_op jit(solution)/shard_map/ppermute | solution.py:561
  25.8 17.5 %collective-permute-start.3 = (bf16[4,256,768]{2,1,0:T(8,128)(2,1)S(1)}, bf16[4,256,768]{2,1,0:T(8,128)(2,1)S(1)}, u32[]{:S(2)}, u32[]{:S(2)}) collective-permute-start(bf16[4,256,768]{2,1,0:T(8,128)(2,1)S(1)} %get-tuple-element.276.refs_2_), channel_id=1, source_target_pairs={{0,1},{1,0},{2,3},{3,2},{4,5},{5,4},{6,7},{7,6},{8,9},{9,8},{10,11... | collective-permute-start | bytes 4718600 | tf_op jit(solution)/shard_map/ppermute | solution.py:561
  46.5 62.3 %collective-permute-start.4 = (bf16[256,768]{1,0:T(8,128)(2,1)}, bf16[256,768]{1,0:T(8,128)(2,1)S(1)}, u32[]{:S(2)}, u32[]{:S(2)}) collective-permute-start(bf16[256,768]{1,0:T(8,128)(2,1)} %get-tuple-element.310), channel_id=1, source_target_pairs={{0,2},{1,3},{2,0},{3,1},{4,6},{5,7},{6,4},{7,5},{8,10},{9,11},{10,... | collective-permute-start | bytes 1179656 | tf_op jit(solution)/shard_map/ppermute | solution.py:561
  47.7 61.1 %collective-permute-start.5 = (bf16[256,768]{1,0:T(8,128)(2,1)S(1)}, bf16[256,768]{1,0:T(8,128)(2,1)S(1)}, u32[]{:S(2)}, u32[]{:S(2)}) collective-permute-start(bf16[256,768]{1,0:T(8,128)(2,1)S(1)} %get-tuple-element.309), channel_id=1, source_target_pairs={{0,4},{1,5},{2,6},{3,7},{4,0},{5,1},{6,2},{7,3},{8,12},{9,13},{10,... | collective-permute-start | bytes 1179656 | tf_op jit(solution)/shard_map/ppermute | solution.py:561
  48.6 60.3 %collective-permute-start.6 = (bf16[256,768]{1,0:T(8,128)(2,1)S(1)}, bf16[256,768]{1,0:T(8,128)(2,1)S(1)}, u32[]{:S(2)}, u32[]{:S(2)}) collective-permute-start(bf16[256,768]{1,0:T(8,128)(2,1)S(1)} %get-tuple-element.308), channel_id=1, source_target_pairs={{0,6},{1,7},{2,4},{3,5},{4,2},{5,3},{6,0},{7,1},{8,14},{9,15},{10,... | collective-permute-start | bytes 1179656 | tf_op jit(solution)/shard_map/ppermute | solution.py:561
  112.3 7.9 %collective-permute-start.7 = (bf16[4,256,384]{2,1,0:T(8,128)(2,1)}, bf16[4,256,384]{2,1,0:T(8,128)(2,1)S(1)}, u32[]{:S(2)}, u32[]{:S(2)}) collective-permute-start(bf16[4,256,384]{2,1,0:T(8,128)(2,1)} %get-tuple-element.302), channel_id=1, source_target_pairs={{0,1},{1,0},{2,3},{3,2},{4,5},{5,4},{6,7},{7,6},{8,9},{9,8},{10,11... | collective-permute-start | bytes 2359304 | tf_op jit(solution)/shard_map/ppermute | solution.py:561
  160.1 12.0 %collective-permute-start.10 = (bf16[256,768]{1,0:T(8,128)(2,1)}, bf16[256,768]{1,0:T(8,128)(2,1)}, u32[]{:S(2)}, u32[]{:S(2)}) collective-permute-start(bf16[256,768]{1,0:T(8,128)(2,1)} %get-tuple-element.304), channel_id=1, source_target_pairs={{0,4},{1,5},{2,6},{3,7},{4,0},{5,1},{6,2},{7,3},{8,12},{9,13},{10,... | collective-permute-start | bytes 1179656 | tf_op jit(solution)/shard_map/ppermute | solution.py:561
  160.1 12.0 %collective-permute-start.9 = (bf16[256,768]{1,0:T(8,128)(2,1)S(1)}, bf16[256,768]{1,0:T(8,128)(2,1)}, u32[]{:S(2)}, u32[]{:S(2)}) collective-permute-start(bf16[256,768]{1,0:T(8,128)(2,1)S(1)} %get-tuple-element.305), channel_id=1, source_target_pairs={{0,2},{1,3},{2,0},{3,1},{4,6},{5,7},{6,4},{7,5},{8,10},{9,11},{10,... | collective-permute-start | bytes 1179656 | tf_op jit(solution)/shard_map/ppermute | solution.py:561
  163.3 8.8 %collective-permute-start.8 = (bf16[4,256,384]{1,2,0:T(8,128)(2,1)}, bf16[4,256,384]{1,2,0:T(8,128)(2,1)S(1)}, u32[]{:S(2)}, u32[]{:S(2)}) collective-permute-start(bf16[4,256,384]{1,2,0:T(8,128)(2,1)} %copy.50), channel_id=1, source_target_pairs={{0,1},{1,0},{2,3},{3,2},{4,5},{5,4},{6,7},{7,6},{8,9},{9,8},{10,11... | collective-permute-start | bytes 2359304 | tf_op jit(solution)/shard_map/ppermute | solution.py:561
  175.0 16.0 %collective-permute-start.11 = (bf16[1536,768]{1,0:T(8,128)(2,1)}, bf16[1536,768]{1,0:T(8,128)(2,1)}, u32[]{:S(2)}, u32[]{:S(2)}) collective-permute-start(bf16[1536,768]{1,0:T(8,128)(2,1)} %dynamic-slice_bitcast_fusion), channel_id=1, source_target_pairs={{0,1},{1,0},{2,3},{3,2},{4,5},{5,4},{6,7},{7,6},{8,9},{9,8},{10,11... | collective-permute-start | bytes 7077896 | tf_op jit(solution)/shard_map/ppermute | solution.py:561
  182.6 12.3 %collective-permute-start.12 = (bf16[256,768]{1,0:T(8,128)(2,1)S(1)}, bf16[256,768]{1,0:T(8,128)(2,1)}, u32[]{:S(2)}, u32[]{:S(2)}) collective-permute-start(bf16[256,768]{1,0:T(8,128)(2,1)S(1)} %slice_bitcast_fusion.4), channel_id=1, source_target_pairs={{0,6},{1,7},{2,4},{3,5},{4,2},{5,3},{6,0},{7,1},{8,14},{9,15},{10,... | collective-permute-start | bytes 1179656 | tf_op jit(solution)/shard_map/ppermute | solution.py:561
  196.4 8.8 %collective-permute-start.14 = (bf16[384,1792]{1,0:T(8,128)(2,1)S(1)}, bf16[384,1792]{1,0:T(8,128)(2,1)S(1)}, u32[]{:S(2)}, u32[]{:S(2)}) collective-permute-start(bf16[384,1792]{1,0:T(8,128)(2,1)S(1)} %dynamic-slice_bitcast_fusion.2), channel_id=1, source_target_pairs={{0,1},{1,0},{2,3},{3,2},{4,5},{5,4},{6,7},{7,6},{8,9},{9,8},{10,11... | collective-permute-start | bytes 4128776 | tf_op jit(solution)/shard_map/ppermute | solution.py:561
  198.1 7.6 %collective-permute-start.13 = (bf16[384,2048]{1,0:T(8,128)(2,1)S(1)}, bf16[384,2048]{1,0:T(8,128)(2,1)S(1)}, u32[]{:S(2)}, u32[]{:S(2)}) collective-permute-start(bf16[384,2048]{1,0:T(8,128)(2,1)S(1)} %dynamic-slice_bitcast_fusion.1), channel_id=1, source_target_pairs={{0,1},{1,0},{2,3},{3,2},{4,5},{5,4},{6,7},{7,6},{8,9},{9,8},{10,11... | collective-permute-start | bytes 4718600 | tf_op jit(solution)/shard_map/ppermute | solution.py:561
  209.2 46.6 %collective-permute-start.17 = (bf16[192,1792]{1,0:T(8,128)(2,1)}, bf16[192,1792]{1,0:T(8,128)(2,1)}, u32[]{:S(2)}, u32[]{:S(2)}) collective-permute-start(bf16[192,1792]{1,0:T(8,128)(2,1)} %dynamic-slice_bitcast_fusion.5), channel_id=1, source_target_pairs={{0,8},{8,0},{16,24},{24,16},{1,9},{9,1},{17,25},{25,17},{2,10},{10... | collective-permute-start | bytes 2064392 | tf_op jit(solution)/shard_map/ppermute | solution.py:561
  213.3 45.0 %collective-permute-start.16 = (bf16[192,2048]{1,0:T(8,128)(2,1)}, bf16[192,2048]{1,0:T(8,128)(2,1)}, u32[]{:S(2)}, u32[]{:S(2)}) collective-permute-start(bf16[192,2048]{1,0:T(8,128)(2,1)} %dynamic-slice_bitcast_fusion.4), channel_id=1, source_target_pairs={{0,4},{1,5},{2,6},{3,7},{4,0},{5,1},{6,2},{7,3},{8,12},{9,13},{10,... | collective-permute-start | bytes 2359304 | tf_op jit(solution)/shard_map/ppermute | solution.py:561
  215.7 44.9 %collective-permute-start.15 = (bf16[768,768]{1,0:T(8,128)(2,1)}, bf16[768,768]{1,0:T(8,128)(2,1)}, u32[]{:S(2)}, u32[]{:S(2)}) collective-permute-start(bf16[768,768]{1,0:T(8,128)(2,1)} %dynamic-slice_bitcast_fusion.3), channel_id=1, source_target_pairs={{0,2},{1,3},{2,0},{3,1},{4,6},{5,7},{6,4},{7,5},{8,10},{9,11},{10,... | collective-permute-start | bytes 3538952 | tf_op jit(solution)/shard_map/ppermute | solution.py:561
  289.7 22.1 %collective-permute-start.21 = (bf16[384,768]{1,0:T(8,128)(2,1)S(1)}, bf16[384,768]{1,0:T(8,128)(2,1)S(1)}, u32[]{:S(2)}, u32[]{:S(2)}) collective-permute-start(bf16[384,768]{1,0:T(8,128)(2,1)S(1)} %dynamic-slice_bitcast_fusion.6), channel_id=1, source_target_pairs={{0,2},{1,3},{2,0},{3,1},{4,6},{5,7},{6,4},{7,5},{8,10},{9,11},{10,... | collective-permute-start | bytes 1769480 | tf_op jit(solution)/shard_map/ppermute | solution.py:561
  289.8 21.7 %collective-permute-start.20 = (bf16[96,1792]{1,0:T(8,128)(2,1)S(1)}, bf16[96,1792]{1,0:T(8,128)(2,1)S(1)}, u32[]{:S(2)}, u32[]{:S(2)}) collective-permute-start(bf16[96,1792]{1,0:T(8,128)(2,1)S(1)} %dynamic-slice_bitcast_fusion.15), channel_id=1, source_target_pairs={{0,2},{1,3},{2,0},{3,1},{4,6},{5,7},{6,4},{7,5},{8,10},{9,11},{10,... | collective-permute-start | bytes 1032200 | tf_op jit(solution)/shard_map/ppermute | solution.py:561
  296.8 14.9 %collective-permute-start.19 = (bf16[96,2048]{1,0:T(8,128)(2,1)S(1)}, bf16[96,2048]{1,0:T(8,128)(2,1)S(1)}, u32[]{:S(2)}, u32[]{:S(2)}) collective-permute-start(bf16[96,2048]{1,0:T(8,128)(2,1)S(1)} %dynamic-slice_bitcast_fusion.8), channel_id=1, source_target_pairs={{0,8},{8,0},{16,24},{24,16},{1,9},{9,1},{17,25},{25,17},{2,10},{10... | collective-permute-start | bytes 1179656 | tf_op jit(solution)/shard_map/ppermute | solution.py:561
  298.9 13.9 %collective-permute-start.18 = (bf16[384,768]{1,0:T(8,128)(2,1)S(1)}, bf16[384,768]{1,0:T(8,128)(2,1)S(1)}, u32[]{:S(2)}, u32[]{:S(2)}) collective-permute-start(bf16[384,768]{1,0:T(8,128)(2,1)S(1)} %dynamic-slice_bitcast_fusion.7), channel_id=1, source_target_pairs={{0,4},{1,5},{2,6},{3,7},{4,0},{5,1},{6,2},{7,3},{8,12},{9,13},{10,... | collective-permute-start | bytes 1769480 | tf_op jit(solution)/shard_map/ppermute | solution.py:561
  318.2 23.2 %collective-permute-start.27 = (bf16[1024,768]{1,0:T(8,128)(2,1)S(1)}, bf16[1024,768]{1,0:T(8,128)(2,1)S(1)}, u32[]{:S(2)}, u32[]{:S(2)}) collective-permute-start(bf16[1024,768]{1,0:T(8,128)(2,1)S(1)} %slice.219), channel_id=1, source_target_pairs={{0,1},{1,0},{2,3},{3,2},{4,5},{5,4},{6,7},{7,6},{8,9},{9,8},{10,11... | collective-permute-start | bytes 4718600 | tf_op jit(solution)/shard_map/ppermute | solution.py:561
  318.3 16.6 %collective-permute-start.26 = (bf16[384,384]{1,0:T(8,128)(2,1)S(1)}, bf16[384,384]{1,0:T(8,128)(2,1)S(1)}, u32[]{:S(2)}, u32[]{:S(2)}) collective-permute-start(bf16[384,384]{1,0:T(8,128)(2,1)S(1)} %dynamic-slice_bitcast_fusion.16), channel_id=1, source_target_pairs={{0,2},{1,3},{2,0},{3,1},{4,6},{5,7},{6,4},{7,5},{8,10},{9,11},{10,... | collective-permute-start | bytes 884744 | tf_op jit(solution)/shard_map/ppermute | solution.py:561
  318.7 16.3 %collective-permute-start.25 = (bf16[192,768]{1,0:T(8,128)(2,1)S(1)}, bf16[192,768]{1,0:T(8,128)(2,1)S(1)}, u32[]{:S(2)}, u32[]{:S(2)}) collective-permute-start(bf16[192,768]{1,0:T(8,128)(2,1)S(1)} %dynamic-slice_bitcast_fusion.17), channel_id=1, source_target_pairs={{0,4},{1,5},{2,6},{3,7},{4,0},{5,1},{6,2},{7,3},{8,12},{9,13},{10,... | collective-permute-start | bytes 884744 | tf_op jit(solution)/shard_map/ppermute | solution.py:561
  320.5 11.1 %collective-permute-start.24 = (bf16[48,1792]{1,0:T(8,128)(2,1)S(1)}, bf16[48,1792]{1,0:T(8,128)(2,1)S(1)}, u32[]{:S(2)}, u32[]{:S(2)}) collective-permute-start(bf16[48,1792]{1,0:T(8,128)(2,1)S(1)} %dynamic-slice_bitcast_fusion.20), channel_id=1, source_target_pairs={{0,4},{1,5},{2,6},{3,7},{4,0},{5,1},{6,2},{7,3},{8,12},{9,13},{10,... | collective-permute-start | bytes 516104 | tf_op jit(solution)/shard_map/ppermute | solution.py:561
  320.9 13.9 %collective-permute-start.23 = (bf16[48,2048]{1,0:T(8,128)(2,1)S(1)}, bf16[48,2048]{1,0:T(8,128)(2,1)S(1)}, u32[]{:S(2)}, u32[]{:S(2)}) collective-permute-start(bf16[48,2048]{1,0:T(8,128)(2,1)S(1)} %dynamic-slice_bitcast_fusion.19), channel_id=1, source_target_pairs={{0,2},{1,3},{2,0},{3,1},{4,6},{5,7},{6,4},{7,5},{8,10},{9,11},{10,... | collective-permute-start | bytes 589832 | tf_op jit(solution)/shard_map/ppermute | solution.py:561
  331.6 9.7 %collective-permute-start.22 = (bf16[192,768]{1,0:T(8,128)(2,1)S(1)}, bf16[192,768]{1,0:T(8,128)(2,1)S(1)}, u32[]{:S(2)}, u32[]{:S(2)}) collective-permute-start(bf16[192,768]{1,0:T(8,128)(2,1)S(1)} %dynamic-slice_bitcast_fusion.18), channel_id=1, source_target_pairs={{0,8},{8,0},{16,24},{24,16},{1,9},{9,1},{17,25},{25,17},{2,10},{10... | collective-permute-start | bytes 884744 | tf_op jit(solution)/shard_map/ppermute | solution.py:561
  345.7 17.9 %collective-permute-start.32 = (bf16[192,384]{1,0:T(8,128)(2,1)S(1)}, bf16[192,384]{1,0:T(8,128)(2,1)S(1)}, u32[]{:S(2)}, u32[]{:S(2)}) collective-permute-start(bf16[192,384]{1,0:T(8,128)(2,1)S(1)} %dynamic-slice_bitcast_fusion.21), channel_id=1, source_target_pairs={{0,4},{1,5},{2,6},{3,7},{4,0},{5,1},{6,2},{7,3},{8,12},{9,13},{10,... | collective-permute-start | bytes 442376 | tf_op jit(solution)/shard_map/ppermute | solution.py:561
  346.4 17.4 %collective-permute-start.31 = (bf16[96,768]{1,0:T(8,128)(2,1)S(1)}, bf16[96,768]{1,0:T(8,128)(2,1)S(1)}, u32[]{:S(2)}, u32[]{:S(2)}) collective-permute-start(bf16[96,768]{1,0:T(8,128)(2,1)S(1)} %dynamic-slice_bitcast_fusion.22), channel_id=1, source_target_pairs={{0,8},{8,0},{16,24},{24,16},{1,9},{9,1},{17,25},{25,17},{2,10},{10... | collective-permute-start | bytes 442376 | tf_op jit(solution)/shard_map/ppermute | solution.py:561
  348.2 13.3 %collective-permute-start.30 = (bf16[24,1792]{1,0:T(8,128)(2,1)S(1)}, bf16[24,1792]{1,0:T(8,128)(2,1)S(1)}, u32[]{:S(2)}, u32[]{:S(2)}) collective-permute-start(bf16[24,1792]{1,0:T(8,128)(2,1)S(1)} %dynamic-slice_bitcast_fusion.25), channel_id=1, source_target_pairs={{0,16},{8,24},{16,0},{24,8},{1,17},{9,25},{17,1},{25,9},{2,18},{10... | collective-permute-start | bytes 258056 | tf_op jit(solution)/shard_map/ppermute | solution.py:561
  351.0 12.7 %collective-permute-start.29 = (bf16[24,2048]{1,0:T(8,128)(2,1)S(1)}, bf16[24,2048]{1,0:T(8,128)(2,1)S(1)}, u32[]{:S(2)}, u32[]{:S(2)}) collective-permute-start(bf16[24,2048]{1,0:T(8,128)(2,1)S(1)} %dynamic-slice_bitcast_fusion.24), channel_id=1, source_target_pairs={{0,16},{8,24},{16,0},{24,8},{1,17},{9,25},{17,1},{25,9},{2,18},{10... | collective-permute-start | bytes 294920 | tf_op jit(solution)/shard_map/ppermute | solution.py:561
  351.2 14.4 %collective-permute-start.28 = (bf16[96,768]{1,0:T(8,128)(2,1)S(1)}, bf16[96,768]{1,0:T(8,128)(2,1)S(1)}, u32[]{:S(2)}, u32[]{:S(2)}) collective-permute-start(bf16[96,768]{1,0:T(8,128)(2,1)S(1)} %dynamic-slice_bitcast_fusion.23), channel_id=1, source_target_pairs={{0,16},{8,24},{16,0},{24,8},{1,17},{9,25},{17,1},{25,9},{2,18},{10... | collective-permute-start | bytes 442376 | tf_op jit(solution)/shard_map/ppermute | solution.py:561
  365.8 5.9 %collective-permute-start.37 = (bf16[96,384]{1,0:T(8,128)(2,1)S(1)}, bf16[96,384]{1,0:T(8,128)(2,1)S(1)}, u32[]{:S(2)}, u32[]{:S(2)}) collective-permute-start(bf16[96,384]{1,0:T(8,128)(2,1)S(1)} %dynamic-slice_bitcast_fusion.26), channel_id=1, source_target_pairs={{0,8},{8,0},{16,24},{24,16},{1,9},{9,1},{17,25},{25,17},{2,10},{10... | collective-permute-start | bytes 221192 | tf_op jit(solution)/shard_map/ppermute | solution.py:561
  365.9 13.2 %collective-permute-start.36 = (bf16[48,768]{1,0:T(8,128)(2,1)S(1)}, bf16[48,768]{1,0:T(8,128)(2,1)S(1)}, u32[]{:S(2)}, u32[]{:S(2)}) collective-permute-start(bf16[48,768]{1,0:T(8,128)(2,1)S(1)} %dynamic-slice_bitcast_fusion.27), channel_id=1, source_target_pairs={{0,16},{8,24},{16,0},{24,8},{1,17},{9,25},{17,1},{25,9},{2,18},{10... | collective-permute-start | bytes 221192 | tf_op jit(solution)/shard_map/ppermute | solution.py:561
  368.4 12.5 %collective-permute-start.35 = (bf16[24,1792]{1,0:T(8,128)(2,1)S(1)}, bf16[24,1792]{1,0:T(8,128)(2,1)S(1)}, u32[]{:S(2)}, u32[]{:S(2)}) collective-permute-start(bf16[24,1792]{1,0:T(8,128)(2,1)S(1)} %fusion.51), channel_id=1, source_target_pairs={{0,16},{8,24},{16,0},{24,8},{1,17},{9,25},{17,1},{25,9},{2,18},{10... | collective-permute-start | bytes 258056 | tf_op jit(solution)/shard_map/ppermute | solution.py:561
  368.9 18.5 %collective-permute-start.39 = (bf16[256,768]{1,0:T(8,128)(2,1)S(1)}, bf16[256,768]{1,0:T(8,128)(2,1)S(1)}, u32[]{:S(2)}, u32[]{:S(2)}) collective-permute-start(bf16[256,768]{1,0:T(8,128)(2,1)S(1)} %get-tuple-element.297), channel_id=1, source_target_pairs={{0,2},{1,3},{2,0},{3,1},{4,6},{5,7},{6,4},{7,5},{8,10},{9,11},{10,... | collective-permute-start | bytes 1179656 | tf_op jit(solution)/shard_map/ppermute | solution.py:561
  369.7 17.7 %collective-permute-start.40 = (bf16[256,768]{1,0:T(8,128)(2,1)S(1)}, bf16[256,768]{1,0:T(8,128)(2,1)S(1)}, u32[]{:S(2)}, u32[]{:S(2)}) collective-permute-start(bf16[256,768]{1,0:T(8,128)(2,1)S(1)} %get-tuple-element.296), channel_id=1, source_target_pairs={{0,4},{1,5},{2,6},{3,7},{4,0},{5,1},{6,2},{7,3},{8,12},{9,13},{10,... | collective-permute-start | bytes 1179656 | tf_op jit(solution)/shard_map/ppermute | solution.py:561
  371.6 13.0 %collective-permute-start.34 = (bf16[24,2048]{1,0:T(8,128)(2,1)S(1)}, bf16[24,2048]{1,0:T(8,128)(2,1)S(1)}, u32[]{:S(2)}, u32[]{:S(2)}) collective-permute-start(bf16[24,2048]{1,0:T(8,128)(2,1)S(1)} %fusion.50), channel_id=1, source_target_pairs={{0,16},{8,24},{16,0},{24,8},{1,17},{9,25},{17,1},{25,9},{2,18},{10... | collective-permute-start | bytes 294920 | tf_op jit(solution)/shard_map/ppermute | solution.py:561
  379.1 8.2 %collective-permute-start.33 = (bf16[96,768]{1,0:T(8,128)(2,1)S(1)}, bf16[96,768]{1,0:T(8,128)(2,1)S(1)}, u32[]{:S(2)}, u32[]{:S(2)}) collective-permute-start(bf16[96,768]{1,0:T(8,128)(2,1)S(1)} %fusion.49), channel_id=1, source_target_pairs={{0,16},{8,24},{16,0},{24,8},{1,17},{9,25},{17,1},{25,9},{2,18},{10... | collective-permute-start | bytes 442376 | tf_op jit(solution)/shard_map/ppermute | solution.py:561
  387.4 6.4 %collective-permute-start.46 = (f32[9216]{0:T(1024)S(1)}, f32[9216]{0:T(1024)S(1)}, u32[]{:S(2)}, u32[]{:S(2)}) collective-permute-start(f32[9216]{0:T(1024)S(1)} %add.533), channel_id=1, source_target_pairs={{0,2},{1,3},{2,0},{3,1},{4,6},{5,7},{6,4},{7,5},{8,10},{9,11},{10,... | collective-permute-start | bytes 110600 | tf_op jit(solution)/shard_map/ppermute | solution.py:561
  388.2 5.6 %collective-permute-start.45 = (bf16[48,384]{1,0:T(8,128)(2,1)S(1)}, bf16[48,384]{1,0:T(8,128)(2,1)S(1)}, u32[]{:S(2)}, u32[]{:S(2)}) collective-permute-start(bf16[48,384]{1,0:T(8,128)(2,1)S(1)} %dynamic-slice_bitcast_fusion.28), channel_id=1, source_target_pairs={{0,16},{8,24},{16,0},{24,8},{1,17},{9,25},{17,1},{25,9},{2,18},{10... | collective-permute-start | bytes 110600 | tf_op jit(solution)/shard_map/ppermute | solution.py:561
  388.2 7.0 %collective-permute-start.44 = (bf16[48,768]{1,0:T(8,128)(2,1)S(1)}, bf16[48,768]{1,0:T(8,128)(2,1)S(1)}, u32[]{:S(2)}, u32[]{:S(2)}) collective-permute-start(bf16[48,768]{1,0:T(8,128)(2,1)S(1)} %fusion.53), channel_id=1, source_target_pairs={{0,16},{8,24},{16,0},{24,8},{1,17},{9,25},{17,1},{25,9},{2,18},{10... | collective-permute-start | bytes 221192 | tf_op jit(solution)/shard_map/ppermute | solution.py:561
  391.1 6.4 %collective-permute-start.43 = (bf16[48,1792]{1,0:T(8,128)(2,1)S(1)}, bf16[48,1792]{1,0:T(8,128)(2,1)S(1)}, u32[]{:S(2)}, u32[]{:S(2)}) collective-permute-start(bf16[48,1792]{1,0:T(8,128)(2,1)S(1)} %pad_maximum_fusion.20), channel_id=1, source_target_pairs={{0,4},{1,5},{2,6},{3,7},{4,0},{5,1},{6,2},{7,3},{8,12},{9,13},{10,... | collective-permute-start | bytes 516104 | tf_op jit(solution)/shard_map/ppermute | solution.py:561
  392.6 7.8 %collective-permute-start.42 = (bf16[48,2048]{1,0:T(8,128)(2,1)S(1)}, bf16[48,2048]{1,0:T(8,128)(2,1)S(1)}, u32[]{:S(2)}, u32[]{:S(2)}) collective-permute-start(bf16[48,2048]{1,0:T(8,128)(2,1)S(1)} %pad_maximum_fusion.19), channel_id=1, source_target_pairs={{0,2},{1,3},{2,0},{3,1},{4,6},{5,7},{6,4},{7,5},{8,10},{9,11},{10,... | collective-permute-start | bytes 589832 | tf_op jit(solution)/shard_map/ppermute | solution.py:561
  393.8 7.1 %collective-permute-start.41 = (bf16[192,768]{1,0:T(8,128)(2,1)S(1)}, bf16[192,768]{1,0:T(8,128)(2,1)S(1)}, u32[]{:S(2)}, u32[]{:S(2)}) collective-permute-start(bf16[192,768]{1,0:T(8,128)(2,1)S(1)} %pad_maximum_fusion.16), channel_id=1, source_target_pairs={{0,8},{8,0},{16,24},{24,16},{1,9},{9,1},{17,25},{25,17},{2,10},{10... | collective-permute-start | bytes 884744 | tf_op jit(solution)/shard_map/ppermute | solution.py:561
  393.9 12.5 %collective-permute-start.47 = (bf16[256,768]{1,0:T(8,128)(2,1)S(1)}, bf16[256,768]{1,0:T(8,128)(2,1)S(1)}, u32[]{:S(2)}, u32[]{:S(2)}) collective-permute-start(bf16[256,768]{1,0:T(8,128)(2,1)S(1)} %slice_bitcast_fusion), channel_id=1, source_target_pairs={{0,6},{1,7},{2,4},{3,5},{4,2},{5,3},{6,0},{7,1},{8,14},{9,15},{10,... | collective-permute-start | bytes 1179656 | tf_op jit(solution)/shard_map/ppermute | solution.py:561
  406.7 6.2 %collective-permute-start.53 = (f32[9216]{0:T(1024)S(1)}, f32[9216]{0:T(1024)S(1)}, u32[]{:S(2)}, u32[]{:S(2)}) collective-permute-start(f32[9216]{0:T(1024)S(1)} %add.535), channel_id=1, source_target_pairs={{0,4},{1,5},{2,6},{3,7},{4,0},{5,1},{6,2},{7,3},{8,12},{9,13},{10,... | collective-permute-start | bytes 110600 | tf_op jit(solution)/shard_map/ppermute | solution.py:561
  408.2 6.9 %collective-permute-start.51 = (bf16[96,768]{1,0:T(8,128)(2,1)S(1)}, bf16[96,768]{1,0:T(8,128)(2,1)S(1)}, u32[]{:S(2)}, u32[]{:S(2)}) collective-permute-start(bf16[96,768]{1,0:T(8,128)(2,1)S(1)} %pad_maximum_fusion.21), channel_id=1, source_target_pairs={{0,8},{8,0},{16,24},{24,16},{1,9},{9,1},{17,25},{25,17},{2,10},{10... | collective-permute-start | bytes 442376 | tf_op jit(solution)/shard_map/ppermute | solution.py:561
  410.4 7.2 %collective-permute-start.50 = (bf16[96,1792]{1,0:T(8,128)(2,1)S(1)}, bf16[96,1792]{1,0:T(8,128)(2,1)S(1)}, u32[]{:S(2)}, u32[]{:S(2)}) collective-permute-start(bf16[96,1792]{1,0:T(8,128)(2,1)S(1)} %pad_maximum_fusion.15), channel_id=1, source_target_pairs={{0,2},{1,3},{2,0},{3,1},{4,6},{5,7},{6,4},{7,5},{8,10},{9,11},{10,... | collective-permute-start | bytes 1032200 | tf_op jit(solution)/shard_map/ppermute | solution.py:561
  410.8 9.6 %collective-permute-start.49 = (bf16[96,2048]{1,0:T(8,128)(2,1)S(1)}, bf16[96,2048]{1,0:T(8,128)(2,1)S(1)}, u32[]{:S(2)}, u32[]{:S(2)}) collective-permute-start(bf16[96,2048]{1,0:T(8,128)(2,1)S(1)} %pad_maximum_fusion.14), channel_id=1, source_target_pairs={{0,8},{8,0},{16,24},{24,16},{1,9},{9,1},{17,25},{25,17},{2,10},{10... | collective-permute-start | bytes 1179656 | tf_op jit(solution)/shard_map/ppermute | solution.py:561
  411.4 11.9 %collective-permute-start.48 = (bf16[384,768]{1,0:T(8,128)(2,1)S(1)}, bf16[384,768]{1,0:T(8,128)(2,1)S(1)}, u32[]{:S(2)}, u32[]{:S(2)}) collective-permute-start(bf16[384,768]{1,0:T(8,128)(2,1)S(1)} %pad_maximum_fusion.11), channel_id=1, source_target_pairs={{0,4},{1,5},{2,6},{3,7},{4,0},{5,1},{6,2},{7,3},{8,12},{9,13},{10,... | collective-permute-start | bytes 1769480 | tf_op jit(solution)/shard_map/ppermute | solution.py:561
  423.5 7.5 %collective-permute-start.58 = (bf16[96,384]{1,0:T(8,128)(2,1)S(1)}, bf16[96,384]{1,0:T(8,128)(2,1)S(1)}, u32[]{:S(2)}, u32[]{:S(2)}) collective-permute-start(bf16[96,384]{1,0:T(8,128)(2,1)S(1)} %pad_maximum_fusion.23), channel_id=1, source_target_pairs={{0,8},{8,0},{16,24},{24,16},{1,9},{9,1},{17,25},{25,17},{2,10},{10... | collective-permute-start | bytes 221192 | tf_op jit(solution)/shard_map/ppermute | solution.py:561
  425.6 9.9 %collective-permute-start.57 = (bf16[192,768]{1,0:T(8,128)(2,1)S(1)}, bf16[192,768]{1,0:T(8,128)(2,1)S(1)}, u32[]{:S(2)}, u32[]{:S(2)}) collective-permute-start(bf16[192,768]{1,0:T(8,128)(2,1)S(1)} %pad_maximum_fusion.17), channel_id=1, source_target_pairs={{0,4},{1,5},{2,6},{3,7},{4,0},{5,1},{6,2},{7,3},{8,12},{9,13},{10,... | collective-permute-start | bytes 884744 | tf_op jit(solution)/shard_map/ppermute | solution.py:561
  427.1 13.5 %collective-permute-start.56 = (bf16[192,1792]{1,0:T(8,128)(2,1)S(1)}, bf16[192,1792]{1,0:T(8,128)(2,1)S(1)}, u32[]{:S(2)}, u32[]{:S(2)}) collective-permute-start(bf16[192,1792]{1,0:T(8,128)(2,1)S(1)} %pad_maximum_fusion.10), channel_id=1, source_target_pairs={{0,8},{8,0},{16,24},{24,16},{1,9},{9,1},{17,25},{25,17},{2,10},{10... | collective-permute-start | bytes 2064392 | tf_op jit(solution)/shard_map/ppermute | solution.py:561
  428.5 18.1 %collective-permute-start.55 = (bf16[192,2048]{1,0:T(8,128)(2,1)S(1)}, bf16[192,2048]{1,0:T(8,128)(2,1)S(1)}, u32[]{:S(2)}, u32[]{:S(2)}) collective-permute-start(bf16[192,2048]{1,0:T(8,128)(2,1)S(1)} %pad_maximum_fusion.9), channel_id=1, source_target_pairs={{0,4},{1,5},{2,6},{3,7},{4,0},{5,1},{6,2},{7,3},{8,12},{9,13},{10,... | collective-permute-start | bytes 2359304 | tf_op jit(solution)/shard_map/ppermute | solution.py:561
  429.5 21.9 %collective-permute-start.54 = (bf16[768,768]{1,0:T(8,128)(2,1)S(1)}, bf16[768,768]{1,0:T(8,128)(2,1)S(1)}, u32[]{:S(2)}, u32[]{:S(2)}) collective-permute-start(bf16[768,768]{1,0:T(8,128)(2,1)S(1)} %pad_maximum_fusion.7), channel_id=1, source_target_pairs={{0,2},{1,3},{2,0},{3,1},{4,6},{5,7},{6,4},{7,5},{8,10},{9,11},{10,... | collective-permute-start | bytes 3538952 | tf_op jit(solution)/shard_map/ppermute | solution.py:561
  451.7 17.6 %collective-permute-start.62 = (bf16[1536,768]{1,0:T(8,128)(2,1)S(1)}, bf16[1536,768]{1,0:T(8,128)(2,1)S(1)}, u32[]{:S(2)}, u32[]{:S(2)}) collective-permute-start(bf16[1536,768]{1,0:T(8,128)(2,1)S(1)} %pad_maximum_fusion.1.refs_0_), channel_id=1, source_target_pairs={{0,1},{1,0},{2,3},{3,2},{4,5},{5,4},{6,7},{7,6},{8,9},{9,8},{10,11... | collective-permute-start | bytes 7077896 | tf_op jit(solution)/shard_map/ppermute | solution.py:561
  451.8 17.5 %collective-permute-start.63 = (bf16[384,2048]{1,0:T(8,128)(2,1)S(1)}, bf16[384,2048]{1,0:T(8,128)(2,1)S(1)}, u32[]{:S(2)}, u32[]{:S(2)}) collective-permute-start(bf16[384,2048]{1,0:T(8,128)(2,1)S(1)} %pad_maximum_fusion.5.refs_0_), channel_id=1, source_target_pairs={{0,1},{1,0},{2,3},{3,2},{4,5},{5,4},{6,7},{7,6},{8,9},{9,8},{10,11... | collective-permute-start | bytes 4718600 | tf_op jit(solution)/shard_map/ppermute | solution.py:561
  452.3 17.0 %collective-permute-start.64 = (bf16[384,1792]{1,0:T(8,128)(2,1)S(1)}, bf16[384,1792]{1,0:T(8,128)(2,1)S(1)}, u32[]{:S(2)}, u32[]{:S(2)}) collective-permute-start(bf16[384,1792]{1,0:T(8,128)(2,1)S(1)} %pad_maximum_fusion.6.refs_1_), channel_id=1, source_target_pairs={{0,1},{1,0},{2,3},{3,2},{4,5},{5,4},{6,7},{7,6},{8,9},{9,8},{10,11... | collective-permute-start | bytes 4128776 | tf_op jit(solution)/shard_map/ppermute | solution.py:561
  452.4 15.7 %collective-permute-start.60 = (bf16[384,768]{1,0:T(8,128)(2,1)S(1)}, bf16[384,768]{1,0:T(8,128)(2,1)S(1)}, u32[]{:S(2)}, u32[]{:S(2)}) collective-permute-start(bf16[384,768]{1,0:T(8,128)(2,1)S(1)} %pad_maximum_fusion.12), channel_id=1, source_target_pairs={{0,2},{1,3},{2,0},{3,1},{4,6},{5,7},{6,4},{7,5},{8,10},{9,11},{10,... | collective-permute-start | bytes 1769480 | tf_op jit(solution)/shard_map/ppermute | solution.py:561
  469.4 8.5 %collective-permute-start.66 = (bf16[384,384]{1,0:T(8,128)(2,1)S(1)}, bf16[384,384]{1,0:T(8,128)(2,1)S(1)}, u32[]{:S(2)}, u32[]{:S(2)}) collective-permute-start(bf16[384,384]{1,0:T(8,128)(2,1)S(1)} %pad_maximum_fusion.18), channel_id=1, source_target_pairs={{0,2},{1,3},{2,0},{3,1},{4,6},{5,7},{6,4},{7,5},{8,10},{9,11},{10,... | collective-permute-start | bytes 884744 | tf_op jit(solution)/shard_map/ppermute | solution.py:561
  471.2 27.4 %collective-permute-start.67 = (bf16[768,768]{1,0:T(8,128)(2,1)}, bf16[768,768]{1,0:T(8,128)(2,1)S(1)}, u32[]{:S(2)}, u32[]{:S(2)}) collective-permute-start(bf16[768,768]{1,0:T(8,128)(2,1)} %pad_maximum_fusion.8.refs_0_), channel_id=1, source_target_pairs={{0,1},{1,0},{2,3},{3,2},{4,5},{5,4},{6,7},{7,6},{8,9},{9,8},{10,11... | collective-permute-start | bytes 3538952 | tf_op jit(solution)/shard_map/ppermute | solution.py:561
  478.1 20.5 %collective-permute-start.68 = (bf16[768,384]{1,0:T(8,128)(2,1)S(1)}, bf16[768,384]{1,0:T(8,128)(2,1)}, u32[]{:S(2)}, u32[]{:S(2)}) collective-permute-start(bf16[768,384]{1,0:T(8,128)(2,1)S(1)} %pad_maximum_fusion.13.refs_1_), channel_id=1, source_target_pairs={{0,1},{1,0},{2,3},{3,2},{4,5},{5,4},{6,7},{7,6},{8,9},{9,8},{10,11... | collective-permute-start | bytes 1769480 | tf_op jit(solution)/shard_map/ppermute | solution.py:561
  (72 other events, 434.5 us)

commit v5 on v4

--- a/solution.py
+++ b/solution.py
@@ -5,7 +5,7 @@
 from jax import lax
 from jax.experimental import pallas as pl
 from jax.experimental.pallas import tpu as pltpu
-from jax.sharding import PartitionSpec as P
+from jax.sharding import Mesh, PartitionSpec as P
 
 HEAD_DIM = 64
 EPS = 1e-05
@@ -489,27 +489,29 @@
     begin = 0
     for which in range(3):
         for p in range(parts):
-            for g, span in enumerate(spans):
+            first = 0
+            for span in spans:
+                lanes = slice(first + which * span, first + (which + 1) * span)
                 piece = None
                 for s in range(parts):
-                    here = refs[s * len(spans) + g][:, which * span : (which + 1) * span]
+                    here = refs[s][:, lanes]
                     piece = here if piece is None else jnp.where((part ^ p) == s, here, piece)
                 out_ref[:, begin : begin + span] = piece.astype(F32)
                 begin += span
+                first += 3 * span
 
 
 def spread(pieces, part, spans):
     parts = len(pieces)
-    count = pieces[0][0].shape[0]
+    count = pieces[0].shape[0]
     tall = next(t for t in (192, 96, 48, count) if count % t == 0)
-    flat = [p for piece in pieces for p in piece]
     columns = 3 * parts * sum(spans)
     return pl.pallas_call(
         functools.partial(spread_kernel, parts, spans),
         grid_spec=pltpu.PrefetchScalarGridSpec(
             num_scalar_prefetch=1,
             grid=(count // tall,),
-            in_specs=[pl.BlockSpec((tall, p.shape[1]), lambda i, b: (i, 0)) for p in flat],
+            in_specs=[pl.BlockSpec((tall, p.shape[1]), lambda i, b: (i, 0)) for p in pieces],
             out_specs=pl.BlockSpec((tall, columns), lambda i, b: (i, 0)),
         ),
         out_shape=jax.ShapeDtypeStruct((count, columns), F32),
@@ -520,7 +522,7 @@
             flops=count * columns, transcendentals=0, bytes_accessed=6 * count * columns
         ),
         name="spread",
-    )(part.reshape(1), *flat)
+    )(part.reshape(1), *pieces)
 
 
 def row_layout(sizes, prefixes, lens, padding, length, size):
@@ -556,8 +558,11 @@
     return info, flags
 
 
+POS = ("own", "part")
+
+
 def swap(values, axis, mask):
-    count = lax.axis_size(axis)
+    count = lax.psum(1, axis)
     return lax.ppermute(values, axis, [(i, i ^ mask) for i in range(count)])
 
 
@@ -584,22 +589,25 @@
     return jnp.concatenate([first, second], axis=0)
 
 
-class Chain:
-    def __init__(self, values, down, up):
-        self.values = values
-        self.left = [(halve, step) for step in down] + [(double, step) for step in up]
-
-    def advance(self):
-        if self.left:
-            move, step = self.left.pop(0)
-            self.values = move(self.values, step)
-
-
-def close(chains, *others):
-    tied, others = lax.optimization_barrier(([c.values for c in chains], others))
-    for chain, values in zip(chains, tied):
-        chain.values = values
-    return others
+def scatter(values, group):
+    axis, stride, count, index = group
+    pieces = values.reshape(count, values.shape[0] // count, *values.shape[1:])
+    total = take(pieces, index).astype(F32)
+    for m in range(1, count):
+        total = total + swap(take(pieces, index ^ m), axis, m * stride).astype(F32)
+    return total.astype(values.dtype)
+
+
+def gather(values, group):
+    axis, stride, count, index = group
+    slabs = [values] + [swap(values, axis, m * stride) for m in range(1, count)]
+    for b in bits(count):
+        slabs = [jnp.where((index & b) == 0, slabs[j], slabs[j ^ b]) for j in range(count)]
+    return jnp.concatenate(slabs, axis=0)
+
+
+def close(*values):
+    return lax.optimization_barrier(values)
 
 
 def per_device(
@@ -626,24 +634,24 @@
     cotangent,
 ):
     rows, size, model = tokens.shape
-    devices = lax.axis_size("pos")
+    devices = lax.psum(1, POS)
     parts = devices // rows
     blocks = devices
     heads = model // HEAD_DIM // parts
     width = heads * HEAD_DIM
-    place = lax.axis_index("pos")
+    place = lax.axis_index(POS)
     owner, part = place // parts, place % parts
 
     def bring(values):
         return jnp.stack(
             [
-                swap(take(values, owner ^ m), "pos", m * parts) if m else take(values, owner)
+                swap(take(values, owner ^ m), POS, m * parts) if m else take(values, owner)
                 for m in range(rows)
             ]
         )
 
     def send_back(values, m):
-        return swap(values[m], "pos", m * parts) if m else values[m]
+        return swap(values[m], POS, m * parts) if m else values[m]
 
     def arrange(slabs):
         out = jnp.zeros((rows, *slabs[0].shape), slabs[0].dtype)
@@ -680,7 +688,7 @@
     bias_v = lax.dynamic_slice_in_dim(value_bias, part * width, width, 0)
 
     mine = bring(tokens)
-    row = jnp.concatenate([mine] + [swap(mine, "pos", s) for s in range(1, parts)], axis=0)
+    row = jnp.concatenate([mine] + [swap(mine, POS, s) for s in range(1, parts)], axis=0)
     cotangent, row = lax.optimization_barrier((cotangent, row))
     own_cotangent = bring(cotangent)
     act_one, query_t, key, key_t, value, value_t = project(
@@ -693,7 +701,7 @@
     mixed_parts = []
     for s in range(parts):
         piece = mixed_all[s * rows : (s + 1) * rows]
-        mixed_parts.append(swap(piece, "pos", s) if s else piece)
+        mixed_parts.append(swap(piece, POS, s) if s else piece)
 
     (act_two, hidden, grad_upper, layer_out, grad_resid, grad_attn), grad_mixed, sums, up_sum = feed(
         mixed_parts, mine, own_cotangent, w_out, part, w_up, w_down,
@@ -710,71 +718,59 @@
     def flat(values):
         return values.reshape(-1, values.shape[-1])
 
-    row_place = lax.axis_index(row_axis)
-    row_steps = [(row_axis, m, (row_place // m) % 2) for m in bits(lax.axis_size(row_axis))]
-    own_steps = [("pos", m * parts, (owner // m) % 2) for m in bits(rows)]
-    part_steps = [("pos", m, (part // m) % 2) for m in bits(parts)]
-    turning, last = own_steps + row_steps[:1], row_steps[1:]
-
-    def order(turn):
-        turn %= len(turning)
-        return turning[turn:] + turning[:turn] + last
-
-    def chain(values, turn, parted=True):
-        down = order(turn)
-        up = down[::-1] + (part_steps[:0:-1] if parted else [])
-        return Chain(values, (part_steps if parted else []) + down, up)
-
+    row_count = lax.psum(1, row_axis)
+    rows_group = (row_axis, 1, row_count, lax.axis_index(row_axis))
+    chips_group = (POS, parts, rows, owner)
+    own_steps = [(POS, m * parts, (owner // m) % 2) for m in bits(rows)]
+    part_steps = [(POS, m, (part // m) % 2) for m in bits(parts)]
     wide = w_up.shape[1]
-    cut = wide * 2 // 3
     near = [m for m in range(1, rows) if m & (m - 1) == 0]
     far = [m for m in range(1, rows) if m & (m - 1)]
 
-    received = [g if s == 0 else swap(g, "pos", s) for s, g in enumerate(grad_mixed)]
+    received = [g if s == 0 else swap(g, POS, s) for s, g in enumerate(grad_mixed)]
     layer_slabs = {m: send_back(layer_out, m) for m in [0] + near}
-    down = chain(matmul(flat(hidden), flat(own_cotangent), TN).astype(BF16), 0)
-    received, layer_slabs, layer_out, grad_upper = close(
-        [down], received, layer_slabs, layer_out, grad_upper
-    )
-    down.advance()
-    layer_slabs.update({m: send_back(layer_out, m) for m in far})
     stacked = jnp.stack(mixed_parts)
     mixed = jnp.concatenate([flat(take(stacked, g ^ part)) for g in range(parts)], axis=1)
-    grad_up_flat = flat(grad_upper)
-    up_one = chain(matmul(flat(act_two), grad_up_flat[:, :cut], TN).astype(BF16), 1)
-    up_two = chain(
-        jnp.concatenate(
-            [
-                matmul(flat(act_two), grad_up_flat[:, cut:], TN).astype(BF16),
-                matmul(mixed, flat(grad_attn), TN).astype(BF16),
-            ],
-            axis=1,
-        ),
-        2,
-    )
-    chains = [down, up_one, up_two]
-    received, layer_slabs = close(chains, received, layer_slabs)
+    up = jnp.concatenate(
+        [
+            matmul(flat(act_two), flat(grad_upper), TN).astype(BF16),
+            matmul(mixed, flat(grad_attn), TN).astype(BF16),
+        ],
+        axis=1,
+    )
+    up, received, layer_slabs, layer_out, hidden = close(
+        up, received, layer_slabs, layer_out, hidden
+    )
+    for step in part_steps:
+        up = halve(up, step)
+    layer_slabs.update({m: send_back(layer_out, m) for m in far})
+    down = matmul(flat(hidden), flat(own_cotangent), TN).astype(BF16)
+    up, down, received, layer_slabs = close(up, down, received, layer_slabs)
+    up_sum_all = lax.psum(up, (row_axis, "own"))
+    for step in part_steps:
+        down = halve(down, step)
     layer_home = arrange([layer_slabs[m] for m in range(rows)])
-    up_one.advance()
-    up_two.advance()
-    for _ in part_steps[1:]:
-        for c in chains:
-            c.advance()
     grad_t = jnp.concatenate(received, axis=0).transpose(0, 2, 1)
-    grad_t, layer_home = close(chains, grad_t, layer_home)
+    pair = [down[: down.shape[0] // 2], down[down.shape[0] // 2 :]]
+    orders = [own_steps, own_steps[::-1]]
+    pair, grad_t, layer_home = close(pair, grad_t, layer_home)
 
     grads, shares = [], []
+    done = 0
     for h, count in groups:
-        for c in chains + shares:
-            c.advance()
+        pair = [halve(p, o[done]) if done < len(o) else p for p, o in zip(pair, orders)]
+        done += 1
+        shares = [scatter(q, chips_group) if i == len(shares) - 1 else q for i, q in enumerate(shares)]
         grad = attention_backward(
             phys, flags, query_t, grad_t, out_t, lse, info, key, key_t, value, count, h
         )
-        grad, grad_t = close(chains + shares, grad, grad_t)
-        grads.append(grad)
-        shares.append(chain(matmul(flat(act_one), flat(grad), TN).astype(BF16), 0, False))
+        grads, grad_t, pair, shares = close(grads + [grad], grad_t, pair, shares)
+        shares.append(matmul(flat(act_one), flat(grad), TN).astype(BF16))
         if len(grads) < len(groups):
-            (grad_t,) = close(chains + shares, grad_t)
+            grad_t, pair, shares = close(grad_t, pair, shares)
+    while done < len(own_steps):
+        pair = [halve(p, o[done]) for p, o in zip(pair, orders)]
+        done += 1
 
     def column_sums(which):
         return jnp.concatenate(
@@ -787,18 +783,18 @@
     def placed(values):
         return lax.dynamic_update_slice_in_dim(jnp.zeros((model,), F32), values, part * width, 0)
 
-    for c in chains + shares:
-        c.advance()
+    both = scatter(jnp.concatenate(pair, axis=1), rows_group)
+    shares[-1] = scatter(shares[-1], chips_group)
     grad_act = sum(matmul(flat(g), w, NT) for g, w in zip(grads, w_groups))
     grad_act_own = grad_act[:local]
     for s in range(1, parts):
         sent = grad_act[s * local : (s + 1) * local].astype(BF16)
-        grad_act_own = grad_act_own + swap(sent, "pos", s).astype(F32)
+        grad_act_own = grad_act_own + swap(sent, POS, s).astype(F32)
     sums_q, sums_v = placed(column_sums(0)), placed(column_sums(2))
-    grad_act_own, sums_q, sums_v = close(chains + shares, grad_act_own, sums_q, sums_v)
-
-    for c in chains + shares:
-        c.advance()
+    both, shares, grad_act_own, sums_q, sums_v = close(both, shares, grad_act_own, sums_q, sums_v)
+
+    both = gather(both, rows_group)
+    share = scatter(jnp.concatenate(shares, axis=1), rows_group)
     inputs = flat(mine).astype(F32)
     _, norm_one_pull = jax.vjp(layer_norm, inputs, attn_gain.astype(F32), attn_shift.astype(F32))
     grad_input_norm, grad_attn_gain, grad_attn_shift = norm_one_pull(grad_act_own)
@@ -813,43 +809,49 @@
             up_sum[0],
         ]
     )
-    tokens_grad, small = close(chains + shares, tokens_grad, small)
-
-    small_steps = part_steps + own_steps + row_steps
+    both, share, tokens_grad, small = close(both, share, tokens_grad, small)
+
+    small_steps = part_steps + own_steps + [(row_axis, m, None) for m in bits(row_count)]
+
+    def small_step(values):
+        if small_steps:
+            axis, mask, _ = small_steps.pop(0)
+            values = values + swap(values, axis, mask)
+        return values
+
+    pair = [both[:, :model], both[:, model:]]
     token_slabs = {}
     waves = [[0] + near, far]
-    while any(c.left for c in chains):
-        for c in chains + shares:
-            c.advance()
-        if small_steps:
-            axis, mask, _ = small_steps.pop(0)
-            small = small + swap(small, axis, mask)
+    for stage in reversed(range(len(own_steps))):
+        pair = [double(p, o[stage]) for p, o in zip(pair, orders)]
+        if stage == len(own_steps) - 1:
+            share = gather(share, rows_group)
+        if stage == 0:
+            share = gather(share, chips_group)
         if waves:
             token_slabs.update({m: send_back(tokens_grad, m) for m in waves.pop(0)})
-        small, token_slabs, tokens_grad = close(chains + shares, small, token_slabs, tokens_grad)
-
+        small = small_step(small)
+        pair, share, small, token_slabs, tokens_grad = close(
+            pair, share, small, token_slabs, tokens_grad
+        )
+    for wave in waves:
+        token_slabs.update({m: send_back(tokens_grad, m) for m in wave})
+
+    down = jnp.concatenate(pair, axis=0)
+    up = up_sum_all
+    for step in part_steps[:0:-1]:
+        down, up = double(down, step), double(up, step)
     axis, mask, bit = part_steps[0]
-    others = [swap(c.values, axis, mask) for c in chains]
-    for c in shares:
-        c.advance()
-    for axis, mask, _ in small_steps:
-        small = small + swap(small, axis, mask)
-    others, small = close(chains + shares, others, small)
-    (sum_w_down,) = join([down.values], others[:1], bit, ((0, 0, 0, 0, model),), (model,))
+    other_down, other_up = swap(down, axis, mask), swap(up, axis, mask)
+    pieces = [share] + [swap(share, POS, s) for s in range(1, parts)]
+    (sum_w_down,) = join([down], [other_down], bit, ((0, 0, 0, 0, model),), (model,))
     sum_w_up, sum_w_out = join(
-        [up_one.values, up_two.values],
-        others[1:],
-        bit,
-        ((0, 0, 0, 0, cut), (1, 0, 0, cut, wide - cut), (1, wide - cut, 1, 0, model)),
-        (wide, model),
+        [up], [other_up], bit, ((0, 0, 0, 0, wide), (0, wide, 1, 0, model)), (wide, model)
     )
     tokens_home = arrange([token_slabs[m] for m in range(rows)])
-    while any(c.left for c in shares):
-        for c in shares:
-            c.advance()
-    summed = [c.values for c in shares]
-    pieces = [summed] + [[swap(g, "pos", s) for g in summed] for s in range(1, parts)]
     sum_w_qkv = spread(pieces, part, spans)
+    while small_steps:
+        small = small_step(small)
 
     vectors = small[: 8 * model].reshape(8, model)
     return (
@@ -872,21 +874,27 @@
 
 
 def solution(mesh):
-    in_specs = (
-        P("rows", "pos", None),
-        P("rows", "pos"),
-        P("rows", None),
-        P("rows", None),
-        P("rows", None, None),
-        P("rows"),
-        *([P()] * 13),
-        P("rows", "pos", None),
-    )
-    out_specs = (P("rows", "pos", None), P("rows", "pos", None), *([P()] * 13))
-    return jax.shard_map(
-        functools.partial(per_device, "rows"),
-        mesh=mesh,
-        in_specs=in_specs,
-        out_specs=out_specs,
-        check_vma=False,
-    )
+    def run(tokens, *others):
+        count = mesh.shape["rows"]
+        rows = tokens.shape[0] // count
+        split = Mesh(mesh.devices.reshape(count, rows, -1), ("rows", *POS))
+        in_specs = (
+            P("rows", POS, None),
+            P("rows", POS),
+            P("rows", None),
+            P("rows", None),
+            P("rows", None, None),
+            P("rows"),
+            *([P()] * 13),
+            P("rows", POS, None),
+        )
+        out_specs = (P("rows", POS, None), P("rows", POS, None), *([P()] * 13))
+        return jax.shard_map(
+            functools.partial(per_device, "rows"),
+            mesh=split,
+            in_specs=in_specs,
+            out_specs=out_specs,
+            check_vma=False,
+        )(tokens, *others)
+
+    return run

time: 511 us -> 518 us (1.014)
  starting transfers between devices: 71.4 us -> 58.3 us
  between operations: 8.48 us -> 21.3 us
  waiting for transfers between devices: 115 us -> 109 us
  matrix products: 29.8 us -> 35.2 us
    ppermute x69 -> x55, starting transfers between devices: 71.4 us -> 58.3 us  [swap(): return lax.ppermute(values, axis, [(i, i ^ mask) for i in range(count)])]
    ppermute x69 -> x55, waiting for transfers between devices: 115 us -> 109 us  [swap(): return lax.ppermute(values, axis, [(i, i ^ mask) for i in range(count)])]
    unnamed x144 -> x123, local copies, waits for them, and re-layouts: 14.4 us -> 8.65 us
    dot_general x8 -> x7, matrix products: 29.8 us -> 35.2 us  [matmul(): return lax.dot_general(left, right, dims, preferred_element_type=F32)]
    convert_element_type x23 -> x6, other arithmetic: 12.3 us -> 8.76 us  [halve(): (take(two, bit).astype(F32) + arrived.astype(F32)).astype(values.dtype)]
  transfers between devices with their start and end apart: 69 -> 56, of which waited for: 33 -> 18; matrix products, arithmetic and copies ran while one was open for 17% -> 22% of each run, Pallas kernels for 23% -> 27%
where the time goes in v5:
time: 518 us; the launch traced here: 512 us
  Pallas kernels  187 us (36%)
  waiting for transfers between devices  109 us (21%)
  starting transfers between devices  58.3 us (11%)
  local copies, waits for them, and re-layouts  57.4 us (11%)
  other arithmetic  43.9 us (8%)
  matrix products  35.2 us (7%)
  between operations  21.3 us (4%)
    ppermute x55, waiting for transfers between devices, swap(): return lax.ppermute(values, axis, [(i, i ^ mask) for i in range(count)])  109 us
    pallas_call x2, Pallas kernels, attention_backward(): pl.pallas_call(functools.partial(backward_kernel, heads, first, blocks),...  64.9 us
    ppermute x55, starting transfers between devices, swap(): return lax.ppermute(values, axis, [(i, i ^ mask) for i in range(count)])  58.3 us
    pallas_call x1, Pallas kernels, attention_forward(): pl.pallas_call(functools.partial(forward_kernel, heads, blocks), grid_spe...  48.3 us
    pallas_call x1, Pallas kernels, feed(): pl.pallas_call(body, grid_spec=pltpu.PrefetchScalarGridSpec(num_scalar_pr...  36.4 us
    dot_general x7, matrix products, matmul(): return lax.dot_general(left, right, dims, preferred_element_type=F32)  35.2 us
    pallas_call x2, Pallas kernels, join(): pl.pallas_call(functools.partial(join_kernel, len(mine), moves), grid_spe...  19.3 us
    pallas_call x1, Pallas kernels, project(): pl.pallas_call(functools.partial(project_kernel, width), grid=(blocks,),...  12.3 us
  transfers between devices with their start and end apart: 56, of which 18 were waited for; matrix products, arithmetic and copies ran while one was open for 22% of the time, Pallas kernels for 27%

profile of v5, /device:TPU:0, one launch (start us, length us, event | category | flops | bytes accessed | tf_op | source)
XLA Modules:
  0.0 511.7 jit_solution(4811215522620780659)
XLA Ops:
  7.3 2.2 dynamic-slice_bitcast_fusion.7
  9.5 3.0 collective-permute-start
  12.5 1.5 collective-permute-start.1
  22.5 1.9 select_select_fusion
  29.6 1.9 collective-permute-done.1
  41.5 2.0 fusion.42
  46.1 1.6 constant_dynamic-slice_fusion.9
  51.8 1.6 collective-permute-start.6
  55.4 12.3 %project.1 = (bf16[8,256,768]{2,1,0:T(8,128)(2,1)}, bf16[8,384,256]{2,1,0:T(8,128)(2,1)}, bf16[8,256,384]{2,1,0:T(8,128)(2,1)}, bf16[8,384,256]{2,1,0:T(8,128)(2...) custom-call(bf16[8,256,768]{2,1,0:T(8,128)(2,1)} %copy-done.38, f32[1,768]{1,0:T(1,128)} %reshape.519.gain_ref, ...), custom_call_target="tpu_custom_call" | custom-call | flops 3623878656 | bytes 14155776 | tf_op jit(solution)/shard_map/project/pallas_call | solution.py:274
  67.7 48.3 %attention_forward.1 = (bf16[8,256,384]{2,1,0:T(8,128)(2,1)}, f32[8,384,256]{2,1,0:T(8,128)}, f32[8,8,256]{2,1,0:T(8,128)}) custom-call(s32[8]{0:T(128)} %fusion.61.phys_ref, s32[64]{0:T(128)} %reshape.555.flag_ref, bf16[8,384,256]{2,1,0:T(8,128)(2,1)} %get-tuple-element.100.query_t_ref, bf16[8,256,384]{2,1,0:T(8,128)(2,1)} %get-tuple-element.101.key_ref, ...), custom_call_target="tpu_custom_call" | custom-call | flops 7247757312 | bytes 12582912 | tf_op jit(solution)/shard_map/attention_forward/pallas_call | solution.py:125
  122.8 36.4 %feed.1 = (bf16[4,256,768]{2,1,0:T(8,128)(2,1)}, bf16[4,256,3072]{2,1,0:T(8,128)(2,1)}, bf16[4,256,3072]{2,1,0:T(8,128)(2,1)}, bf16[4,256,768]{2,1,0:T(8,128)(2,...) custom-call(s32[1]{0:T(128)} %bitcast.p_ref.part_ref, ...), custom_call_target="tpu_custom_call" | custom-call | flops 21743271936 | bytes 25165824 | tf_op jit(solution)/shard_map/feed/pallas_call | solution.py:391
  159.3 2.4 copy.53
  163.3 8.6 %bitcast_convert_fusion.1 = bf16[768,3072]{1,0:T(8,128)(2,1)S(1)} fusion(bf16[4,256,768]{2,1,0:T(8,128)(2,1)S(1)} %copy-done.53, bf16[4,256,3072]{2,1,0:T(8,128)(2,1)} %get-tuple-element.108), kind=kOutput, calls=%fused_computation.1 | convolution fusion | flops 4834197504 | bytes 12582912 | tf_op jit(solution)/shard_map/dot_general | solution.py:32
  173.3 2.5 fusion.7
  175.8 1.7 pad_maximum_fusion
  177.5 2.0 dynamic-slice_bitcast_fusion
  182.9 2.8 collective-permute-start.12
  185.6 9.1 %bitcast_convert_fusion = bf16[3072,768]{1,0:T(8,128)(2,1)} fusion(bf16[4,256,3072]{2,1,0:T(8,128)(2,1)} %get-tuple-element.115, bf16[4,256,768]{2,1,0:T(8,128)(2,1)} %pad_maximum_fusion.4.refs_3_), kind=kOutput, calls=%fused_computation | convolution fusion | flops 4834197504 | bytes 12582912 | tf_op jit(solution)/shard_map/dot_general | solution.py:32
  194.8 2.4 fusion
  197.2 3.2 dynamic-slice_bitcast_fusion.1
  200.6 2.1 constant_dynamic-slice_fusion.2
  202.7 2.3 constant_dynamic-slice_fusion.5
  208.1 2.5 maximum_bitcast_fusion.grad_t_ref
  215.0 3.0 fusion.1
  220.7 1.5 collective-permute-start.15
  222.2 40.3 %attention_backward.2 = bf16[8,256,768]{2,1,0:T(8,128)(2,1)} custom-call(s32[8]{0:T(128)} %fusion.61.phys_ref, s32[64]{0:T(128)} %reshape.555.flag_ref, bf16[8,384,256]{2,1,0:T(8,128)(2,1)} %get-tuple-element.100.query_t_ref, bf16[8,384,256]{2,1,0:T(8,128)(2,1)} %maximum_bitcast_fusion.grad_t_ref, f32[8,384,256]{2,1,0:T(8,128)} %get-tuple-element.131.out_t_ref, ...), custom_call_target="tpu_custom_call" | custom-call | flops 12079595520 | bytes 10485760 | tf_op jit(solution)/shard_map/attention_backward/pallas_call | solution.py:234
  262.5 6.6 %bitcast_convert_fusion.2 = bf16[768,768]{1,0:T(8,128)(2,1)} fusion(bf16[8,256,768]{2,1,0:T(8,128)(2,1)} %get-tuple-element.141, bf16[8,256,768]{2,1,0:T(8,128)(2,1)} %attention_backward.2), kind=kOutput, calls=%fused_computation.19 | convolution fusion | flops 2416508928 | bytes 7471104 | tf_op jit(solution)/shard_map/dot_general | solution.py:32
  269.1 2.0 fusion.18
  272.4 24.6 %attention_backward.3 = bf16[8,256,384]{2,1,0:T(8,128)(2,1)} custom-call(s32[8]{0:T(128)} %fusion.61.phys_ref, s32[64]{0:T(128)} %reshape.555.flag_ref, bf16[8,384,256]{2,1,0:T(8,128)(2,1)} %get-tuple-element.100.query_t_ref, bf16[8,384,256]{2,1,0:T(8,128)(2,1)} %maximum_bitcast_fusion.grad_t_ref, f32[8,384,256]{2,1,0:T(8,128)} %get-tuple-element.131.out_t_ref, ...), custom_call_target="tpu_custom_call" | custom-call | flops 6039797760 | bytes 5242880 | tf_op jit(solution)/shard_map/attention_backward/pallas_call | solution.py:234
  298.6 3.4 collective-permute-start.20
  302.6 3.9 fusion.10
  306.6 3.0 collective-permute-done.16
  310.4 8.3 %collective-permute-done.20 = bf16[192,768]{1,0:T(8,128)(2,1)S(1)} collective-permute-done((bf16[192,768]{1,0:T(8,128)(2,1)S(1)}, bf16[192,768]{1,0:T(8,128)(2,1)S(1)}, u32[]{:S(2)}, u32[]{:S(2)}) %collective-permute-start.20) | collective-permute-done | bytes 294944 | tf_op jit(solution)/shard_map/ppermute | solution.py:566
  318.9 6.1 %collective-permute-done.19 = bf16[192,768]{1,0:T(8,128)(2,1)S(1)} collective-permute-done((bf16[192,768]{1,0:T(8,128)(2,1)S(1)}, bf16[192,768]{1,0:T(8,128)(2,1)S(1)}, u32[]{:S(2)}, u32[]{:S(2)}) %collective-permute-start.19) | collective-permute-done | bytes 294944 | tf_op jit(solution)/shard_map/ppermute | solution.py:566
  326.2 2.7 fusion.11
  328.9 1.8 convolution_add_fusion
  331.2 1.6 collective-permute-start.23
  333.8 1.8 collective-permute-start.21
  336.5 4.6 collective-permute-done.23
  341.1 20.0 %collective-permute-done.22 = bf16[48,1536]{1,0:T(8,128)(2,1)S(1)} collective-permute-done((bf16[48,1536]{1,0:T(8,128)(2,1)S(1)}, bf16[48,1536]{1,0:T(8,128)(2,1)S(1)}, u32[]{:S(2)}, u32[]{:S(2)}) %collective-permute-start.22) | collective-permute-done | bytes 147488 | tf_op jit(solution)/shard_map/ppermute | solution.py:566
  361.5 1.5 collective-permute-start.28
  363.0 4.0 collective-permute-start.29
  367.1 1.5 collective-permute-start.32
  368.7 2.8 collective-permute-start.31
  372.5 1.9 multiply_reduce_fusion
  376.0 4.4 collective-permute-done.33
  381.0 9.4 %collective-permute-done.32 = bf16[48,1152]{1,0:T(8,128)(2,1)S(1)} collective-permute-done((bf16[48,1152]{1,0:T(8,128)(2,1)S(1)}, bf16[48,1152]{1,0:T(8,128)(2,1)S(1)}, u32[]{:S(2)}, u32[]{:S(2)}) %collective-permute-start.32) | collective-permute-done | bytes 110624 | tf_op jit(solution)/shard_map/ppermute | solution.py:566
  390.7 3.6 collective-permute-start.36
  396.9 1.5 collective-permute-start.35
  402.0 2.4 collective-permute-done.37
  404.4 1.6 collective-permute-start.41
  406.1 3.5 collective-permute-done.34
  412.4 4.7 collective-permute-done.41
  421.4 17.4 %collective-permute-done.47 = f32[9216]{0:T(1024)S(1)} collective-permute-done((f32[9216]{0:T(1024)S(1)}, f32[9216]{0:T(1024)S(1)}, u32[]{:S(2)}, u32[]{:S(2)}) %collective-permute-start.47) | collective-permute-done | bytes 36896 | tf_op jit(solution)/shard_map/ppermute | solution.py:566
  440.0 1.7 collective-permute-start.43
  444.4 10.9 %collective-permute-done.42 = bf16[384,768]{1,0:T(8,128)(2,1)S(1)} collective-permute-done((bf16[384,768]{1,0:T(8,128)(2,1)}, bf16[384,768]{1,0:T(8,128)(2,1)S(1)}, u32[]{:S(2)}, u32[]{:S(2)}) %collective-permute-start.42) | collective-permute-done | bytes 589856 | tf_op jit(solution)/shard_map/ppermute | solution.py:566
  456.5 5.7 %collective-permute-done.43 = bf16[384,768]{1,0:T(8,128)(2,1)S(1)} collective-permute-done((bf16[384,768]{1,0:T(8,128)(2,1)}, bf16[384,768]{1,0:T(8,128)(2,1)S(1)}, u32[]{:S(2)}, u32[]{:S(2)}) %collective-permute-start.43) | collective-permute-done | bytes 589856 | tf_op jit(solution)/shard_map/ppermute | solution.py:566
  464.2 8.0 %join.2 = (f32[768,3072]{1,0:T(8,128)}, f32[768,768]{1,0:T(8,128)}) custom-call(s32[1]{0:T(128)} %bitcast.98.bit_ref, bf16[384,3840]{1,0:T(8,128)(2,1)} %all-reduce.2.cloned.1.call-done.refs_0_, bf16[384,3840]{1,0:T(8,128)(2,1)} %collective-permute-done.53.refs_1_), custom_call_target="tpu_custom_call" | custom-call | flops 2949120 | bytes 17694720 | tf_op jit(solution)/shard_map/join/pallas_call | solution.py:464
  472.2 1.7 collective-permute-start.49
  475.2 1.8 bitcast_dynamic-update-slice_fusion.3
  479.6 2.2 collective-permute-done.50
  483.9 2.8 collective-permute-done.51
  487.9 5.4 %spread.1 = f32[768,2304]{1,0:T(8,128)} custom-call(s32[1]{0:T(128)} %bitcast.p_ref.part_ref, bf16[768,1152]{1,0:T(8,128)(2,1)} %copy-done.6, bf16[768,1152]{1,0:T(8,128)(2,1)} %collective-permute-done.52.refs_1_), custom_call_target="tpu_custom_call" | custom-call | flops 1769472 | bytes 10616832 | tf_op jit(solution)/shard_map/spread/pallas_call | solution.py:509
  493.3 11.4 %join.3 = f32[3072,768]{1,0:T(8,128)} custom-call(s32[1]{0:T(128)} %bitcast.98.bit_ref, bf16[1536,768]{1,0:T(8,128)(2,1)} %copy-done.7, bf16[1536,768]{1,0:T(8,128)(2,1)} %collective-permute-done.54.refs_1_), custom_call_target="tpu_custom_call" | custom-call | flops 2359296 | bytes 14155776 | tf_op jit(solution)/shard_map/join/pallas_call | solution.py:464
  (326 shorter events, 89.1 us)
Async XLA Ops:
  7.2 413.4 %all-reduce.2.cloned.1.call-start = ((), (), s32[]{:S(2)}) async-start(), calls=%async_computation | async-start | bytes 5898240 | tf_op jit(solution)/shard_map/psum | solution.py:749
  9.5 20.0 %collective-permute-start = (bf16[256,768]{1,0:T(8,128)(2,1)S(1)}, bf16[256,768]{1,0:T(8,128)(2,1)S(1)}, u32[]{:S(2)}, u32[]{:S(2)}) collective-permute-start(bf16[256,768]{1,0:T(8,128)(2,1)S(1)} %get-tuple-element.230), channel_id=1, source_target_pairs={{0,2},{1,3},{2,0},{3,1},{4,6},{5,7},{6,4},{7,5},{8,10},{9,11},{10,... | collective-permute-start | bytes 1179656 | tf_op jit(solution)/shard_map/ppermute | solution.py:566
  12.5 19.0 %collective-permute-start.1 = (bf16[256,768]{1,0:T(8,128)(2,1)S(1)}, bf16[256,768]{1,0:T(8,128)(2,1)S(1)}, u32[]{:S(2)}, u32[]{:S(2)}) collective-permute-start(bf16[256,768]{1,0:T(8,128)(2,1)S(1)} %get-tuple-element.233), channel_id=1, source_target_pairs={{0,4},{1,5},{2,6},{3,7},{4,0},{5,1},{6,2},{7,3},{8,12},{9,13},{10,... | collective-permute-start | bytes 1179656 | tf_op jit(solution)/shard_map/ppermute | solution.py:566
  14.0 17.5 %collective-permute-start.2 = (bf16[256,768]{1,0:T(8,128)(2,1)S(1)}, bf16[256,768]{1,0:T(8,128)(2,1)S(1)}, u32[]{:S(2)}, u32[]{:S(2)}) collective-permute-start(bf16[256,768]{1,0:T(8,128)(2,1)S(1)} %get-tuple-element.229), channel_id=1, source_target_pairs={{0,6},{1,7},{2,4},{3,5},{4,2},{5,3},{6,0},{7,1},{8,14},{9,15},{10,... | collective-permute-start | bytes 1179656 | tf_op jit(solution)/shard_map/ppermute | solution.py:566
  32.4 16.7 %copy-start.2 = (bf16[4,256,768]{2,1,0:T(8,128)(2,1)}, bf16[4,256,768]{2,1,0:T(8,128)(2,1)S(1)}, u32[]{:S(2)}) copy-start(bf16[4,256,768]{2,1,0:T(8,128)(2,1)S(1)} %get-tuple-element.192.refs_2_) | copy-start | bytes 4718596
  32.4 18.0 %collective-permute-start.3 = (bf16[4,256,768]{2,1,0:T(8,128)(2,1)S(1)}, bf16[4,256,768]{2,1,0:T(8,128)(2,1)S(1)}, u32[]{:S(2)}, u32[]{:S(2)}) collective-permute-start(bf16[4,256,768]{2,1,0:T(8,128)(2,1)S(1)} %get-tuple-element.192.refs_2_), channel_id=1, source_target_pairs={{0,1},{1,0},{2,3},{3,2},{4,5},{5,4},{6,7},{7,6},{8,9},{9,8},{10,11... | collective-permute-start | bytes 4718600 | tf_op jit(solution)/shard_map/ppermute | solution.py:566
  51.8 64.1 %collective-permute-start.6 = (bf16[256,768]{1,0:T(8,128)(2,1)S(1)}, bf16[256,768]{1,0:T(8,128)(2,1)S(1)}, u32[]{:S(2)}, u32[]{:S(2)}) collective-permute-start(bf16[256,768]{1,0:T(8,128)(2,1)S(1)} %get-tuple-element.226), channel_id=1, source_target_pairs={{0,6},{1,7},{2,4},{3,5},{4,2},{5,3},{6,0},{7,1},{8,14},{9,15},{10,... | collective-permute-start | bytes 1179656 | tf_op jit(solution)/shard_map/ppermute | solution.py:566
  53.4 62.6 %collective-permute-start.5 = (bf16[256,768]{1,0:T(8,128)(2,1)S(1)}, bf16[256,768]{1,0:T(8,128)(2,1)S(1)}, u32[]{:S(2)}, u32[]{:S(2)}) collective-permute-start(bf16[256,768]{1,0:T(8,128)(2,1)S(1)} %get-tuple-element.227), channel_id=1, source_target_pairs={{0,4},{1,5},{2,6},{3,7},{4,0},{5,1},{6,2},{7,3},{8,12},{9,13},{10,... | collective-permute-start | bytes 1179656 | tf_op jit(solution)/shard_map/ppermute | solution.py:566
  54.6 61.4 %collective-permute-start.4 = (bf16[256,768]{1,0:T(8,128)(2,1)S(1)}, bf16[256,768]{1,0:T(8,128)(2,1)S(1)}, u32[]{:S(2)}, u32[]{:S(2)}) collective-permute-start(bf16[256,768]{1,0:T(8,128)(2,1)S(1)} %get-tuple-element.228), channel_id=1, source_target_pairs={{0,2},{1,3},{2,0},{3,1},{4,6},{5,7},{6,4},{7,5},{8,10},{9,11},{10,... | collective-permute-start | bytes 1179656 | tf_op jit(solution)/shard_map/ppermute | solution.py:566
  119.0 2.9 collective-permute-start.7
  161.7 15.8 %collective-permute-start.8 = (bf16[4,256,384]{1,2,0:T(8,128)(2,1)}, bf16[4,256,384]{1,2,0:T(8,128)(2,1)}, u32[]{:S(2)}, u32[]{:S(2)}) collective-permute-start(bf16[4,256,384]{1,2,0:T(8,128)(2,1)} %copy.53), channel_id=1, source_target_pairs={{0,1},{1,0},{2,3},{3,2},{4,5},{5,4},{6,7},{7,6},{8,9},{9,8},{10,11... | collective-permute-start | bytes 2359304 | tf_op jit(solution)/shard_map/ppermute | solution.py:566
  163.2 14.2 %collective-permute-start.9 = (bf16[256,768]{1,0:T(8,128)(2,1)}, bf16[256,768]{1,0:T(8,128)(2,1)}, u32[]{:S(2)}, u32[]{:S(2)}) collective-permute-start(bf16[256,768]{1,0:T(8,128)(2,1)} %get-tuple-element.218), channel_id=1, source_target_pairs={{0,2},{1,3},{2,0},{3,1},{4,6},{5,7},{6,4},{7,5},{8,10},{9,11},{10,... | collective-permute-start | bytes 1179656 | tf_op jit(solution)/shard_map/ppermute | solution.py:566
  163.2 14.2 %collective-permute-start.10 = (bf16[256,768]{1,0:T(8,128)(2,1)}, bf16[256,768]{1,0:T(8,128)(2,1)}, u32[]{:S(2)}, u32[]{:S(2)}) collective-permute-start(bf16[256,768]{1,0:T(8,128)(2,1)} %get-tuple-element.217), channel_id=1, source_target_pairs={{0,4},{1,5},{2,6},{3,7},{4,0},{5,1},{6,2},{7,3},{8,12},{9,13},{10,... | collective-permute-start | bytes 1179656 | tf_op jit(solution)/shard_map/ppermute | solution.py:566
  180.9 13.8 %collective-permute-start.11 = (bf16[384,3840]{1,0:T(8,128)(2,1)}, bf16[384,3840]{1,0:T(8,128)(2,1)S(1)}, u32[]{:S(2)}, u32[]{:S(2)}) collective-permute-start(bf16[384,3840]{1,0:T(8,128)(2,1)} %dynamic-slice_bitcast_fusion), channel_id=1, source_target_pairs={{0,1},{1,0},{2,3},{3,2},{4,5},{5,4},{6,7},{7,6},{8,9},{9,8},{10,11... | collective-permute-start | bytes 8847368 | tf_op jit(solution)/shard_map/ppermute | solution.py:566
  181.7 13.1 %slice-start = ((s8[5898240]{0:T(1024)(128)(4,1)}), s8[4194304]{0:T(1024)(128)(4,1)S(1)}, s32[]{:S(2)}) async-start(s8[5898240]{0:T(1024)(128)(4,1)} %bitcast.208), calls=%async_computation.1 | async-start | bytes 8388608
  182.9 14.3 %collective-permute-start.12 = (bf16[256,768]{1,0:T(8,128)(2,1)S(1)}, bf16[256,768]{1,0:T(8,128)(2,1)}, u32[]{:S(2)}, u32[]{:S(2)}) collective-permute-start(bf16[256,768]{1,0:T(8,128)(2,1)S(1)} %slice_bitcast_fusion.4), channel_id=1, source_target_pairs={{0,6},{1,7},{2,4},{3,5},{4,2},{5,3},{6,0},{7,1},{8,14},{9,15},{10,... | collective-permute-start | bytes 1179656 | tf_op jit(solution)/shard_map/ppermute | solution.py:566
  200.4 14.6 %collective-permute-start.13 = (bf16[1536,768]{1,0:T(8,128)(2,1)}, bf16[1536,768]{1,0:T(8,128)(2,1)}, u32[]{:S(2)}, u32[]{:S(2)}) collective-permute-start(bf16[1536,768]{1,0:T(8,128)(2,1)} %dynamic-slice_bitcast_fusion.1), channel_id=1, source_target_pairs={{0,1},{1,0},{2,3},{3,2},{4,5},{5,4},{6,7},{7,6},{8,9},{9,8},{10,11... | collective-permute-start | bytes 7077896 | tf_op jit(solution)/shard_map/ppermute | solution.py:566
  220.0 49.1 %collective-permute-start.14 = (bf16[384,768]{1,0:T(8,128)(2,1)}, bf16[384,768]{1,0:T(8,128)(2,1)}, u32[]{:S(2)}, u32[]{:S(2)}) collective-permute-start(bf16[384,768]{1,0:T(8,128)(2,1)} %dynamic-slice_bitcast_fusion.3), channel_id=1, source_target_pairs={{0,2},{1,3},{2,0},{3,1},{4,6},{5,7},{6,4},{7,5},{8,10},{9,11},{10,... | collective-permute-start | bytes 1769480 | tf_op jit(solution)/shard_map/ppermute | solution.py:566
  220.7 50.4 %collective-permute-start.15 = (bf16[384,768]{1,0:T(8,128)(2,1)S(1)}, bf16[384,768]{1,0:T(8,128)(2,1)}, u32[]{:S(2)}, u32[]{:S(2)}) collective-permute-start(bf16[384,768]{1,0:T(8,128)(2,1)S(1)} %dynamic-slice_bitcast_fusion.2), channel_id=1, source_target_pairs={{0,4},{1,5},{2,6},{3,7},{4,0},{5,1},{6,2},{7,3},{8,12},{9,13},{10,... | collective-permute-start | bytes 1769480 | tf_op jit(solution)/shard_map/ppermute | solution.py:566
  272.4 24.6 %copy-start.11 = (bf16[384,768]{1,0:T(8,128)(2,1)S(1)}, bf16[384,768]{1,0:T(8,128)(2,1)}, u32[]{:S(2)}) copy-start(bf16[384,768]{1,0:T(8,128)(2,1)} %fusion.18) | copy-start | bytes 1769476
  297.1 12.6 %collective-permute-start.16 = (bf16[192,768]{1,0:T(8,128)(2,1)S(1)}, bf16[192,768]{1,0:T(8,128)(2,1)S(1)}, u32[]{:S(2)}, u32[]{:S(2)}) collective-permute-start(bf16[192,768]{1,0:T(8,128)(2,1)S(1)} %dynamic-slice_bitcast_fusion.14), channel_id=1, source_target_pairs={{0,4},{1,5},{2,6},{3,7},{4,0},{5,1},{6,2},{7,3},{8,12},{9,13},{10,... | collective-permute-start | bytes 884744 | tf_op jit(solution)/shard_map/ppermute | solution.py:566
  297.2 12.5 %collective-permute-start.17 = (bf16[192,768]{1,0:T(8,128)(2,1)S(1)}, bf16[192,768]{1,0:T(8,128)(2,1)S(1)}, u32[]{:S(2)}, u32[]{:S(2)}) collective-permute-start(bf16[192,768]{1,0:T(8,128)(2,1)S(1)} %dynamic-slice_bitcast_fusion.13), channel_id=1, source_target_pairs={{0,2},{1,3},{2,0},{3,1},{4,6},{5,7},{6,4},{7,5},{8,10},{9,11},{10,... | collective-permute-start | bytes 884744 | tf_op jit(solution)/shard_map/ppermute | solution.py:566
  298.6 20.1 %collective-permute-start.20 = (bf16[192,768]{1,0:T(8,128)(2,1)S(1)}, bf16[192,768]{1,0:T(8,128)(2,1)S(1)}, u32[]{:S(2)}, u32[]{:S(2)}) collective-permute-start(bf16[192,768]{1,0:T(8,128)(2,1)S(1)} %get-tuple-element.239), channel_id=1, source_target_pairs={{0,6},{1,7},{2,4},{3,5},{4,2},{5,3},{6,0},{7,1},{8,14},{9,15},{10,... | collective-permute-start | bytes 884744 | tf_op jit(solution)/shard_map/ppermute | solution.py:566
  302.0 23.1 %collective-permute-start.19 = (bf16[192,768]{1,0:T(8,128)(2,1)S(1)}, bf16[192,768]{1,0:T(8,128)(2,1)S(1)}, u32[]{:S(2)}, u32[]{:S(2)}) collective-permute-start(bf16[192,768]{1,0:T(8,128)(2,1)S(1)} %get-tuple-element.240), channel_id=1, source_target_pairs={{0,4},{1,5},{2,6},{3,7},{4,0},{5,1},{6,2},{7,3},{8,12},{9,13},{10,... | collective-permute-start | bytes 884744 | tf_op jit(solution)/shard_map/ppermute | solution.py:566
  302.0 23.0 %collective-permute-start.18 = (bf16[192,768]{1,0:T(8,128)(2,1)S(1)}, bf16[192,768]{1,0:T(8,128)(2,1)S(1)}, u32[]{:S(2)}, u32[]{:S(2)}) collective-permute-start(bf16[192,768]{1,0:T(8,128)(2,1)S(1)} %get-tuple-element.238), channel_id=1, source_target_pairs={{0,2},{1,3},{2,0},{3,1},{4,6},{5,7},{6,4},{7,5},{8,10},{9,11},{10,... | collective-permute-start | bytes 884744 | tf_op jit(solution)/shard_map/ppermute | solution.py:566
  302.6 23.5 %copy-start.29 = (bf16[768,256]{1,0:T(8,128)(2,1)S(1)}, bf16[768,256]{1,0:T(8,128)(2,1)}, u32[]{:S(2)}) copy-start(bf16[768,256]{1,0:T(8,128)(2,1)} %get-tuple-element.204) | copy-start | bytes 1179652
  306.5 19.6 %copy-start.21 = (bf16[8,256,768]{2,1,0:T(8,128)(2,1)S(1)}, bf16[8,256,768]{2,1,0:T(8,128)(2,1)}, u32[]{:S(2)}) copy-start(bf16[8,256,768]{2,1,0:T(8,128)(2,1)} %attention_backward.2) | copy-start | bytes 9437188
  306.5 19.6 %copy-start.27 = (bf16[768,256]{1,0:T(8,128)(2,1)S(1)}, bf16[768,256]{1,0:T(8,128)(2,1)}, u32[]{:S(2)}) copy-start(bf16[768,256]{1,0:T(8,128)(2,1)} %get-tuple-element.202) | copy-start | bytes 1179652
  306.6 19.6 %copy-start.28 = (bf16[768,256]{1,0:T(8,128)(2,1)S(1)}, bf16[768,256]{1,0:T(8,128)(2,1)}, u32[]{:S(2)}) copy-start(bf16[768,256]{1,0:T(8,128)(2,1)} %get-tuple-element.203) | copy-start | bytes 1179652
  309.6 21.4 %collective-permute-start.26 = (bf16[192,384]{1,0:T(8,128)(2,1)S(1)}, bf16[192,384]{1,0:T(8,128)(2,1)S(1)}, u32[]{:S(2)}, u32[]{:S(2)}) collective-permute-start(bf16[192,384]{1,0:T(8,128)(2,1)S(1)} %get-tuple-element.254), channel_id=1, source_target_pairs={{0,6},{1,7},{2,4},{3,5},{4,2},{5,3},{6,0},{7,1},{8,14},{9,15},{10,... | collective-permute-start | bytes 442376 | tf_op jit(solution)/shard_map/ppermute | solution.py:566
  309.7 21.3 %collective-permute-start.25 = (bf16[192,384]{1,0:T(8,128)(2,1)S(1)}, bf16[192,384]{1,0:T(8,128)(2,1)S(1)}, u32[]{:S(2)}, u32[]{:S(2)}) collective-permute-start(bf16[192,384]{1,0:T(8,128)(2,1)S(1)} %get-tuple-element.255), channel_id=1, source_target_pairs={{0,4},{1,5},{2,6},{3,7},{4,0},{5,1},{6,2},{7,3},{8,12},{9,13},{10,... | collective-permute-start | bytes 442376 | tf_op jit(solution)/shard_map/ppermute | solution.py:566
  318.7 12.3 %collective-permute-start.24 = (bf16[192,384]{1,0:T(8,128)(2,1)S(1)}, bf16[192,384]{1,0:T(8,128)(2,1)S(1)}, u32[]{:S(2)}, u32[]{:S(2)}) collective-permute-start(bf16[192,384]{1,0:T(8,128)(2,1)S(1)} %get-tuple-element.253), channel_id=1, source_target_pairs={{0,2},{1,3},{2,0},{3,1},{4,6},{5,7},{6,4},{7,5},{8,10},{9,11},{10,... | collective-permute-start | bytes 442376 | tf_op jit(solution)/shard_map/ppermute | solution.py:566
  330.9 30.3 %collective-permute-start.27 = (bf16[1024,768]{1,0:T(8,128)(2,1)S(1)}, bf16[1024,768]{1,0:T(8,128)(2,1)S(1)}, u32[]{:S(2)}, u32[]{:S(2)}) collective-permute-start(bf16[1024,768]{1,0:T(8,128)(2,1)S(1)} %slice.232), channel_id=1, source_target_pairs={{0,1},{1,0},{2,3},{3,2},{4,5},{5,4},{6,7},{7,6},{8,9},{9,8},{10,11... | collective-permute-start | bytes 4718600 | tf_op jit(solution)/shard_map/ppermute | solution.py:566
  331.2 9.9 %collective-permute-start.23 = (bf16[48,1536]{1,0:T(8,128)(2,1)S(1)}, bf16[48,1536]{1,0:T(8,128)(2,1)S(1)}, u32[]{:S(2)}, u32[]{:S(2)}) collective-permute-start(bf16[48,1536]{1,0:T(8,128)(2,1)S(1)} %get-tuple-element.257), channel_id=1, source_target_pairs={{0,24},{8,16},{16,8},{24,0},{1,25},{9,17},{17,9},{25,1},{2,26},{10... | collective-permute-start | bytes 442376 | tf_op jit(solution)/shard_map/ppermute | solution.py:566
  332.8 28.3 %collective-permute-start.22 = (bf16[48,1536]{1,0:T(8,128)(2,1)S(1)}, bf16[48,1536]{1,0:T(8,128)(2,1)S(1)}, u32[]{:S(2)}, u32[]{:S(2)}) collective-permute-start(bf16[48,1536]{1,0:T(8,128)(2,1)S(1)} %get-tuple-element.258), channel_id=1, source_target_pairs={{0,16},{8,24},{16,0},{24,8},{1,17},{9,25},{17,1},{25,9},{2,18},{10... | collective-permute-start | bytes 442376 | tf_op jit(solution)/shard_map/ppermute | solution.py:566
  333.8 27.3 %collective-permute-start.21 = (bf16[48,1536]{1,0:T(8,128)(2,1)S(1)}, bf16[48,1536]{1,0:T(8,128)(2,1)S(1)}, u32[]{:S(2)}, u32[]{:S(2)}) collective-permute-start(bf16[48,1536]{1,0:T(8,128)(2,1)S(1)} %get-tuple-element.256), channel_id=1, source_target_pairs={{0,8},{8,0},{16,24},{24,16},{1,9},{9,1},{17,25},{25,17},{2,10},{10... | collective-permute-start | bytes 442376 | tf_op jit(solution)/shard_map/ppermute | solution.py:566
  361.5 29.0 %collective-permute-start.28 = (bf16[48,1536]{1,0:T(8,128)(2,1)S(1)}, bf16[48,1536]{1,0:T(8,128)(2,1)S(1)}, u32[]{:S(2)}, u32[]{:S(2)}) collective-permute-start(bf16[48,1536]{1,0:T(8,128)(2,1)S(1)} %fusion.36), channel_id=1, source_target_pairs={{0,8},{8,0},{16,24},{24,16},{1,9},{9,1},{17,25},{25,17},{2,10},{10... | collective-permute-start | bytes 442376 | tf_op jit(solution)/shard_map/ppermute | solution.py:566
  363.0 27.5 %collective-permute-start.29 = (bf16[48,1536]{1,0:T(8,128)(2,1)S(1)}, bf16[48,1536]{1,0:T(8,128)(2,1)S(1)}, u32[]{:S(2)}, u32[]{:S(2)}) collective-permute-start(bf16[48,1536]{1,0:T(8,128)(2,1)S(1)} %fusion.36), channel_id=1, source_target_pairs={{0,16},{8,24},{16,0},{24,8},{1,17},{9,25},{17,1},{25,9},{2,18},{10... | collective-permute-start | bytes 442376 | tf_op jit(solution)/shard_map/ppermute | solution.py:566
  367.0 13.4 %collective-permute-start.33 = (bf16[48,1152]{1,0:T(8,128)(2,1)S(1)}, bf16[48,1152]{1,0:T(8,128)(2,1)S(1)}, u32[]{:S(2)}, u32[]{:S(2)}) collective-permute-start(bf16[48,1152]{1,0:T(8,128)(2,1)S(1)} %get-tuple-element.264), channel_id=1, source_target_pairs={{0,24},{8,16},{16,8},{24,0},{1,25},{9,17},{17,9},{25,1},{2,26},{10... | collective-permute-start | bytes 331784 | tf_op jit(solution)/shard_map/ppermute | solution.py:566
  367.1 23.3 %collective-permute-start.32 = (bf16[48,1152]{1,0:T(8,128)(2,1)S(1)}, bf16[48,1152]{1,0:T(8,128)(2,1)S(1)}, u32[]{:S(2)}, u32[]{:S(2)}) collective-permute-start(bf16[48,1152]{1,0:T(8,128)(2,1)S(1)} %get-tuple-element.265), channel_id=1, source_target_pairs={{0,16},{8,24},{16,0},{24,8},{1,17},{9,25},{17,1},{25,9},{2,18},{10... | collective-permute-start | bytes 331784 | tf_op jit(solution)/shard_map/ppermute | solution.py:566
  368.7 21.8 %collective-permute-start.31 = (bf16[48,1152]{1,0:T(8,128)(2,1)S(1)}, bf16[48,1152]{1,0:T(8,128)(2,1)S(1)}, u32[]{:S(2)}, u32[]{:S(2)}) collective-permute-start(bf16[48,1152]{1,0:T(8,128)(2,1)S(1)} %get-tuple-element.263), channel_id=1, source_target_pairs={{0,8},{8,0},{16,24},{24,16},{1,9},{9,1},{17,25},{25,17},{2,10},{10... | collective-permute-start | bytes 331784 | tf_op jit(solution)/shard_map/ppermute | solution.py:566
  380.4 10.2 %collective-permute-start.30 = (bf16[48,1536]{1,0:T(8,128)(2,1)S(1)}, bf16[48,1536]{1,0:T(8,128)(2,1)S(1)}, u32[]{:S(2)}, u32[]{:S(2)}) collective-permute-start(bf16[48,1536]{1,0:T(8,128)(2,1)S(1)} %fusion.36), channel_id=1, source_target_pairs={{0,24},{8,16},{16,8},{24,0},{1,25},{9,17},{17,9},{25,1},{2,26},{10... | collective-permute-start | bytes 442376 | tf_op jit(solution)/shard_map/ppermute | solution.py:566
  390.7 10.0 %collective-permute-start.36 = (bf16[48,1152]{1,0:T(8,128)(2,1)S(1)}, bf16[48,1152]{1,0:T(8,128)(2,1)S(1)}, u32[]{:S(2)}, u32[]{:S(2)}) collective-permute-start(bf16[48,1152]{1,0:T(8,128)(2,1)S(1)} %fusion.39), channel_id=1, source_target_pairs={{0,8},{8,0},{16,24},{24,16},{1,9},{9,1},{17,25},{25,17},{2,10},{10... | collective-permute-start | bytes 331784 | tf_op jit(solution)/shard_map/ppermute | solution.py:566
  394.3 10.1 %collective-permute-start.37 = (bf16[48,1152]{1,0:T(8,128)(2,1)S(1)}, bf16[48,1152]{1,0:T(8,128)(2,1)S(1)}, u32[]{:S(2)}, u32[]{:S(2)}) collective-permute-start(bf16[48,1152]{1,0:T(8,128)(2,1)S(1)} %fusion.39), channel_id=1, source_target_pairs={{0,16},{8,24},{16,0},{24,8},{1,17},{9,25},{17,1},{25,9},{2,18},{10... | collective-permute-start | bytes 331784 | tf_op jit(solution)/shard_map/ppermute | solution.py:566
  395.5 10.5 %collective-permute-start.38 = (bf16[48,1152]{1,0:T(8,128)(2,1)S(1)}, bf16[48,1152]{1,0:T(8,128)(2,1)S(1)}, u32[]{:S(2)}, u32[]{:S(2)}) collective-permute-start(bf16[48,1152]{1,0:T(8,128)(2,1)S(1)} %fusion.39), channel_id=1, source_target_pairs={{0,24},{8,16},{16,8},{24,0},{1,25},{9,17},{17,9},{25,1},{2,26},{10... | collective-permute-start | bytes 331784 | tf_op jit(solution)/shard_map/ppermute | solution.py:566
  396.9 9.2 %collective-permute-start.35 = (bf16[192,768]{1,0:T(8,128)(2,1)S(1)}, bf16[192,768]{1,0:T(8,128)(2,1)S(1)}, u32[]{:S(2)}, u32[]{:S(2)}) collective-permute-start(bf16[192,768]{1,0:T(8,128)(2,1)S(1)} %get-tuple-element.247), channel_id=1, source_target_pairs={{0,2},{1,3},{2,0},{3,1},{4,6},{5,7},{6,4},{7,5},{8,10},{9,11},{10,... | collective-permute-start | bytes 884744 | tf_op jit(solution)/shard_map/ppermute | solution.py:566
  398.4 1.2 collective-permute-start.39
  399.7 9.9 %collective-permute-start.34 = (bf16[192,768]{1,0:T(8,128)(2,1)S(1)}, bf16[192,768]{1,0:T(8,128)(2,1)S(1)}, u32[]{:S(2)}, u32[]{:S(2)}) collective-permute-start(bf16[192,768]{1,0:T(8,128)(2,1)S(1)} %get-tuple-element.248), channel_id=1, source_target_pairs={{0,4},{1,5},{2,6},{3,7},{4,0},{5,1},{6,2},{7,3},{8,12},{9,13},{10,... | collective-permute-start | bytes 884744 | tf_op jit(solution)/shard_map/ppermute | solution.py:566
  400.7 11.7 %collective-permute-start.40 = (bf16[256,768]{1,0:T(8,128)(2,1)S(1)}, bf16[256,768]{1,0:T(8,128)(2,1)S(1)}, u32[]{:S(2)}, u32[]{:S(2)}) collective-permute-start(bf16[256,768]{1,0:T(8,128)(2,1)S(1)} %get-tuple-element.215), channel_id=1, source_target_pairs={{0,2},{1,3},{2,0},{3,1},{4,6},{5,7},{6,4},{7,5},{8,10},{9,11},{10,... | collective-permute-start | bytes 1179656 | tf_op jit(solution)/shard_map/ppermute | solution.py:566
  404.4 12.8 %collective-permute-start.41 = (bf16[256,768]{1,0:T(8,128)(2,1)S(1)}, bf16[256,768]{1,0:T(8,128)(2,1)S(1)}, u32[]{:S(2)}, u32[]{:S(2)}) collective-permute-start(bf16[256,768]{1,0:T(8,128)(2,1)S(1)} %get-tuple-element.214), channel_id=1, source_target_pairs={{0,4},{1,5},{2,6},{3,7},{4,0},{5,1},{6,2},{7,3},{8,12},{9,13},{10,... | collective-permute-start | bytes 1179656 | tf_op jit(solution)/shard_map/ppermute | solution.py:566
  417.2 22.9 %collective-permute-start.44 = (bf16[192,1152]{1,0:T(8,128)(2,1)S(1)}, bf16[192,1152]{1,0:T(8,128)(2,1)S(1)}, u32[]{:S(2)}, u32[]{:S(2)}) collective-permute-start(bf16[192,1152]{1,0:T(8,128)(2,1)S(1)} %pad_maximum_fusion.12), channel_id=1, source_target_pairs={{0,2},{1,3},{2,0},{3,1},{4,6},{5,7},{6,4},{7,5},{8,10},{9,11},{10,... | collective-permute-start | bytes 1327112 | tf_op jit(solution)/shard_map/ppermute | solution.py:566
  417.9 23.8 %collective-permute-start.45 = (bf16[192,1152]{1,0:T(8,128)(2,1)S(1)}, bf16[192,1152]{1,0:T(8,128)(2,1)S(1)}, u32[]{:S(2)}, u32[]{:S(2)}) collective-permute-start(bf16[192,1152]{1,0:T(8,128)(2,1)S(1)} %pad_maximum_fusion.12), channel_id=1, source_target_pairs={{0,4},{1,5},{2,6},{3,7},{4,0},{5,1},{6,2},{7,3},{8,12},{9,13},{10,... | collective-permute-start | bytes 1327112 | tf_op jit(solution)/shard_map/ppermute | solution.py:566
  419.4 23.6 %collective-permute-start.46 = (bf16[192,1152]{1,0:T(8,128)(2,1)S(1)}, bf16[192,1152]{1,0:T(8,128)(2,1)}, u32[]{:S(2)}, u32[]{:S(2)}) collective-permute-start(bf16[192,1152]{1,0:T(8,128)(2,1)S(1)} %pad_maximum_fusion.12), channel_id=1, source_target_pairs={{0,6},{1,7},{2,4},{3,5},{4,2},{5,3},{6,0},{7,1},{8,14},{9,15},{10,... | collective-permute-start | bytes 1327112 | tf_op jit(solution)/shard_map/ppermute | solution.py:566
  420.7 43.5 %collective-permute-start.53 = (bf16[384,3840]{1,0:T(8,128)(2,1)}, bf16[384,3840]{1,0:T(8,128)(2,1)}, u32[]{:S(2)}, u32[]{:S(2)}) collective-permute-start(bf16[384,3840]{1,0:T(8,128)(2,1)} %all-reduce.2.cloned.1.call-done.refs_0_), channel_id=1, source_target_pairs={{0,1},{1,0},{2,3},{3,2},{4,5},{5,4},{6,7},{7,6},{8,9},{9,8},{10,11... | collective-permute-start | bytes 8847368 | tf_op jit(solution)/shard_map/ppermute | solution.py:566
  420.7 18.2 %collective-permute-start.47 = (f32[9216]{0:T(1024)S(1)}, f32[9216]{0:T(1024)S(1)}, u32[]{:S(2)}, u32[]{:S(2)}) collective-permute-start(f32[9216]{0:T(1024)S(1)} %add.478), channel_id=1, source_target_pairs={{0,2},{1,3},{2,0},{3,1},{4,6},{5,7},{6,4},{7,5},{8,10},{9,11},{10,... | collective-permute-start | bytes 110600 | tf_op jit(solution)/shard_map/ppermute | solution.py:566
  438.9 16.4 %collective-permute-start.42 = (bf16[384,768]{1,0:T(8,128)(2,1)}, bf16[384,768]{1,0:T(8,128)(2,1)S(1)}, u32[]{:S(2)}, u32[]{:S(2)}) collective-permute-start(bf16[384,768]{1,0:T(8,128)(2,1)} %pad_maximum_fusion.9), channel_id=1, source_target_pairs={{0,2},{1,3},{2,0},{3,1},{4,6},{5,7},{6,4},{7,5},{8,10},{9,11},{10,... | collective-permute-start | bytes 1769480 | tf_op jit(solution)/shard_map/ppermute | solution.py:566
  440.0 22.1 %collective-permute-start.43 = (bf16[384,768]{1,0:T(8,128)(2,1)}, bf16[384,768]{1,0:T(8,128)(2,1)S(1)}, u32[]{:S(2)}, u32[]{:S(2)}) collective-permute-start(bf16[384,768]{1,0:T(8,128)(2,1)} %pad_maximum_fusion.10), channel_id=1, source_target_pairs={{0,4},{1,5},{2,6},{3,7},{4,0},{5,1},{6,2},{7,3},{8,12},{9,13},{10,... | collective-permute-start | bytes 1769480 | tf_op jit(solution)/shard_map/ppermute | solution.py:566
  441.7 21.7 %collective-permute-start.48 = (bf16[256,768]{1,0:T(8,128)(2,1)S(1)}, bf16[256,768]{1,0:T(8,128)(2,1)S(1)}, u32[]{:S(2)}, u32[]{:S(2)}) collective-permute-start(bf16[256,768]{1,0:T(8,128)(2,1)S(1)} %slice_bitcast_fusion), channel_id=1, source_target_pairs={{0,6},{1,7},{2,4},{3,5},{4,2},{5,3},{6,0},{7,1},{8,14},{9,15},{10,... | collective-permute-start | bytes 1179656 | tf_op jit(solution)/shard_map/ppermute | solution.py:566
  444.4 19.3 %copy-start.6 = (bf16[768,1152]{1,0:T(8,128)(2,1)}, bf16[768,1152]{1,0:T(8,128)(2,1)S(1)}, u32[]{:S(2)}) copy-start(bf16[768,1152]{1,0:T(8,128)(2,1)S(1)} %pad_maximum_fusion.2.refs_0_) | copy-start | bytes 5308420
  463.6 29.7 %collective-permute-start.54 = (bf16[1536,768]{1,0:T(8,128)(2,1)S(1)}, bf16[1536,768]{1,0:T(8,128)(2,1)}, u32[]{:S(2)}, u32[]{:S(2)}) collective-permute-start(bf16[1536,768]{1,0:T(8,128)(2,1)S(1)} %constant_dynamic-update-slice_fusion.6.refs_0_), channel_id=1, source_target_pairs={{0,1},{1,0},{2,3},{3,2},{4,5},{5,4},{6,7},{7,6},{8,9},{9,8},{10,11... | collective-permute-start | bytes 7077896 | tf_op jit(solution)/shard_map/ppermute | solution.py:566
  463.7 24.2 %collective-permute-start.52 = (bf16[768,1152]{1,0:T(8,128)(2,1)S(1)}, bf16[768,1152]{1,0:T(8,128)(2,1)}, u32[]{:S(2)}, u32[]{:S(2)}) collective-permute-start(bf16[768,1152]{1,0:T(8,128)(2,1)S(1)} %pad_maximum_fusion.2.refs_0_), channel_id=1, source_target_pairs={{0,1},{1,0},{2,3},{3,2},{4,5},{5,4},{6,7},{7,6},{8,9},{9,8},{10,11... | collective-permute-start | bytes 5308424 | tf_op jit(solution)/shard_map/ppermute | solution.py:566
  472.2 5.5 %collective-permute-start.49 = (f32[9216]{0:T(1024)}, f32[9216]{0:T(1024)S(1)}, u32[]{:S(2)}, u32[]{:S(2)}) collective-permute-start(f32[9216]{0:T(1024)} %add.479), channel_id=1, source_target_pairs={{0,4},{1,5},{2,6},{3,7},{4,0},{5,1},{6,2},{7,3},{8,12},{9,13},{10,... | collective-permute-start | bytes 110600 | tf_op jit(solution)/shard_map/ppermute | solution.py:566
  477.7 4.0 collective-permute-start.50
  481.8 4.9 collective-permute-start.51
  (48 other events, 195.6 us)
Sparse Core Ops, SparseCore 0:
  208.2 166.5 all-reduce.1
